TPU v7x, 128 devices: a whole 4x4x4 slice. The times are simulated.
128 devices in a mesh: elem: 32 (over x, y, core), freq: 4 (over z).
Axes of the slice: x: 4, y: 4, z: 4, core: 2. Of those that a mesh axis runs over, the one named last changes fastest.
Arguments:
- load: float32 [48, 128, 2, 4096], P(None, 'freq', None, 'elem'), may hold values from -6 to 6
- stiffness: float32 [96, 96], replicated, as said below
- mass_template: float32 [96], replicated, may hold values from 0.5 to 2
- modulus: float32 [4096], P('elem'), may hold values from 0.5 to 2
- element_mass: float32 [4096], P('elem'), may hold values from 0.5 to 2
- strain_map: float32 [6, 96], replicated, may hold values from -0.625 to 0.625
- curves: float32 [4, 16], replicated, may hold values from 0.2 to 1
- soil_type: int32 [4096], P(('elem', 'freq')), may hold values from 0 to 3
Outputs:
- new_modulus: float32 [4096], P(('elem', 'freq'))
- peak_strain: float32 [4096], P(('elem', 'freq'))
Inputs may be any that keep to these rules, and one draw needn't show every extreme that they name: `stiffness`: symmetric positive definite.
All inputs are finite; a program needn't handle non-finite values.
Results may differ from a plain program's by a relative error of at most 0.00013.
Values sent between devices are 32-bit elements; how exact they have to be, the bound alone decides.
No kernel may reach another device: no remote copies, remote signals or barrier semaphores. Data moves between devices by JAX's collectives and lax.ppermute only.
A program may use at most 128 MiB of HBM per device.

v0:
```python
import jax
import jax.numpy as jnp
from jax import lax
from jax.sharding import PartitionSpec as P

NT = 512
ITERS = 3


PRECISE = lax.Precision.HIGHEST
MASS_COEF = 0.5
LOG_LOW = -1.5
LOG_STEP = 0.2
STRAIN_FACTOR = 0.65
EPSILON = 1e-06


def passed_along(value, axis, by):
    length = lax.axis_size(axis)
    pairs = [(i, i + by) for i in range(length) if 0 <= i + by < length]
    return lax.ppermute(value, axis, pairs)


def element_vectors(field):
    beyond = passed_along(field[..., :1], "elem", -1)
    ahead = jnp.concatenate([field[..., 1:], beyond], axis=-1)
    return jnp.concatenate([field, ahead], axis=0)


def operate(field, stiffness, mass_template, modulus, mass_scale):
    half_size = stiffness.shape[0] // 2
    stacked = element_vectors(field)
    product = jnp.dot(stiffness, stacked.reshape(2 * half_size, -1), precision=PRECISE).reshape(
        stacked.shape
    )
    forces = modulus * product + mass_scale * mass_template[:, None, None, None] * stacked
    arriving = passed_along(forces[half_size:, ..., -1:], "elem", 1)
    behind = jnp.concatenate([arriving, forces[half_size:, ..., :-1]], axis=-1)
    return forces[:half_size] + behind


def local_dot(left, right):
    return jnp.sum(left * right, axis=(0, 2, 3))


def per_freq(values):
    return values[:, None, None]


def norm_sum(residual, precond):
    return lax.psum(local_dot(residual, precond), "elem")


def per_device(
    load, stiffness, mass_template, modulus, element_mass, strain_map, curves, soil_type
):
    half_size = stiffness.shape[0] // 2
    freq_dev = load.shape[1]
    node_count = load.shape[3]
    groups = lax.axis_size("freq")
    total_freq = freq_dev * groups
    group_index = lax.axis_index("freq")
    order = (group_index * freq_dev + jnp.arange(freq_dev, dtype=jnp.int32) + 1).astype(jnp.float32)
    mass_shift = MASS_COEF * (order / total_freq) ** 2
    mass_scale = mass_shift[:, None, None] * element_mass
    rim_modulus, rim_mass = passed_along((modulus[-1:], element_mass[-1:]), "elem", 1)
    prev_modulus = jnp.concatenate([rim_modulus, modulus[:-1]])
    prev_mass = jnp.concatenate([rim_mass, element_mass[:-1]])
    kdiag = jnp.diagonal(stiffness)
    diag_own = (
        kdiag[:half_size, None, None, None] * modulus
        + mass_scale * mass_template[:half_size, None, None, None]
    )
    diag_prev = (
        kdiag[half_size:, None, None, None] * prev_modulus
        + mass_shift[:, None, None] * prev_mass * mass_template[half_size:, None, None, None]
    )
    inv_diag = 1.0 / (diag_own + diag_prev)
    solution = jnp.zeros_like(load)
    residual = load
    precond = residual * inv_diag
    direction = precond
    rho_now = norm_sum(residual, precond)
    for iteration in range(ITERS):
        image = operate(direction, stiffness, mass_template, modulus, mass_scale)
        curvature = lax.psum(local_dot(direction, image), "elem")
        alpha = rho_now / curvature
        solution = solution + per_freq(alpha) * direction
        if iteration + 1 < ITERS:
            residual = residual - per_freq(alpha) * image
            precond = residual * inv_diag
            rho_next = norm_sum(residual, precond)
            direction = precond + per_freq(rho_next / rho_now) * direction
            rho_now = rho_next
    stacked = element_vectors(solution)
    spectra = jnp.dot(strain_map, stacked.reshape(2 * half_size, -1), precision=PRECISE)
    spectra = spectra.reshape(strain_map.shape[0], freq_dev, 2, node_count)
    times = jnp.arange(NT, dtype=jnp.int32)
    scale = 1.0 / jnp.sqrt(jnp.float32(total_freq))
    local_freqs = group_index * freq_dev + jnp.arange(freq_dev, dtype=jnp.int32) + 1
    phase = (local_freqs[:, None] * times[None, :] % NT).astype(jnp.float32) * (2.0 * jnp.pi / NT)
    table = jnp.stack([jnp.cos(phase), -jnp.sin(phase)], axis=1)
    partials = jnp.einsum("fkt,cfke->cte", table, spectra, precision=PRECISE)
    history = lax.psum_scatter(partials, "freq", scatter_dimension=2, tiled=True) * scale
    peak = jnp.max(jnp.sum(history * history, axis=0), axis=0)
    peak_strain = STRAIN_FACTOR * jnp.sqrt(peak + EPSILON)
    position = (jnp.log10(peak_strain) - LOG_LOW) / LOG_STEP
    levels = jnp.arange(curves.shape[1], dtype=jnp.float32)
    hats = jnp.maximum(0.0, 1.0 - jnp.abs(position[:, None] - levels[None, :]))
    onehot = (soil_type[:, None] == jnp.arange(curves.shape[0], dtype=jnp.int32)[None, :]).astype(
        jnp.float32
    )
    own_curve = jnp.dot(onehot, curves, precision=PRECISE)
    ratio = jnp.sum(own_curve * hats, axis=1)
    quarter = node_count // groups
    own_modulus = lax.dynamic_slice_in_dim(modulus, group_index * quarter, quarter)
    return (own_modulus * ratio, peak_strain)


def solution(mesh):
    in_specs = (
        P(None, "freq", None, "elem"),
        P(),
        P(),
        P("elem"),
        P("elem"),
        P(),
        P(),
        P(("elem", "freq")),
    )
    out_specs = (P(("elem", "freq")), P(("elem", "freq")))
    return jax.shard_map(
        per_device, mesh=mesh, in_specs=in_specs, out_specs=out_specs, check_vma=False
    )
```

profile of v0, /device:TPU:1, one launch (start us, length us, event | category | flops | bytes accessed | tf_op | source)
XLA Modules:
  0.0 585.4 jit_solution(16286616721584442370)
XLA Ops:
  46.0 5.5 reshape.307
  51.5 6.4 %convolution_bitcast_fusion.2 = f32[96,8192]{1,0:T(8,128)} fusion(f32[96,8192]{1,0:T(8,128)} %reshape.307, f32[96,96]{1,0:T(8,128)S(1)} %copy-done), kind=kOutput, calls=%fused_computation.3 | convolution fusion | flops 905969664 | bytes 6328320 | tf_op jit(solution)/shard_map/dot_general | solution.py:33
  57.9 5.6 reshape.308
  68.7 6.5 %multiply_add_fusion.5 = f32[96,32,2,128]{0,1,3,2:T(8,128)S(1)} fusion(f32[96,32,2,128]{0,1,3,2:T(8,128)} %copy.65, f32[96,32,128]{0,1,2:T(8,128)} %broadcast_multiply_fusion.1, f32[128]{0:T(128)S(1)} %copy-done.14, f32[48,32,2,1]{0,1,3,2:T(8,128)S(1)} %collective-permute-done.2, f32[48,32,2,127]{0,1,3,2:T(8,128)} %copy-done.11, f32[48,32,2,128]{0,1,3,2:T(8,128)} %copy-done.6), kind=kLoop, calls=%fused_computation.27 | loop fusion | flops 3932160 | bytes 11010560 | tf_op jit(solution)/shard_map/add | solution.py:36
  82.0 62.8 %all-reduce = (f32[32]{0:T(128)S(1)}, f32[32]{0:T(128)S(1)}) all-reduce(f32[32]{0:T(128)S(1)} %get-tuple-element.3, f32[32]{0:T(128)S(1)} %get-tuple-element.2), channel_id=1, replica_groups=mesh['elem'=32,'freq'=4] {'elem'}, use_global_device_ids=true, to_apply=%region_1.2 | all-reduce | flops 64 | bytes 512 | tf_op jit(solution)/shard_map/psum | solution.py:51
  144.8 7.4 %fusion = (f32[32]{0:T(128)S(1)}, f32[48,32,2,128]{0,1,3,2:T(8,128)}) fusion(f32[48,32,128]{0,1,2:T(8,128)S(1)} %add_divide_fusion, f32[48,32,2,128]{0,1,3,2:T(8,128)} %copy.63, f32[48,32,2,127]{0,1,3,2:T(8,128)} %copy-done.10, f32[48,32,2,1]{0,1,3,2:T(8,128)S(1)} %collective-permute-done.3, f32[96,32,2,128]{0,1,3,2:T(8,128)} %copy-done.8, f32[32]{0:T(128)S(1)} %div.42), kind=kLoop, calls=%fused_computation.9 | loop fusion | flops 2752480 | bytes 7078144 | tf_op jit(solution)/shard_map/reduce_sum | solution.py:43
  152.2 65.2 %psum.44 = f32[32]{0:T(128)S(1)} all-reduce(f32[32]{0:T(128)S(1)} %get-tuple-element.10), channel_id=1, replica_groups=mesh['elem'=32,'freq'=4] {'elem'}, use_global_device_ids=true, to_apply=%region_5.6 | all-reduce | flops 32 | bytes 256 | tf_op jit(solution)/shard_map/psum | solution.py:51
  230.8 5.3 copy.67
  236.0 5.5 reshape.309
  241.5 6.5 %convolution_bitcast_fusion.1 = f32[96,8192]{1,0:T(8,128)} fusion(f32[96,8192]{1,0:T(8,128)} %reshape.309, f32[96,96]{1,0:T(8,128)S(1)} %copy-done), kind=kOutput, calls=%fused_computation.2 | convolution fusion | flops 905969664 | bytes 6328320 | tf_op jit(solution)/shard_map/dot_general | solution.py:33
  248.0 5.7 reshape.310
  258.8 6.5 %multiply_add_fusion.4 = f32[96,32,2,128]{0,1,3,2:T(8,128)S(1)} fusion(f32[96,32,2,128]{0,1,3,2:T(8,128)} %copy.68, f32[96,32,128]{0,1,2:T(8,128)} %broadcast_multiply_fusion.1, f32[128]{0:T(128)S(1)} %copy-done.14, f32[48,32,2,1]{0,1,3,2:T(8,128)S(1)} %collective-permute-done.4, f32[48,32,2,127]{0,1,3,2:T(8,128)} %copy-done.13, f32[48,32,2,128]{0,1,3,2:T(8,128)} %copy-done.1), kind=kLoop, calls=%fused_computation.24 | loop fusion | flops 3932160 | bytes 11010560 | tf_op jit(solution)/shard_map/add | solution.py:36
  273.3 61.6 %psum.45 = f32[32]{0:T(128)S(1)} all-reduce(f32[32]{0:T(128)S(1)} %multiply_reduce_fusion), channel_id=1, replica_groups=mesh['elem'=32,'freq'=4] {'elem'}, use_global_device_ids=true, to_apply=%region_7.8 | all-reduce | flops 32 | bytes 256 | tf_op jit(solution)/shard_map/psum | solution.py:86
  334.9 7.4 %fusion.1 = (f32[32]{0:T(128)S(1)}, f32[48,32,2,128]{0,1,3,2:T(8,128)}) fusion(f32[48,32,128]{0,1,2:T(8,128)S(1)} %add_divide_fusion, f32[48,32,2,128]{0,1,3,2:T(8,128)} %get-tuple-element.11, f32[48,32,2,127]{0,1,3,2:T(8,128)} %copy-done.9, f32[48,32,2,1]{0,1,3,2:T(8,128)S(1)} %collective-permute-done.5, f32[96,32,2,128]{0,1,3,2:T(8,128)} %copy-done.7, ...), kind=kLoop, calls=%fused_computation.10 | loop fusion | flops 2752480 | bytes 7078144 | tf_op jit(solution)/shard_map/reduce_sum | solution.py:43
  342.3 63.6 %psum.46 = f32[32]{0:T(128)S(1)} all-reduce(f32[32]{0:T(128)S(1)} %get-tuple-element.8), channel_id=1, replica_groups=mesh['elem'=32,'freq'=4] {'elem'}, use_global_device_ids=true, to_apply=%region_9.10 | all-reduce | flops 32 | bytes 256 | tf_op jit(solution)/shard_map/psum | solution.py:51
  419.3 5.3 copy.69
  424.6 5.5 reshape.311
  430.1 6.5 %convolution_bitcast_fusion = f32[96,8192]{1,0:T(8,128)} fusion(f32[96,8192]{1,0:T(8,128)} %reshape.311, f32[96,96]{1,0:T(8,128)S(1)} %copy-done), kind=kOutput, calls=%fused_computation.1 | convolution fusion | flops 905969664 | bytes 6328320 | tf_op jit(solution)/shard_map/dot_general | solution.py:33
  436.5 5.7 reshape.312
  447.4 6.5 %multiply_add_fusion.3 = f32[96,32,2,128]{0,1,3,2:T(8,128)S(1)} fusion(f32[96,32,2,128]{0,1,3,2:T(8,128)} %copy.70, f32[96,32,128]{0,1,2:T(8,128)} %broadcast_multiply_fusion.1, f32[128]{0:T(128)S(1)} %copy-done.14, f32[48,32,2,1]{0,1,3,2:T(8,128)S(1)} %collective-permute-done.6, f32[48,32,2,127]{0,1,3,2:T(8,128)} %copy-done.12, f32[48,32,2,128]{0,1,3,2:T(8,128)} %copy-done.4), kind=kLoop, calls=%fused_computation.21 | loop fusion | flops 3932160 | bytes 11010560 | tf_op jit(solution)/shard_map/add | solution.py:36
  460.0 61.6 %psum.47 = f32[32]{0:T(128)S(1)} all-reduce(f32[32]{0:T(128)S(1)} %fusion.3), channel_id=1, replica_groups=mesh['elem'=32,'freq'=4] {'elem'}, use_global_device_ids=true, to_apply=%region_11.12 | all-reduce | flops 32 | bytes 256 | tf_op jit(solution)/shard_map/psum | solution.py:86
  521.6 6.5 %multiply_add_fusion.2 = f32[48,32,2,128]{0,1,3,2:T(8,128)S(1)} fusion(f32[48,32,2,128]{0,1,3,2:T(8,128)} %copy-done.4, f32[48,32,2,128]{0,1,3,2:T(8,128)} %copy-done.1, f32[32]{0:T(128)S(1)} %div.46, f32[32]{0:T(128)S(1)} %div.44, f32[32]{0:T(128)S(1)} %div.42, f32[48,32,2,128]{0,1,3,2:T(8,128)} %copy.63, f32[48,32,128]{0,1,2:T(8,128)S(1)} %add_divide_fusion), kind=kLoop, calls=%fused_computation.20 | loop fusion | flops 2359296 | bytes 7078272 | tf_op jit(solution)/shard_map/add | solution.py:88
  541.8 5.5 reshape.313
  553.8 22.1 %reduce-scatter.2.cloned.1.call-done = f32[6,512,32]{1,2,0:T(8,128)} async-done(((f32[6,512,128]{1,2,0:T(8,128)}), f32[6,512,32]{1,2,0:T(8,128)}) %reduce-scatter.2.cloned.1.call-update) | async-done | bytes 393232 | tf_op jit(solution)/shard_map/reduce_scatter | solution.py:104
  (119 shorter events, 124.1 us)
Async XLA Ops:
  7.2 9.1 %copy-start = (f32[96,96]{1,0:T(8,128)S(1)}, f32[96,96]{1,0:T(8,128)}, u32[]{:S(2)}) copy-start(f32[96,96]{1,0:T(8,128)} %param.9) | copy-start | bytes 110596
  7.2 16.8 %copy-start.17 = (f32[128]{0:T(128)S(1)}, f32[128]{0:T(128)}, u32[]{:S(2)}) copy-start(f32[128]{0:T(128)} %param.12) | copy-start | bytes 1540
  7.2 17.6 %copy-start.14 = (f32[128]{0:T(128)S(1)}, f32[128]{0:T(128)}, u32[]{:S(2)}) copy-start(f32[128]{0:T(128)} %param.11) | copy-start | bytes 1540
  7.2 568.6 %reduce-scatter.2.cloned.1.call-start = ((), (), s32[]{:S(2)}) async-start(), calls=%async_computation.1 | async-start | bytes 1966080 | tf_op jit(solution)/shard_map/reduce_scatter | solution.py:104
  8.5 15.5 %collective-permute-start.1 = (f32[1]{0:T(128)}, f32[1]{0:T(128)}, u32[]{:S(2)}, u32[]{:S(2)}) collective-permute-start(f32[1]{0:T(128)} %slice.80), channel_id=1, source_target_pairs={{0,4},{4,8},{8,12},{12,16},{16,20},{20,24},{24,28},{28,32},{32,36}... | collective-permute-start | bytes 20 | tf_op jit(solution)/shard_map/ppermute | solution.py:21
  14.3 10.5 %collective-permute-start = (f32[1]{0:T(128)}, f32[1]{0:T(128)}, u32[]{:S(2)}, u32[]{:S(2)}) collective-permute-start(f32[1]{0:T(128)} %slice.78), channel_id=1, source_target_pairs={{0,4},{4,8},{8,12},{12,16},{16,20},{20,24},{24,28},{28,32},{32,36}... | collective-permute-start | bytes 20 | tf_op jit(solution)/shard_map/ppermute | solution.py:21
  26.7 6.4 %copy-start.15 = (f32[96]{0:T(128)S(1)}, f32[96]{0:T(128)}, u32[]{:S(2)}) copy-start(f32[96]{0:T(128)} %param.10) | copy-start | bytes 1156
  29.7 5.9 %copy-start.6 = (f32[48,32,2,128]{0,1,3,2:T(8,128)}, f32[48,32,2,128]{0,1,3,2:T(8,128)S(1)}, u32[]{:S(2)}) copy-start(f32[48,32,2,128]{0,1,3,2:T(8,128)S(1)} %broadcast_multiply_fusion) | copy-start | bytes 4718596
  29.7 5.8 collective-permute-start.2
  75.2 6.4 %copy-start.8 = (f32[96,32,2,128]{0,1,3,2:T(8,128)}, f32[96,32,2,128]{0,1,3,2:T(8,128)S(1)}, u32[]{:S(2)}) copy-start(f32[96,32,2,128]{0,1,3,2:T(8,128)S(1)} %multiply_add_fusion.5) | copy-start | bytes 9437188
  75.3 4.2 collective-permute-start.3
  222.3 5.3 copy-start.1
  222.4 5.2 collective-permute-start.4
  265.3 4.4 copy-start.7
  265.3 6.4 %copy-start.2 = (f32[48,32,2,128]{0,1,3,2:T(8,128)S(1)}, f32[48,32,2,128]{0,1,3,2:T(8,128)}, u32[]{:S(2)}) copy-start(f32[48,32,2,128]{0,1,3,2:T(8,128)} %copy-done.1) | copy-start | bytes 4718596
  265.4 4.3 collective-permute-start.5
  410.8 5.3 copy-start.4
  410.8 5.2 collective-permute-start.6
  453.9 4.5 copy-start.5
  454.0 4.4 collective-permute-start.7
  528.2 5.2 collective-permute-start.8
  541.8 5.5 copy-start.16
  547.3 30.2 %copy-start.18 = (f32[4,16]{1,0:T(4,128)S(1)}, f32[4,16]{1,0:T(4,128)}, u32[]{:S(2)}) copy-start(f32[4,16]{1,0:T(4,128)} %param.14) | copy-start | bytes 772
  547.3 30.2 %copy-start.19 = (s32[32]{0:T(128)S(1)}, s32[32]{0:T(128)}, u32[]{:S(2)}) copy-start(s32[32]{0:T(128)} %param.15) | copy-start | bytes 388
  (6 other events, 15.1 us)
Sparse Core Ops, SparseCore 0:
  553.9 21.8 reduce-scatter.1
where the time goes:
time: 590 us; the launch traced here: 585 us
  blocking collectives  315 us (53%)
  local copies, waits for them, and re-layouts  95.1 us (16%)
  other arithmetic  79.5 us (13%)
  starting transfers between devices  28.6 us (5%)
  waiting for transfers between devices  26.9 us (5%)
  matrix products  25.8 us (4%)
  between operations  14.7 us (2%)
    psum x3, blocking collectives, norm_sum(): return lax.psum(local_dot(residual, precond), 'elem')  192 us
    psum x2, blocking collectives, per_device(): curvature = lax.psum(local_dot(direction, image), 'elem')  123 us
    reshape x6, local copies, waits for them, and re-layouts, operate(): jnp.dot(stiffness, stacked.reshape(2 * half_size, -1), precision=PRECISE)  32.4 us
    ppermute x9, starting transfers between devices, passed_along(): return lax.ppermute(value, axis, pairs)  28.5 us
    reduce_scatter x1, waiting for transfers between devices, per_device(): lax.psum_scatter(partials, 'freq', scatter_dimension=2, tiled=True) * scale  22.1 us
    concatenate x4, local copies, waits for them, and re-layouts, element_vectors(): return jnp.concatenate([field, ahead], axis=0)  21 us
    reduce_sum x5, other arithmetic, local_dot(): return jnp.sum(left * right, axis=(0, 2, 3))  20.2 us
    add x3, other arithmetic, operate(): modulus * product  19.5 us
  transfers between devices with their start and end apart: 10, of which 4 were waited for; matrix products, arithmetic and copies ran while one was open for 3% of the time, Pallas kernels for 0%

commit v1 on v0

v1 whole, which is shorter than its diff:
```python
import jax
import jax.numpy as jnp
import numpy as np
from jax import lax
from jax.experimental import pallas as pl
from jax.experimental.pallas import tpu as pltpu
from jax.sharding import PartitionSpec as P

NT = 512
MASS_COEF = 0.5
LOG_LOW = -1.5
LOG_STEP = 0.2
STRAIN_FACTOR = 0.65
EPSILON = 1e-06
LANES = 128
SLOT = 8
PER_PATCH = LANES // SLOT
DOTS = 6
F32 = jnp.float32
BF16 = jnp.bfloat16
VMEM = pl.BlockSpec(memory_space=pltpu.VMEM)
SMEM = pl.BlockSpec(memory_space=pltpu.SMEM)


def lane_ids(rows=1):
    return lax.broadcasted_iota(jnp.int32, (rows, LANES), 1)


def later(x):
    return pltpu.roll(x, 127, 1)


def earlier(x):
    return pltpu.roll(x, 1, 1)


def halves(x):
    high = x.astype(BF16)
    return high, (x - high.astype(F32)).astype(BF16)


def edges_kernel(load_ref, modulus_ref, mass_ref, out_ref):
    half = load_ref.shape[0] // 64
    parts = 64
    slot = lane_ids(half) // SLOT
    for group in range(parts // PER_PATCH):

        def place(i, held):
            field = load_ref[pl.ds(group * PER_PATCH + i, half, stride=parts), :]
            moved = pltpu.roll(field, 2 + SLOT * i, 1)
            return jnp.where(slot == i, moved, held)

        held = lax.fori_loop(0, PER_PATCH, place, jnp.zeros((half, LANES), F32), unroll=16)
        out_ref[group * half : (group + 1) * half, :] = held
    base = parts // PER_PATCH * half
    out_ref[base : base + 1, :] = modulus_ref[...]
    out_ref[base + 1 : base + 2, :] = mass_ref[...]
    out_ref[base + 2 : base + 8, :] = jnp.zeros((6, LANES), F32)


def pattern(row):
    row = jnp.where(lane_ids() < SLOT, row, 0.0)
    for step in (8, 16, 32, 64):
        row = row + pltpu.roll(row, step, 1)
    return row


def main_kernel(
    info_ref, load_ref, own_ref, left_ref, right_ref, lhs_ref, cols_ref,
    out0_ref, out1_ref, out2_ref, out3_ref, dots_out_ref,
    field_ref, inv_ref, strain_ref, border_ref, dots_ref,
):
    half = lhs_ref.shape[1] // 3
    parts = 64
    freqs = parts // 2
    groups = parts // PER_PATCH
    base = groups * half
    freq_group = info_ref[0]
    is_last = info_ref[1]
    first_order = (freq_group * freqs + 1).astype(F32)
    lanes = lane_ids()
    place = lanes % SLOT

    def shift_of(order):
        return MASS_COEF * (order * (1.0 / (4 * freqs))) ** 2

    cols = cols_ref[...]
    kd_top, kd_low, mt_top, mt_low = (cols[:, i : i + 1] for i in range(4))

    def rows_of(at):
        own, left, right = (r[base + at : base + at + 1, :] for r in (own_ref, left_ref, right_ref))
        prev = jnp.where(lanes == 0, earlier(left), earlier(own))
        right_prev = jnp.where(lanes == 0, earlier(own), earlier(right))
        own2, prev2 = pltpu.roll(own, 2, 1), pltpu.roll(prev, 2, 1)
        near = lanes < 2
        lower = pattern(jnp.where(near, pltpu.roll(left, 2, 1), own2))
        lower_prev = pattern(jnp.where(near, pltpu.roll(left, 3, 1), prev2))
        upper = pattern(jnp.where(near, own2, pltpu.roll(right, 2, 1)))
        upper_prev = pattern(jnp.where(near, prev2, pltpu.roll(right_prev, 2, 1)))
        return (own, prev), (lower, lower_prev), (upper, upper_prev)

    mod_main, mod_lower, mod_upper = rows_of(0)
    mass_main, mass_lower, mass_upper = rows_of(1)

    def diagonals(mod, mass):
        return kd_top * mod[0] + kd_low * mod[1], mt_top * mass[0] + mt_low * mass[1]

    lhs = lhs_ref[...]

    def products(left, right):
        left_high, left_low = halves(left)
        right_high, right_low = halves(right)
        high = jnp.concatenate([left_high, right_high], 1)
        low = jnp.concatenate([left_low, right_low], 1)
        result = jnp.dot(lhs, jnp.concatenate([high, low, high], 0), preferred_element_type=F32)
        cut = [half * i for i in range(5)] + [4 * half + 8, 4 * half + 16]
        return [
            [result[cut[i] : cut[i + 1], LANES * k : LANES * (k + 1)] for i in range(6)]
            for k in range(2)
        ]

    stiff_lower, mass_diag_lower = diagonals(mod_lower, mass_lower)
    stiff_upper, mass_diag_upper = diagonals(mod_upper, mass_upper)
    fixed = jnp.logical_and(is_last == 1, place >= 2)
    for group in range(groups):
        order = first_order + (group * (PER_PATCH // 2) + lanes // (2 * SLOT)).astype(F32)
        shift = shift_of(order)
        diag_lower = stiff_lower + shift * mass_diag_lower
        diag_upper = stiff_upper + shift * mass_diag_upper
        inv_lower = jnp.where(diag_lower > 0, 1.0 / diag_lower, 0.0)
        inv_upper = jnp.where(
            jnp.logical_and(diag_upper > 0, jnp.logical_not(fixed)), 1.0 / diag_upper, 0.0
        )
        rows = slice(group * half, (group + 1) * half)
        own, left, right = own_ref[rows, :], left_ref[rows, :], right_ref[rows, :]
        lower = jnp.where(place < 2, left, own) * inv_lower
        upper = jnp.where(place < 2, own, right) * inv_upper
        for stage in range(3):
            lower_p, upper_p = products(lower, upper)
            l11, l22, l12, l21, _, _ = lower_p
            u11, u22, u12, u21, _, u_strain = upper_p
            from_above = later(mod_upper[1] * u12)
            at = stage * groups + group
            if stage < 2:
                from_below = earlier(mod_lower[0] * l21)
                border = jnp.where(
                    place == 1, from_above, jnp.where(place == 2, from_below, 0.0)
                )
                lower = -inv_lower * (
                    mod_lower[0] * l11 + mod_lower[1] * l22 + later(mod_lower[1] * l12) + from_below
                )
                tail = u_strain
                upper_next = -inv_upper * (
                    mod_upper[0] * u11 + mod_upper[1] * u22 + from_above
                    + earlier(mod_upper[0] * u21)
                )
            else:
                border = jnp.where(place == 1, from_above, 0.0)
                energy = jnp.sum(mod_upper[1] * upper * u22, axis=0, keepdims=True)
                row = lax.broadcasted_iota(jnp.int32, (8, LANES), 0)
                tail = jnp.where(row == 6, energy, u_strain)
                upper_next = None
            border_ref[at, :half, :] = border
            border_ref[at, half:, :] = jnp.where(place == 1, later(tail), 0.0)
            upper = upper_next

    stiff_main, mass_diag_main = diagonals(mod_main, mass_main)
    mod_own, mod_prev = mod_main
    mod_sent_up = jnp.where(lanes == 127, 0.0, mod_own)
    mod_sent_down = jnp.where(lanes == 0, 0.0, mod_prev)
    rim = jnp.logical_or(lanes == 0, lanes == 127)

    def borders(stage, f, k):
        part = 2 * f + k
        group = part // PER_PATCH
        i = part % PER_PATCH
        moved = pltpu.roll(border_ref[stage * groups + group], (126 + LANES - SLOT * i) % LANES, 1)
        moved = jnp.where(rim, moved, 0.0)
        return moved[:half], moved[half:]

    def strain_of(top, low, added):
        return top + jnp.where(lanes == 127, 0.0, later(low)) + added

    def put_dot(which, f, pairs):
        total = sum(a * b for a, b in pairs)
        dots_ref[pl.ds(which * freqs + f, 1), :] = jnp.sum(total, axis=0, keepdims=True)

    def put_strain(stage, f, k, value):
        start = ((stage * 2 + k) * freqs + f) * 8
        strain_ref[pl.ds(pl.multiple_of(start, 8), 8), :] = value

    def images(f, stage, fields):
        result = []
        for k, z in enumerate(products(*fields)):
            z11, z22, z12, z21, s_top, s_low = z
            added, added_strain = borders(stage, f, k)
            image = (
                mod_own * z11 + mod_prev * z22 + later(mod_sent_down * z12)
                + earlier(mod_sent_up * z21) + added
            )
            put_strain(stage, f, k, strain_of(s_top, s_low, added_strain))
            result.append(-image)
        return result

    def first(f, carry):
        inv = 1.0 / (stiff_main + shift_of(first_order + f.astype(F32)) * mass_diag_main)
        inv_ref[f] = inv
        loads = [load_ref[pl.ds(2 * f + k, half, stride=parts), :] for k in range(2)]
        fields = [inv * b for b in loads]
        image = images(f, 0, fields)
        nexts = [inv * t for t in image]
        for k in range(2):
            field_ref[2 * f + k] = nexts[k]
        put_dot(0, f, zip(fields, loads))
        put_dot(1, f, zip(fields, image))
        put_dot(2, f, zip(nexts, image))
        return carry

    def second(f, carry):
        inv = inv_ref[f]
        fields = [field_ref[2 * f + k] for k in range(2)]
        image = images(f, 1, fields)
        nexts = [inv * t for t in image]
        for k in range(2):
            field_ref[2 * f + k] = nexts[k]
        put_dot(3, f, zip(fields, image))
        put_dot(4, f, zip(nexts, image))
        return carry

    def third(f, carry):
        fields = [field_ref[2 * f + k] for k in range(2)]
        total, extra = 0.0, 0.0
        for k, z in enumerate(products(*fields)):
            z11, z22, z12, _, s_top, s_low = z
            added, added_strain = borders(2, f, k)
            twice = 2.0 * (later(mod_sent_down * z12) + added)
            total = total + fields[k] * (mod_own * z11 + mod_sent_down * z22 + twice)
            strain = strain_of(s_top, s_low, added_strain)
            put_strain(2, f, k, strain)
            extra = extra + strain[6:7]
        dots_ref[pl.ds(5 * freqs + f, 1), :] = -(jnp.sum(total, axis=0, keepdims=True) + extra)
        return carry

    lax.fori_loop(0, freqs, first, 0, unroll=2)
    lax.fori_loop(0, freqs, second, 0, unroll=2)
    lax.fori_loop(0, freqs, third, 0, unroll=2)

    dots_ref[DOTS * freqs :, :] = jnp.zeros((256 - DOTS * freqs, LANES), F32)
    sums = lax.dot_general(
        jnp.ones((8, LANES), F32), dots_ref[...], (((1,), (1,)), ((), ())),
        precision=lax.Precision.HIGHEST, preferred_element_type=F32,
    )
    row = lax.broadcasted_iota(jnp.int32, (8, LANES), 0)
    pair = jnp.where(row % 2 == 0, sums[:, :LANES], sums[:, LANES:])
    for i in range(dots_out_ref.shape[0] // 8):
        dots_out_ref[8 * i : 8 * i + 8, :] = pair

    quarter = LANES // 4
    cell = lane_ids(8) // quarter
    outs = (out0_ref, out1_ref, out2_ref, out3_ref)

    def pack(block, carry):
        comps = [
            strain_ref[pl.ds(block * 64 + c, 8, stride=8), :] for c in range(6)
        ]
        for step in range(4):
            dest = (freq_group + step) % 4
            for side in range(2):
                held = jnp.zeros((8, LANES), F32)
                for c in range(4 * side, min(6, 4 * side + 4)):
                    moved = pltpu.roll(comps[c], quarter * ((c + 4 - dest) % 4), 1)
                    held = jnp.where(cell == c % 4, moved, held)
                start = pl.multiple_of(side * 3 * parts + block * 8, 8)
                outs[step][pl.ds(start, 8), :] = held
        return carry

    lax.fori_loop(0, 3 * parts // 8, pack, 0, unroll=2)


def coefficients(h):
    def dot(a, b, energy):
        total = None
        for i, x in enumerate(a):
            for j, y in enumerate(b):
                weight = h[i + j] - h[i + j + 1] if energy else h[i + j]
                term = x * y * weight
                total = term if total is None else total + term
        return total

    one = jnp.ones_like(h[0])
    residual, direction = [one], [one]
    rho = h[0]
    result = []
    for iteration in range(3):
        alpha = rho / dot(direction, direction, True)
        result = [
            (result[i] if i < len(result) else 0.0) + alpha * direction[i]
            for i in range(len(direction))
        ]
        if iteration == 2:
            break
        image = (
            [direction[0]]
            + [direction[i] - direction[i - 1] for i in range(1, len(direction))]
            + [-direction[-1]]
        )
        residual = [
            (residual[i] if i < len(residual) else 0.0) - alpha * image[i]
            for i in range(len(image))
        ]
        rho_next = dot(residual, residual, False)
        beta = rho_next / rho
        rho = rho_next
        direction = [
            residual[i] + (beta * direction[i] if i < len(direction) else 0.0)
            for i in range(len(residual))
        ]
    return result


def final_kernel(
    info_ref, curves_ref, dots_ref, part0_ref, part1_ref, part2_ref, part3_ref,
    table_high_ref, table_low_ref, modulus_ref, soil_ref,
    modulus_out_ref, strain_out_ref, spectra_ref,
):
    freq_group = info_ref[0]
    parts, freqs = 64, 32
    total = jnp.zeros((8, LANES), F32)
    for i in range(dots_ref.shape[0] // 8):
        total = total + dots_ref[8 * i : 8 * i + 8, :]
    square = jnp.concatenate([total, jnp.zeros((LANES - 8, LANES), F32)], 0)
    turned = jnp.transpose(square)
    beside = pltpu.roll(turned, 127, 1)
    h = [turned[freqs * i : freqs * (i + 1)] for i in range(4)]
    h += [beside[freqs * i : freqs * (i + 1)] for i in range(2)]
    coefs = coefficients(h)
    lanes = lane_ids(freqs)
    for step, part_ref in enumerate((part0_ref, part1_ref, part2_ref, part3_ref)):
        source = (freq_group + 4 - step) % 4
        weights = [
            jnp.sum(jnp.where(lanes == 2 * source, c, 0.0), axis=1, keepdims=True) for c in coefs
        ]
        for k in range(2):
            start = pl.multiple_of(source * parts + k * freqs, freqs)
            for side in range(2):
                value = None
                for j in range(3):
                    at = (side * 3 + j) * parts + k * freqs
                    term = weights[j] * part_ref[at : at + freqs, :]
                    value = term if value is None else value + term
                spectra_ref[pl.ds(start, freqs), side * LANES : (side + 1) * LANES] = value
    high, low = halves(spectra_ref[...])
    table_high, table_low = table_high_ref[...], table_low_ref[...]
    history = (
        jnp.dot(table_high, low, preferred_element_type=F32)
        + jnp.dot(table_low, high, preferred_element_type=F32)
        + jnp.dot(table_high, high, preferred_element_type=F32)
    )
    squares = history[:, :LANES] ** 2 + history[:, LANES:] ** 2
    squares = squares + pltpu.roll(squares, 64, 1)
    squares = squares + pltpu.roll(squares, 32, 1)
    peak = jnp.max(squares, axis=0, keepdims=True)[:, : LANES // 4] * (1.0 / (4 * freqs))
    peak_strain = STRAIN_FACTOR * jnp.sqrt(peak + EPSILON)
    position = (jnp.log(peak_strain) * (1.0 / np.log(10.0)) - LOG_LOW) / LOG_STEP
    soil = soil_ref[...]
    ratio = jnp.zeros_like(position)
    for level in range(curves_ref.shape[1]):
        value = jnp.where(soil == 0, curves_ref[0, level], 0.0)
        for kind in range(1, curves_ref.shape[0]):
            value = jnp.where(soil == kind, curves_ref[kind, level], value)
        ratio = ratio + value * jnp.maximum(0.0, 1.0 - jnp.abs(position - level))
    own = pltpu.roll(modulus_ref[...], (LANES - LANES // 4 * freq_group) % LANES, 1)
    modulus_out_ref[...] = own[:, : LANES // 4] * ratio
    strain_out_ref[...] = peak_strain


def time_table(total_freq):
    order = np.arange(1, total_freq + 1)
    phase = (np.arange(NT)[:, None] * order[None, :] % NT) * (2.0 * np.pi / NT)
    waves = np.stack([np.cos(phase), -np.sin(phase)], 1)
    table = waves.reshape(NT, 2, 4, total_freq // 4).transpose(0, 2, 1, 3).reshape(NT, -1)
    high = table.astype(np.float32).astype(jnp.bfloat16)
    low = (table - high.astype(np.float64)).astype(np.float32).astype(jnp.bfloat16)
    return high, low


def per_device(
    load, stiffness, mass_template, modulus, element_mass, strain_map, curves, soil_type
):
    half, freq_dev, _, nodes = load.shape
    parts = 2 * freq_dev
    groups = lax.axis_size("freq")
    slabs = lax.axis_size("elem")
    freq_group = lax.axis_index("freq")
    is_last = (lax.axis_index("elem") == slabs - 1).astype(jnp.int32)
    info = jnp.stack([freq_group.astype(jnp.int32), is_last])
    rows = load.reshape(half * parts, nodes)
    modulus_row, mass_row = modulus.reshape(1, nodes), element_mass.reshape(1, nodes)
    edge_rows = parts // PER_PATCH * half + 8
    edges = pl.pallas_call(
        edges_kernel,
        out_shape=jax.ShapeDtypeStruct((edge_rows, LANES), F32),
        in_specs=[VMEM] * 3,
        out_specs=VMEM,
        name="edges",
    )(rows, modulus_row, mass_row)
    from_left = lax.ppermute(edges, "elem", [(i, i + 1) for i in range(slabs - 1)])
    from_right = lax.ppermute(edges, "elem", [(i + 1, i) for i in range(slabs - 1)])

    kdiag = jnp.diagonal(stiffness)
    off = stiffness * (1.0 - jnp.eye(2 * half, dtype=F32))
    comps = strain_map.shape[0]
    strain_rows = jnp.pad(strain_map, ((0, 8 - comps), (0, 0)))
    stacked = jnp.concatenate(
        [off[:half, :half], off[half:, half:], off[:half, half:], off[half:, :half],
         strain_rows[:, :half], strain_rows[:, half:]], 0
    )
    high, low = halves(stacked)
    lhs = jnp.concatenate([high, high, low], 1)
    cols = jnp.stack([kdiag[:half], kdiag[half:], mass_template[:half], mass_template[half:]], 1)
    packed = 6 * parts
    outs = pl.pallas_call(
        main_kernel,
        out_shape=[jax.ShapeDtypeStruct((packed, LANES), F32)] * 4
        + [jax.ShapeDtypeStruct((2 * slabs * groups, LANES), F32)],
        in_specs=[SMEM] + [VMEM] * 6,
        out_specs=[VMEM] * 5,
        scratch_shapes=[
            pltpu.VMEM((parts, half, LANES), F32),
            pltpu.VMEM((freq_dev, half, LANES), F32),
            pltpu.VMEM((3 * parts * 8, LANES), F32),
            pltpu.VMEM((3 * parts // PER_PATCH, half + 8, LANES), F32),
            pltpu.VMEM((256, LANES), F32),
        ],
        compiler_params=pltpu.CompilerParams(vmem_limit_bytes=32 * 1024 * 1024),
        name="krylov",
    )(info, rows, edges, from_left, from_right, lhs, cols)
    received = [outs[0]] + [
        lax.ppermute(outs[step], "freq", [(i, (i + step) % groups) for i in range(groups)])
        for step in range(1, groups)
    ]
    dots = lax.all_to_all(
        outs[4].reshape(slabs * groups, 2, LANES), ("elem", "freq"), 0, 0
    ).reshape(-1, LANES)
    table_high, table_low = time_table(freq_dev * groups)
    quarter = nodes // groups
    new_modulus, peak_strain = pl.pallas_call(
        final_kernel,
        out_shape=[jax.ShapeDtypeStruct((1, quarter), F32)] * 2,
        in_specs=[SMEM] * 2 + [VMEM] * 9,
        out_specs=[VMEM] * 2,
        scratch_shapes=[pltpu.VMEM((groups * parts, 2 * LANES), F32)],
        compiler_params=pltpu.CompilerParams(vmem_limit_bytes=32 * 1024 * 1024),
        name="response",
    )(info, curves, dots, *received, jnp.asarray(table_high), jnp.asarray(table_low),
      modulus_row, soil_type.reshape(1, quarter))
    return new_modulus.reshape(quarter), peak_strain.reshape(quarter)


def solution(mesh):
    in_specs = (
        P(None, "freq", None, "elem"),
        P(),
        P(),
        P("elem"),
        P("elem"),
        P(),
        P(),
        P(("elem", "freq")),
    )
    out_specs = (P(("elem", "freq")), P(("elem", "freq")))
    return jax.shard_map(
        per_device, mesh=mesh, in_specs=in_specs, out_specs=out_specs, check_vma=False
    )
```

time: 590 us -> 61.5 us (0.10)
  blocking collectives: 315 us -> 20.2 us
  local copies, waits for them, and re-layouts: 95.1 us -> 2.05 us
  other arithmetic: 79.5 us -> 0.27 us
  waiting for transfers between devices: 26.9 us -> 0.01 us
  matrix products: 25.8 us -> 0 us
  Pallas kernels: 0 us -> 25.5 us
  starting transfers between devices: 28.6 us -> 12.4 us
  between operations: 14.7 us -> 0.88 us
    psum x5 -> x0, blocking collectives: 315 us -> none  [the longest x3 192 us: norm_sum(): return lax.psum(local_dot(residual, precond), 'elem')]
    reshape x11 -> x0, local copies, waits for them, and re-layouts: 54.6 us -> none  [the longest x6 32.4 us: operate(): jnp.dot(stiffness, stacked.reshape(2 * half_size, -1), precision=PRECISE)]
    add x7 -> x0, other arithmetic: 35.7 us -> none  [the longest x3 19.5 us: operate(): modulus * product]
    dot_general x6 -> x0, matrix products: 25.8 us -> none  [the longest x3 19.3 us: operate(): jnp.dot(stiffness, stacked.reshape(2 * half_size, -1), precision=PRECISE)]
    pallas_call x0 -> x3, Pallas kernels: none -> 25.5 us  [the longest x1 20.3 us: per_device(): pl.pallas_call(main_kernel, out_shape=[jax.ShapeDtypeStruct((packed, LANE...]
    reduce_scatter x1 -> x0, waiting for transfers between devices: 22.1 us -> none  [per_device(): lax.psum_scatter(partials, 'freq', scatter_dimension=2, tiled=True) * scale]
    reduce_sum x6 -> x0, other arithmetic: 21.2 us -> none  [the longest x5 20.2 us: local_dot(): return jnp.sum(left * right, axis=(0, 2, 3))]
    concatenate x4 -> x2, local copies, waits for them, and re-layouts: 21 us -> 0.21 us  [per_device(): jnp.concatenate([off[:half, :half], off[half:, half:], off[:half, half:],...]
  transfers between devices with their start and end apart: 10 -> 5, of which waited for: 4 -> 0; matrix products, arithmetic and copies ran while one was open for 3% -> 4% of each run, Pallas kernels for 0% -> 0%
where the time goes in v1:
time: 61.5 us; the launch traced here: 61.3 us
  Pallas kernels  25.5 us (41%)
  blocking collectives  20.2 us (33%)
  starting transfers between devices  12.4 us (20%)
  local copies, waits for them, and re-layouts  2.05 us (3%)
  between operations  0.88 us (1%)
    pallas_call x1, Pallas kernels, per_device(): pl.pallas_call(main_kernel, out_shape=[jax.ShapeDtypeStruct((packed, LANE...  20.3 us
    all_to_all x1, blocking collectives, per_device(): lax.all_to_all(outs[4].reshape(slabs * groups, 2, LANES), ('elem', 'freq'...  20.2 us
    ppermute x3, starting transfers between devices, per_device(): lax.ppermute(outs[step], 'freq', [(i, (i + step) % groups) for i in range...  5.74 us
    ppermute x1, starting transfers between devices, per_device(): lax.ppermute(edges, 'elem', [(i + 1, i) for i in range(slabs - 1)])  3.45 us
    pallas_call x1, Pallas kernels, per_device(): pl.pallas_call(edges_kernel, out_shape=jax.ShapeDtypeStruct((edge_rows, L...  3.22 us
    ppermute x1, starting transfers between devices, per_device(): lax.ppermute(edges, 'elem', [(i, i + 1) for i in range(slabs - 1)])  3.18 us
    pallas_call x1, Pallas kernels, per_device(): pl.pallas_call(final_kernel, out_shape=[jax.ShapeDtypeStruct((1, quarter)...  2 us
    gather x1, local copies, waits for them, and re-layouts, per_device(): kdiag = jnp.diagonal(stiffness)  1.25 us
  transfers between devices with their start and end apart: 5, of which 0 were waited for; matrix products, arithmetic and copies ran while one was open for 4% of the time, Pallas kernels for 0%

profile of v1, /device:TPU:1, one launch (start us, length us, event | category | flops | bytes accessed | tf_op | source)
XLA Modules:
  0.0 61.3 jit_solution(6492919859044582865)
XLA Ops:
  0.7 3.2 %edges.1.own_ref = f32[200,128]{1,0:T(8,128)} custom-call(f32[3072,128]{1,0:T(8,128)} %bitcast.20, f32[1,128]{1,0:T(1,128)} %bitcast.24, f32[1,128]{1,0:T(1,128)} %bitcast.27), custom_call_target="tpu_custom_call" | custom-call | tf_op jit(solution)/shard_map/edges/pallas_call | solution.py:400
  3.9 3.4 %collective-permute-start.1 = (f32[200,128]{1,0:T(8,128)}, f32[200,128]{1,0:T(8,128)S(1)}, u32[]{:S(2)}, u32[]{:S(2)}) collective-permute-start(f32[200,128]{1,0:T(8,128)} %edges.1.own_ref), channel_id=1, source_target_pairs={{4,0},{8,4},{12,8},{16,12},{20,16},{24,20},{28,24},{32,28},{36,32}... | collective-permute-start | bytes 307208 | tf_op jit(solution)/shard_map/ppermute | solution.py:408
  7.3 3.2 %collective-permute-start = (f32[200,128]{1,0:T(8,128)}, f32[200,128]{1,0:T(8,128)S(1)}, u32[]{:S(2)}, u32[]{:S(2)}) collective-permute-start(f32[200,128]{1,0:T(8,128)} %edges.1.own_ref), channel_id=1, source_target_pairs={{0,4},{4,8},{8,12},{12,16},{16,20},{20,24},{24,28},{28,32},{32,36}... | collective-permute-start | bytes 307208 | tf_op jit(solution)/shard_map/ppermute | solution.py:407
  10.6 0.1 copy.26
  10.7 0.1 copy.25
  10.8 0.1 fusion
  10.9 0.1 concatenate.10
  11.0 0.1 copy.28
  11.1 0.0 copy-start.2
  11.1 0.0 copy-start.3
  11.1 0.0 copy-start.4
  11.2 0.0 copy-start.6
  11.2 1.2 %gather_fusion = f32[96]{0:T(128)S(1)} fusion(f32[96,96]{1,0:T(8,128)S(1)} %copy-done.7, s32[96]{0:T(128)S(1)} %or_bitcast_fusion), kind=kCustom, calls=%fused_computation | custom fusion | bytes 1536 | tf_op jit(solution)/shard_map/jit(diagonal)/cond/branch_0_fun/gather | solution.py:410
  12.4 0.1 slice_bitcast_fusion.1
  12.5 0.1 copy.31.cols_ref
  12.6 0.1 copy.29
  12.8 0.1 pad_maximum_fusion.lhs_ref
  12.9 0.1 pad_add_fusion.info_ref
  13.0 20.3 %krylov.1 = (f32[384,128]{1,0:T(8,128)S(1)}, f32[384,128]{1,0:T(8,128)S(1)}, f32[384,128]{1,0:T(8,128)S(1)}, f32[384,128]{1,0:T(8,128)S(1)}, f32[256,128]{1,0:T(8,128)S(1)}) custom-call(s32[2]{0:T(128)S(1)} %pad_add_fusion.info_ref, f32[3072,128]{1,0:T(8,128)S(1)} %bitcast.21, f32[200,128]{1,0:T(8,128)S(1)} %copy-done.1, ...), custom_call_target="tpu_custom_call" | custom-call | tf_op jit(solution)/shard_map/krylov/pallas_call | solution.py:422
  33.3 1.7 %collective-permute-start.2 = (f32[384,128]{1,0:T(8,128)S(1)}, f32[384,128]{1,0:T(8,128)S(1)}, u32[]{:S(2)}, u32[]{:S(2)}) collective-permute-start(f32[384,128]{1,0:T(8,128)S(1)} %get-tuple-element.11), channel_id=1, source_target_pairs={{0,1},{1,2},{2,3},{3,0},{4,5},{5,6},{6,7},{7,4},{8,9},{9,10},{10,1... | collective-permute-start | bytes 589832 | tf_op jit(solution)/shard_map/ppermute | solution.py:439
  35.0 3.3 %collective-permute-start.3 = (f32[384,128]{1,0:T(8,128)S(1)}, f32[384,128]{1,0:T(8,128)S(1)}, u32[]{:S(2)}, u32[]{:S(2)}) collective-permute-start(f32[384,128]{1,0:T(8,128)S(1)} %get-tuple-element.12), channel_id=1, source_target_pairs={{0,2},{1,3},{2,0},{3,1},{4,6},{5,7},{6,4},{7,5},{8,10},{9,11},{10,... | collective-permute-start | bytes 589832 | tf_op jit(solution)/shard_map/ppermute | solution.py:439
  38.3 0.7 %collective-permute-start.4 = (f32[384,128]{1,0:T(8,128)S(1)}, f32[384,128]{1,0:T(8,128)S(1)}, u32[]{:S(2)}, u32[]{:S(2)}) collective-permute-start(f32[384,128]{1,0:T(8,128)S(1)} %get-tuple-element.13), channel_id=1, source_target_pairs={{0,3},{1,0},{2,1},{3,2},{4,7},{5,4},{6,5},{7,6},{8,11},{9,8},{10,9... | collective-permute-start | bytes 589832 | tf_op jit(solution)/shard_map/ppermute | solution.py:439
  39.0 20.2 %all_to_all.5 = f32[128,2,128]{2,1,0:T(2,128)S(1)} all-to-all(f32[128,2,128]{2,1,0:T(2,128)S(1)} %bitcast.23), channel_id=1, replica_groups=mesh['elem'=32,'freq'=4] {'elem','freq'}, dimensions={0} | all-to-all | bytes 262144 | tf_op jit(solution)/shard_map/all_to_all | solution.py:442
  59.3 2.0 %response.1 = (f32[1,32]{1,0:T(1,128)}, f32[1,32]{1,0:T(1,128)}) custom-call(s32[2]{0:T(128)S(1)} %pad_add_fusion.info_ref, f32[4,16]{1,0:T(4,128)S(1)} %copy-done.4, f32[256,128]{1,0:T(8,128)S(1)} %bitcast.22, f32[384,128]{1,0:T(8,128)S(1)} %get-tuple-element.10.part0_ref, f32[384,128]{1,0:T(8,128)S(1)} %collective-permute-done.2.part1_ref, ...), custom_call_target="tpu_custom_call" | custom-call | tf_op jit(solution)/shard_map/response/pallas_call | solution.py:447
  (27 shorter events, 0.1 us)
Async XLA Ops:
  0.6 9.9 %copy-start.8 = (f32[6,96]{1,0:T(8,128)S(1)}, f32[6,96]{1,0:T(8,128)}, u32[]{:S(2)}) copy-start(f32[6,96]{1,0:T(8,128)} %param.15) | copy-start | bytes 6916
  0.6 10.0 %copy-start.7 = (f32[96,96]{1,0:T(8,128)S(1)}, f32[96,96]{1,0:T(8,128)}, u32[]{:S(2)}) copy-start(f32[96,96]{1,0:T(8,128)} %param.11) | copy-start | bytes 110596
  0.7 11.8 %copy-start.9 = (f32[96]{0:T(128)S(1)}, f32[96]{0:T(128)}, u32[]{:S(2)}) copy-start(f32[96]{0:T(128)} %param.12) | copy-start | bytes 1156
  0.7 12.3 %copy-start = (f32[48,32,2,128]{3,2,1,0:T(2,128)S(1)}, f32[48,32,2,128]{3,2,1,0:T(2,128)}, u32[]{:S(2)}) copy-start(f32[48,32,2,128]{3,2,1,0:T(2,128)} %param.10) | copy-start | bytes 4718596
  3.9 9.1 %copy-start.1 = (f32[200,128]{1,0:T(8,128)S(1)}, f32[200,128]{1,0:T(8,128)}, u32[]{:S(2)}) copy-start(f32[200,128]{1,0:T(8,128)} %edges.1.own_ref) | copy-start | bytes 307204
  3.9 9.1 %collective-permute-start.1 = (f32[200,128]{1,0:T(8,128)}, f32[200,128]{1,0:T(8,128)S(1)}, u32[]{:S(2)}, u32[]{:S(2)}) collective-permute-start(f32[200,128]{1,0:T(8,128)} %edges.1.own_ref), channel_id=1, source_target_pairs={{4,0},{8,4},{12,8},{16,12},{20,16},{24,20},{28,24},{32,28},{36,32}... | collective-permute-start | bytes 307208 | tf_op jit(solution)/shard_map/ppermute | solution.py:408
  7.3 5.6 %collective-permute-start = (f32[200,128]{1,0:T(8,128)}, f32[200,128]{1,0:T(8,128)S(1)}, u32[]{:S(2)}, u32[]{:S(2)}) collective-permute-start(f32[200,128]{1,0:T(8,128)} %edges.1.own_ref), channel_id=1, source_target_pairs={{0,4},{4,8},{8,12},{12,16},{16,20},{20,24},{24,28},{28,32},{32,36}... | collective-permute-start | bytes 307208 | tf_op jit(solution)/shard_map/ppermute | solution.py:407
  11.1 48.2 %copy-start.2 = (bf16[512,256]{1,0:T(8,128)(2,1)S(1)}, bf16[512,256]{1,0:T(8,128)(2,1)}, u32[]{:S(2)}) copy-start(bf16[512,256]{1,0:T(8,128)(2,1)} %constant.26.clone.table_low_ref) | copy-start | bytes 786436
  11.1 48.2 %copy-start.3 = (bf16[512,256]{1,0:T(8,128)(2,1)S(1)}, bf16[512,256]{1,0:T(8,128)(2,1)}, u32[]{:S(2)}) copy-start(bf16[512,256]{1,0:T(8,128)(2,1)} %constant.25.clone.table_high_ref) | copy-start | bytes 786436
  11.1 48.2 %copy-start.4 = (f32[4,16]{1,0:T(4,128)S(1)}, f32[4,16]{1,0:T(4,128)}, u32[]{:S(2)}) copy-start(f32[4,16]{1,0:T(4,128)} %curves_ref.1) | copy-start | bytes 772
  11.2 48.2 %copy-start.5 = (f32[128]{0:T(128)S(1)}, f32[128]{0:T(128)}, u32[]{:S(2)}) copy-start(f32[128]{0:T(128)} %param.13) | copy-start | bytes 1540
  11.2 48.2 %copy-start.6 = (s32[32]{0:T(128)S(1)}, s32[32]{0:T(128)}, u32[]{:S(2)}) copy-start(s32[32]{0:T(128)} %param.17) | copy-start | bytes 388
  33.3 26.0 %collective-permute-start.2 = (f32[384,128]{1,0:T(8,128)S(1)}, f32[384,128]{1,0:T(8,128)S(1)}, u32[]{:S(2)}, u32[]{:S(2)}) collective-permute-start(f32[384,128]{1,0:T(8,128)S(1)} %get-tuple-element.11), channel_id=1, source_target_pairs={{0,1},{1,2},{2,3},{3,0},{4,5},{5,6},{6,7},{7,4},{8,9},{9,10},{10,1... | collective-permute-start | bytes 589832 | tf_op jit(solution)/shard_map/ppermute | solution.py:439
  35.0 24.3 %collective-permute-start.3 = (f32[384,128]{1,0:T(8,128)S(1)}, f32[384,128]{1,0:T(8,128)S(1)}, u32[]{:S(2)}, u32[]{:S(2)}) collective-permute-start(f32[384,128]{1,0:T(8,128)S(1)} %get-tuple-element.12), channel_id=1, source_target_pairs={{0,2},{1,3},{2,0},{3,1},{4,6},{5,7},{6,4},{7,5},{8,10},{9,11},{10,... | collective-permute-start | bytes 589832 | tf_op jit(solution)/shard_map/ppermute | solution.py:439
  38.3 21.0 %collective-permute-start.4 = (f32[384,128]{1,0:T(8,128)S(1)}, f32[384,128]{1,0:T(8,128)S(1)}, u32[]{:S(2)}, u32[]{:S(2)}) collective-permute-start(f32[384,128]{1,0:T(8,128)S(1)} %get-tuple-element.13), channel_id=1, source_target_pairs={{0,3},{1,0},{2,1},{3,2},{4,7},{5,4},{6,5},{7,6},{8,11},{9,8},{10,9... | collective-permute-start | bytes 589832 | tf_op jit(solution)/shard_map/ppermute | solution.py:439

commit v2 on v1

--- a/solution.py
+++ b/solution.py
@@ -15,6 +15,7 @@
 LANES = 128
 SLOT = 8
 PER_PATCH = LANES // SLOT
+UNROLL = 32
 DOTS = 6
 F32 = jnp.float32
 BF16 = jnp.bfloat16
@@ -67,8 +68,7 @@
 
 def main_kernel(
     info_ref, load_ref, own_ref, left_ref, right_ref, lhs_ref, cols_ref,
-    out0_ref, out1_ref, out2_ref, out3_ref, dots_out_ref,
-    field_ref, inv_ref, strain_ref, border_ref, dots_ref,
+    strain_ref, dots_out_ref, field_ref, inv_ref, border_ref, dots_ref,
 ):
     half = lhs_ref.shape[1] // 3
     parts = 64
@@ -241,9 +241,9 @@
         dots_ref[pl.ds(5 * freqs + f, 1), :] = -(jnp.sum(total, axis=0, keepdims=True) + extra)
         return carry
 
-    lax.fori_loop(0, freqs, first, 0, unroll=2)
-    lax.fori_loop(0, freqs, second, 0, unroll=2)
-    lax.fori_loop(0, freqs, third, 0, unroll=2)
+    lax.fori_loop(0, freqs, first, 0, unroll=UNROLL)
+    lax.fori_loop(0, freqs, second, 0, unroll=UNROLL)
+    lax.fori_loop(0, freqs, third, 0, unroll=UNROLL)
 
     dots_ref[DOTS * freqs :, :] = jnp.zeros((256 - DOTS * freqs, LANES), F32)
     sums = lax.dot_general(
@@ -254,27 +254,6 @@
     pair = jnp.where(row % 2 == 0, sums[:, :LANES], sums[:, LANES:])
     for i in range(dots_out_ref.shape[0] // 8):
         dots_out_ref[8 * i : 8 * i + 8, :] = pair
-
-    quarter = LANES // 4
-    cell = lane_ids(8) // quarter
-    outs = (out0_ref, out1_ref, out2_ref, out3_ref)
-
-    def pack(block, carry):
-        comps = [
-            strain_ref[pl.ds(block * 64 + c, 8, stride=8), :] for c in range(6)
-        ]
-        for step in range(4):
-            dest = (freq_group + step) % 4
-            for side in range(2):
-                held = jnp.zeros((8, LANES), F32)
-                for c in range(4 * side, min(6, 4 * side + 4)):
-                    moved = pltpu.roll(comps[c], quarter * ((c + 4 - dest) % 4), 1)
-                    held = jnp.where(cell == c % 4, moved, held)
-                start = pl.multiple_of(side * 3 * parts + block * 8, 8)
-                outs[step][pl.ds(start, 8), :] = held
-        return carry
-
-    lax.fori_loop(0, 3 * parts // 8, pack, 0, unroll=2)
 
 
 def coefficients(h):
@@ -318,37 +297,55 @@
     return result
 
 
+def combine_kernel(info_ref, dots_ref, strain_ref, out0_ref, out1_ref, out2_ref, out3_ref):
+    freq_group = info_ref[0]
+    freqs, comps = 32, 6
+    total = jnp.zeros((8, LANES), F32)
+    for i in range(dots_ref.shape[0] // 8):
+        total = total + dots_ref[8 * i : 8 * i + 8, :]
+    square = jnp.concatenate([total, jnp.zeros((LANES - 8, LANES), F32)], 0)
+    turned = jnp.transpose(square)
+    odd = lane_ids(LANES) % 2 == 1
+    even_sums = jnp.sum(jnp.where(odd, 0.0, turned), axis=1, keepdims=True)
+    odd_sums = jnp.sum(jnp.where(odd, turned, 0.0), axis=1, keepdims=True)
+    h = [even_sums[freqs * i : freqs * (i + 1)] for i in range(4)]
+    h += [odd_sums[freqs * i : freqs * (i + 1)] for i in range(2)]
+    weights = [jnp.broadcast_to(c, (freqs, LANES)) for c in coefficients(h)]
+    quarter = LANES // 4
+    cell = lane_ids(freqs) // quarter
+    outs = (out0_ref, out1_ref, out2_ref, out3_ref)
+    for k in range(2):
+        spectra = [
+            sum(
+                weights[j] * strain_ref[pl.ds((2 * j + k) * freqs * 8 + c, freqs, stride=8), :]
+                for j in range(3)
+            )
+            for c in range(comps)
+        ]
+        for step in range(4):
+            dest = (freq_group + step) % 4
+            for side in range(2):
+                held = jnp.zeros((freqs, LANES), F32)
+                for c in range(4 * side, min(comps, 4 * side + 4)):
+                    moved = pltpu.roll(spectra[c], quarter * ((c + 4 - dest) % 4), 1)
+                    held = jnp.where(cell == c % 4, moved, held)
+                start = (2 * side + k) * freqs
+                outs[step][start : start + freqs, :] = held
+
+
 def final_kernel(
-    info_ref, curves_ref, dots_ref, part0_ref, part1_ref, part2_ref, part3_ref,
+    info_ref, curves_ref, part0_ref, part1_ref, part2_ref, part3_ref,
     table_high_ref, table_low_ref, modulus_ref, soil_ref,
     modulus_out_ref, strain_out_ref, spectra_ref,
 ):
     freq_group = info_ref[0]
     parts, freqs = 64, 32
-    total = jnp.zeros((8, LANES), F32)
-    for i in range(dots_ref.shape[0] // 8):
-        total = total + dots_ref[8 * i : 8 * i + 8, :]
-    square = jnp.concatenate([total, jnp.zeros((LANES - 8, LANES), F32)], 0)
-    turned = jnp.transpose(square)
-    beside = pltpu.roll(turned, 127, 1)
-    h = [turned[freqs * i : freqs * (i + 1)] for i in range(4)]
-    h += [beside[freqs * i : freqs * (i + 1)] for i in range(2)]
-    coefs = coefficients(h)
-    lanes = lane_ids(freqs)
     for step, part_ref in enumerate((part0_ref, part1_ref, part2_ref, part3_ref)):
-        source = (freq_group + 4 - step) % 4
-        weights = [
-            jnp.sum(jnp.where(lanes == 2 * source, c, 0.0), axis=1, keepdims=True) for c in coefs
-        ]
-        for k in range(2):
-            start = pl.multiple_of(source * parts + k * freqs, freqs)
-            for side in range(2):
-                value = None
-                for j in range(3):
-                    at = (side * 3 + j) * parts + k * freqs
-                    term = weights[j] * part_ref[at : at + freqs, :]
-                    value = term if value is None else value + term
-                spectra_ref[pl.ds(start, freqs), side * LANES : (side + 1) * LANES] = value
+        start = pl.multiple_of((freq_group + 4 - step) % 4 * parts, parts)
+        for side in range(2):
+            spectra_ref[pl.ds(start, parts), side * LANES : (side + 1) * LANES] = part_ref[
+                side * parts : (side + 1) * parts, :
+            ]
     high, low = halves(spectra_ref[...])
     table_high, table_low = table_high_ref[...], table_low_ref[...]
     history = (
@@ -418,41 +415,46 @@
     high, low = halves(stacked)
     lhs = jnp.concatenate([high, high, low], 1)
     cols = jnp.stack([kdiag[:half], kdiag[half:], mass_template[:half], mass_template[half:]], 1)
-    packed = 6 * parts
-    outs = pl.pallas_call(
+    strains, dots = pl.pallas_call(
         main_kernel,
-        out_shape=[jax.ShapeDtypeStruct((packed, LANES), F32)] * 4
-        + [jax.ShapeDtypeStruct((2 * slabs * groups, LANES), F32)],
+        out_shape=[
+            jax.ShapeDtypeStruct((3 * parts * 8, LANES), F32),
+            jax.ShapeDtypeStruct((2 * slabs, LANES), F32),
+        ],
         in_specs=[SMEM] + [VMEM] * 6,
-        out_specs=[VMEM] * 5,
+        out_specs=[VMEM] * 2,
         scratch_shapes=[
             pltpu.VMEM((parts, half, LANES), F32),
             pltpu.VMEM((freq_dev, half, LANES), F32),
-            pltpu.VMEM((3 * parts * 8, LANES), F32),
             pltpu.VMEM((3 * parts // PER_PATCH, half + 8, LANES), F32),
             pltpu.VMEM((256, LANES), F32),
         ],
         compiler_params=pltpu.CompilerParams(vmem_limit_bytes=32 * 1024 * 1024),
         name="krylov",
     )(info, rows, edges, from_left, from_right, lhs, cols)
+    dots = lax.all_to_all(dots.reshape(slabs, 2, LANES), "elem", 0, 0).reshape(-1, LANES)
+    outs = pl.pallas_call(
+        combine_kernel,
+        out_shape=[jax.ShapeDtypeStruct((2 * parts, LANES), F32)] * groups,
+        in_specs=[SMEM] + [VMEM] * 2,
+        out_specs=[VMEM] * groups,
+        name="combine",
+    )(info, dots, strains)
     received = [outs[0]] + [
         lax.ppermute(outs[step], "freq", [(i, (i + step) % groups) for i in range(groups)])
         for step in range(1, groups)
     ]
-    dots = lax.all_to_all(
-        outs[4].reshape(slabs * groups, 2, LANES), ("elem", "freq"), 0, 0
-    ).reshape(-1, LANES)
     table_high, table_low = time_table(freq_dev * groups)
     quarter = nodes // groups
     new_modulus, peak_strain = pl.pallas_call(
         final_kernel,
         out_shape=[jax.ShapeDtypeStruct((1, quarter), F32)] * 2,
-        in_specs=[SMEM] * 2 + [VMEM] * 9,
+        in_specs=[SMEM] * 2 + [VMEM] * 8,
         out_specs=[VMEM] * 2,
         scratch_shapes=[pltpu.VMEM((groups * parts, 2 * LANES), F32)],
         compiler_params=pltpu.CompilerParams(vmem_limit_bytes=32 * 1024 * 1024),
         name="response",
-    )(info, curves, dots, *received, jnp.asarray(table_high), jnp.asarray(table_low),
+    )(info, curves, *received, jnp.asarray(table_high), jnp.asarray(table_low),
       modulus_row, soil_type.reshape(1, quarter))
     return new_modulus.reshape(quarter), peak_strain.reshape(quarter)
 

time: 61.5 us -> 52.7 us (0.86)
  Pallas kernels: 25.5 us -> 14.4 us
  blocking collectives: 20.2 us -> 16.8 us
  waiting for transfers between devices: 0.01 us -> 2.9 us
  local copies, waits for them, and re-layouts: 2.05 us -> 4.45 us
    pallas_call x1 -> x2, Pallas kernels: 20.3 us -> 9.5 us  [the longest x1 7.14 us: per_device(): pl.pallas_call(main_kernel, out_shape=[jax.ShapeDtypeStruct((3 * parts *...]
    all_to_all x1, blocking collectives: 20.2 us -> 16.8 us  [per_device(): lax.all_to_all(dots.reshape(slabs, 2, LANES), 'elem', 0, 0)]
    ppermute x3, waiting for transfers between devices: 0.01 us -> 2.89 us  [per_device(): lax.ppermute(outs[step], 'freq', [(i, (i + step) % groups) for i in range...]
    unnamed x22 -> x30, local copies, waits for them, and re-layouts: 0.24 us -> 2.64 us
  transfers between devices with their start and end apart: 5 -> 5, of which waited for: 0 -> 3; matrix products, arithmetic and copies ran while one was open for 4% -> 4% of each run, Pallas kernels for 0% -> 0%
where the time goes in v2:
time: 52.7 us; the launch traced here: 52 us
  blocking collectives  16.8 us (32%)
  Pallas kernels  14.4 us (27%)
  starting transfers between devices  12.3 us (23%)
  local copies, waits for them, and re-layouts  4.45 us (8%)
  waiting for transfers between devices  2.9 us (6%)
  between operations  0.87 us (2%)
    all_to_all x1, blocking collectives, per_device(): lax.all_to_all(dots.reshape(slabs, 2, LANES), 'elem', 0, 0)  16.8 us
    pallas_call x1, Pallas kernels, per_device(): pl.pallas_call(main_kernel, out_shape=[jax.ShapeDtypeStruct((3 * parts *...  7.14 us
    ppermute x3, starting transfers between devices, per_device(): lax.ppermute(outs[step], 'freq', [(i, (i + step) % groups) for i in range...  5.67 us
    ppermute x1, starting transfers between devices, per_device(): lax.ppermute(edges, 'elem', [(i + 1, i) for i in range(slabs - 1)])  3.45 us
    pallas_call x1, Pallas kernels, per_device(): pl.pallas_call(edges_kernel, out_shape=jax.ShapeDtypeStruct((edge_rows, L...  3.23 us
    ppermute x1, starting transfers between devices, per_device(): lax.ppermute(edges, 'elem', [(i, i + 1) for i in range(slabs - 1)])  3.18 us
    ppermute x3, waiting for transfers between devices, per_device(): lax.ppermute(outs[step], 'freq', [(i, (i + step) % groups) for i in range...  2.89 us
    unnamed x30, local copies, waits for them, and re-layouts  2.64 us
  transfers between devices with their start and end apart: 5, of which 3 were waited for; matrix products, arithmetic and copies ran while one was open for 4% of the time, Pallas kernels for 0%

profile of v2, /device:TPU:1, one launch (start us, length us, event | category | flops | bytes accessed | tf_op | source)
XLA Modules:
  0.0 52.0 jit_solution(14798813041993130022)
XLA Ops:
  0.7 3.2 %edges.1.own_ref = f32[200,128]{1,0:T(8,128)} custom-call(f32[3072,128]{1,0:T(8,128)} %bitcast.20, f32[1,128]{1,0:T(1,128)} %bitcast.23, f32[1,128]{1,0:T(1,128)} %bitcast.27), custom_call_target="tpu_custom_call" | custom-call | tf_op jit(solution)/shard_map/edges/pallas_call | solution.py:397
  3.9 3.4 %collective-permute-start.1 = (f32[200,128]{1,0:T(8,128)}, f32[200,128]{1,0:T(8,128)S(1)}, u32[]{:S(2)}, u32[]{:S(2)}) collective-permute-start(f32[200,128]{1,0:T(8,128)} %edges.1.own_ref), channel_id=1, source_target_pairs={{4,0},{8,4},{12,8},{16,12},{20,16},{24,20},{28,24},{32,28},{36,32}... | collective-permute-start | bytes 307208 | tf_op jit(solution)/shard_map/ppermute | solution.py:405
  7.4 3.2 %collective-permute-start = (f32[200,128]{1,0:T(8,128)}, f32[200,128]{1,0:T(8,128)S(1)}, u32[]{:S(2)}, u32[]{:S(2)}) collective-permute-start(f32[200,128]{1,0:T(8,128)} %edges.1.own_ref), channel_id=1, source_target_pairs={{0,4},{4,8},{8,12},{12,16},{16,20},{20,24},{24,28},{28,32},{32,36}... | collective-permute-start | bytes 307208 | tf_op jit(solution)/shard_map/ppermute | solution.py:404
  10.6 0.1 copy.26
  10.7 0.1 copy.25
  10.9 0.1 concatenate.10
  11.0 0.1 copy.28
  11.1 1.2 %gather_fusion = f32[96]{0:T(128)S(1)} fusion(f32[96,96]{1,0:T(8,128)S(1)} %copy-done.11, s32[96]{0:T(128)S(1)} %or_bitcast_fusion), kind=kCustom, calls=%fused_computation | custom fusion | bytes 1536 | tf_op jit(solution)/shard_map/jit(diagonal)/cond/branch_0_fun/gather | solution.py:407
  12.5 0.1 copy.31.cols_ref
  12.6 0.1 copy.29
  12.8 0.1 pad_maximum_fusion.lhs_ref
  13.0 7.1 %krylov.1 = (f32[1536,128]{1,0:T(8,128)S(1)}, f32[64,128]{1,0:T(8,128)S(1)}) custom-call(s32[2]{0:T(128)S(1)} %pad_add_fusion.info_ref, f32[3072,128]{1,0:T(8,128)S(1)} %bitcast.21, f32[200,128]{1,0:T(8,128)S(1)} %copy-done.2, f32[200,128]{1,0:T(8,128)S(1)} %collective-permute-done.left_ref, f32[200,128]{1,0:T(8,128)S(1)} %collective-permute-done.1.right_ref, ...), custom_call_target="tpu_custom_call" | custom-call | tf_op jit(solution)/shard_map/krylov/pallas_call | solution.py:418
  20.2 0.9 %copy-done.1 = f32[1536,128]{1,0:T(8,128)} copy-done((f32[1536,128]{1,0:T(8,128)}, f32[1536,128]{1,0:T(8,128)S(1)}, u32[]{:S(2)}) %copy-start.1) | copy-done | bytes 786456
  21.1 16.8 %all_to_all.5 = f32[32,2,128]{2,1,0:T(2,128)} all-to-all(f32[32,2,128]{2,1,0:T(2,128)S(1)} %bitcast.22), channel_id=1, replica_groups=mesh['elem'=32,'freq'=4] {'elem'}, dimensions={0} | all-to-all | bytes 65536 | tf_op jit(solution)/shard_map/all_to_all | solution.py:435
  37.9 2.4 %combine.1 = (f32[128,128]{1,0:T(8,128)}, f32[128,128]{1,0:T(8,128)}, f32[128,128]{1,0:T(8,128)}, f32[128,128]{1,0:T(8,128)}) custom-call(s32[2]{0:T(128)} %copy-done.6, f32[64,128]{1,0:T(8,128)} %bitcast.26, f32[1536,128]{1,0:T(8,128)} %copy-done.1), custom_call_target="tpu_custom_call" | custom-call | tf_op jit(solution)/shard_map/combine/pallas_call | solution.py:436
  40.2 1.6 %collective-permute-start.2 = (f32[128,128]{1,0:T(8,128)}, f32[128,128]{1,0:T(8,128)S(1)}, u32[]{:S(2)}, u32[]{:S(2)}) collective-permute-start(f32[128,128]{1,0:T(8,128)} %get-tuple-element.13), channel_id=1, source_target_pairs={{0,1},{1,2},{2,3},{3,0},{4,5},{5,6},{6,7},{7,4},{8,9},{9,10},{10,1... | collective-permute-start | bytes 196616 | tf_op jit(solution)/shard_map/ppermute | solution.py:444
  41.9 3.3 %collective-permute-start.3 = (f32[128,128]{1,0:T(8,128)}, f32[128,128]{1,0:T(8,128)S(1)}, u32[]{:S(2)}, u32[]{:S(2)}) collective-permute-start(f32[128,128]{1,0:T(8,128)} %get-tuple-element.14), channel_id=1, source_target_pairs={{0,2},{1,3},{2,0},{3,1},{4,6},{5,7},{6,4},{7,5},{8,10},{9,11},{10,... | collective-permute-start | bytes 196616 | tf_op jit(solution)/shard_map/ppermute | solution.py:444
  45.2 0.7 %collective-permute-start.4 = (f32[128,128]{1,0:T(8,128)}, f32[128,128]{1,0:T(8,128)S(1)}, u32[]{:S(2)}, u32[]{:S(2)}) collective-permute-start(f32[128,128]{1,0:T(8,128)} %get-tuple-element.15), channel_id=1, source_target_pairs={{0,3},{1,0},{2,1},{3,2},{4,7},{5,4},{6,5},{7,6},{8,11},{9,8},{10,9... | collective-permute-start | bytes 196616 | tf_op jit(solution)/shard_map/ppermute | solution.py:444
  45.9 0.4 collective-permute-done.2.part1_ref
  46.3 2.0 %collective-permute-done.3.part2_ref = f32[128,128]{1,0:T(8,128)S(1)} collective-permute-done((f32[128,128]{1,0:T(8,128)}, f32[128,128]{1,0:T(8,128)S(1)}, u32[]{:S(2)}, u32[]{:S(2)}) %collective-permute-start.3) | collective-permute-done | bytes 65568 | tf_op jit(solution)/shard_map/ppermute | solution.py:444
  48.3 0.5 collective-permute-done.4.part3_ref
  48.8 0.8 %copy-done.5 = f32[128,128]{1,0:T(8,128)S(1)} copy-done((f32[128,128]{1,0:T(8,128)S(1)}, f32[128,128]{1,0:T(8,128)}, u32[]{:S(2)}) %copy-start.5) | copy-done | bytes 65560
  49.7 0.7 %copy-done.7 = s32[2]{0:T(128)S(1)} copy-done((s32[2]{0:T(128)S(1)}, s32[2]{0:T(128)}, u32[]{:S(2)}) %copy-start.7) | copy-done | bytes 32
  50.3 1.7 %response.1 = (f32[1,32]{1,0:T(1,128)}, f32[1,32]{1,0:T(1,128)}) custom-call(s32[2]{0:T(128)S(1)} %copy-done.7, f32[4,16]{1,0:T(4,128)S(1)} %copy-done.8, f32[128,128]{1,0:T(8,128)S(1)} %copy-done.5, f32[128,128]{1,0:T(8,128)S(1)} %collective-permute-done.2.part1_ref, f32[128,128]{1,0:T(8,128)S(1)} %collective-permute-done.3.part2_ref, ...), custom_call_target="tpu_custom_call" | custom-call | tf_op jit(solution)/shard_map/response/pallas_call | solution.py:449
  (36 shorter events, 0.4 us)
Async XLA Ops:
  0.6 9.9 %copy-start.12 = (f32[6,96]{1,0:T(8,128)S(1)}, f32[6,96]{1,0:T(8,128)}, u32[]{:S(2)}) copy-start(f32[6,96]{1,0:T(8,128)} %param.15) | copy-start | bytes 6916
  0.6 10.1 %copy-start.11 = (f32[96,96]{1,0:T(8,128)S(1)}, f32[96,96]{1,0:T(8,128)}, u32[]{:S(2)}) copy-start(f32[96,96]{1,0:T(8,128)} %param.11) | copy-start | bytes 110596
  0.7 11.7 %copy-start.13 = (f32[96]{0:T(128)S(1)}, f32[96]{0:T(128)}, u32[]{:S(2)}) copy-start(f32[96]{0:T(128)} %param.12) | copy-start | bytes 1156
  0.7 12.3 %copy-start = (f32[48,32,2,128]{3,2,1,0:T(2,128)S(1)}, f32[48,32,2,128]{3,2,1,0:T(2,128)}, u32[]{:S(2)}) copy-start(f32[48,32,2,128]{3,2,1,0:T(2,128)} %param.10) | copy-start | bytes 4718596
  3.9 9.1 %copy-start.2 = (f32[200,128]{1,0:T(8,128)S(1)}, f32[200,128]{1,0:T(8,128)}, u32[]{:S(2)}) copy-start(f32[200,128]{1,0:T(8,128)} %edges.1.own_ref) | copy-start | bytes 307204
  3.9 9.1 %collective-permute-start.1 = (f32[200,128]{1,0:T(8,128)}, f32[200,128]{1,0:T(8,128)S(1)}, u32[]{:S(2)}, u32[]{:S(2)}) collective-permute-start(f32[200,128]{1,0:T(8,128)} %edges.1.own_ref), channel_id=1, source_target_pairs={{4,0},{8,4},{12,8},{16,12},{20,16},{24,20},{28,24},{32,28},{36,32}... | collective-permute-start | bytes 307208 | tf_op jit(solution)/shard_map/ppermute | solution.py:405
  7.4 5.6 %collective-permute-start = (f32[200,128]{1,0:T(8,128)}, f32[200,128]{1,0:T(8,128)S(1)}, u32[]{:S(2)}, u32[]{:S(2)}) collective-permute-start(f32[200,128]{1,0:T(8,128)} %edges.1.own_ref), channel_id=1, source_target_pairs={{0,4},{4,8},{8,12},{12,16},{16,20},{20,24},{24,28},{28,32},{32,36}... | collective-permute-start | bytes 307208 | tf_op jit(solution)/shard_map/ppermute | solution.py:404
  12.7 36.1 %copy-start.3 = (bf16[512,256]{1,0:T(8,128)(2,1)S(1)}, bf16[512,256]{1,0:T(8,128)(2,1)}, u32[]{:S(2)}) copy-start(bf16[512,256]{1,0:T(8,128)(2,1)} %constant.26.clone.table_low_ref) | copy-start | bytes 786436
  12.7 36.1 %copy-start.4 = (bf16[512,256]{1,0:T(8,128)(2,1)S(1)}, bf16[512,256]{1,0:T(8,128)(2,1)}, u32[]{:S(2)}) copy-start(bf16[512,256]{1,0:T(8,128)(2,1)} %constant.25.clone.table_high_ref) | copy-start | bytes 786436
  12.7 36.0 %copy-start.8 = (f32[4,16]{1,0:T(4,128)S(1)}, f32[4,16]{1,0:T(4,128)}, u32[]{:S(2)}) copy-start(f32[4,16]{1,0:T(4,128)} %curves_ref.1) | copy-start | bytes 772
  12.8 36.0 %copy-start.9 = (f32[128]{0:T(128)S(1)}, f32[128]{0:T(128)}, u32[]{:S(2)}) copy-start(f32[128]{0:T(128)} %param.13) | copy-start | bytes 1540
  12.8 36.0 %copy-start.10 = (s32[32]{0:T(128)S(1)}, s32[32]{0:T(128)}, u32[]{:S(2)}) copy-start(s32[32]{0:T(128)} %param.17) | copy-start | bytes 388
  13.0 24.9 %copy-start.6 = (s32[2]{0:T(128)}, s32[2]{0:T(128)S(1)}, u32[]{:S(2)}) copy-start(s32[2]{0:T(128)S(1)} %pad_add_fusion.info_ref) | copy-start | bytes 28
  20.2 0.9 %copy-start.1 = (f32[1536,128]{1,0:T(8,128)}, f32[1536,128]{1,0:T(8,128)S(1)}, u32[]{:S(2)}) copy-start(f32[1536,128]{1,0:T(8,128)S(1)} %get-tuple-element.11.strain_ref) | copy-start | bytes 2359300
  40.2 6.1 %collective-permute-start.2 = (f32[128,128]{1,0:T(8,128)}, f32[128,128]{1,0:T(8,128)S(1)}, u32[]{:S(2)}, u32[]{:S(2)}) collective-permute-start(f32[128,128]{1,0:T(8,128)} %get-tuple-element.13), channel_id=1, source_target_pairs={{0,1},{1,2},{2,3},{3,0},{4,5},{5,6},{6,7},{7,4},{8,9},{9,10},{10,1... | collective-permute-start | bytes 196616 | tf_op jit(solution)/shard_map/ppermute | solution.py:444
  41.9 6.4 %collective-permute-start.3 = (f32[128,128]{1,0:T(8,128)}, f32[128,128]{1,0:T(8,128)S(1)}, u32[]{:S(2)}, u32[]{:S(2)}) collective-permute-start(f32[128,128]{1,0:T(8,128)} %get-tuple-element.14), channel_id=1, source_target_pairs={{0,2},{1,3},{2,0},{3,1},{4,6},{5,7},{6,4},{7,5},{8,10},{9,11},{10,... | collective-permute-start | bytes 196616 | tf_op jit(solution)/shard_map/ppermute | solution.py:444
  45.2 3.6 %collective-permute-start.4 = (f32[128,128]{1,0:T(8,128)}, f32[128,128]{1,0:T(8,128)S(1)}, u32[]{:S(2)}, u32[]{:S(2)}) collective-permute-start(f32[128,128]{1,0:T(8,128)} %get-tuple-element.15), channel_id=1, source_target_pairs={{0,3},{1,0},{2,1},{3,2},{4,7},{5,4},{6,5},{7,6},{8,11},{9,8},{10,9... | collective-permute-start | bytes 196616 | tf_op jit(solution)/shard_map/ppermute | solution.py:444
  48.8 0.8 %copy-start.5 = (f32[128,128]{1,0:T(8,128)S(1)}, f32[128,128]{1,0:T(8,128)}, u32[]{:S(2)}) copy-start(f32[128,128]{1,0:T(8,128)} %get-tuple-element.12.part0_ref) | copy-start | bytes 196612
  49.7 0.7 %copy-start.7 = (s32[2]{0:T(128)S(1)}, s32[2]{0:T(128)}, u32[]{:S(2)}) copy-start(s32[2]{0:T(128)} %copy-done.6) | copy-start | bytes 28

commit v3 on v2

--- a/solution.py
+++ b/solution.py
@@ -14,13 +14,16 @@
 EPSILON = 1e-06
 LANES = 128
 SLOT = 8
-PER_PATCH = LANES // SLOT
+DEPTH = 176
 UNROLL = 32
 DOTS = 6
 F32 = jnp.float32
 BF16 = jnp.bfloat16
 VMEM = pl.BlockSpec(memory_space=pltpu.VMEM)
 SMEM = pl.BlockSpec(memory_space=pltpu.SMEM)
+HBM = pl.BlockSpec(memory_space=pltpu.HBM)
+PAIR_ROWS, ROW_AT = 96, 96
+UP_ROWS, DOWN_ROWS = 104, 152
 
 
 def lane_ids(rows=1):
@@ -40,46 +43,97 @@
     return high, (x - high.astype(F32)).astype(BF16)
 
 
-def edges_kernel(load_ref, modulus_ref, mass_ref, out_ref):
-    half = load_ref.shape[0] // 64
-    parts = 64
-    slot = lane_ids(half) // SLOT
-    for group in range(parts // PER_PATCH):
-
-        def place(i, held):
-            field = load_ref[pl.ds(group * PER_PATCH + i, half, stride=parts), :]
-            moved = pltpu.roll(field, 2 + SLOT * i, 1)
-            return jnp.where(slot == i, moved, held)
-
-        held = lax.fori_loop(0, PER_PATCH, place, jnp.zeros((half, LANES), F32), unroll=16)
-        out_ref[group * half : (group + 1) * half, :] = held
-    base = parts // PER_PATCH * half
-    out_ref[base : base + 1, :] = modulus_ref[...]
-    out_ref[base + 1 : base + 2, :] = mass_ref[...]
-    out_ref[base + 2 : base + 8, :] = jnp.zeros((6, LANES), F32)
-
-
-def pattern(row):
-    row = jnp.where(lane_ids() < SLOT, row, 0.0)
-    for step in (8, 16, 32, 64):
-        row = row + pltpu.roll(row, step, 1)
-    return row
+def edges_kernel(
+    load_ref, modulus_ref, mass_ref, stiffness_ref, template_ref, strain_map_ref,
+    up_ref, down_ref, lhs_ref, cols_ref,
+    buffer_ref, slots_ref, turned_ref, square_ref, copied,
+):
+    half, parts, chunks = 48, 64, 3
+    per = half // chunks
+    length = per * parts
+    copies = [
+        pltpu.make_async_copy(
+            load_ref.at[pl.ds(i * length, length)], buffer_ref.at[pl.ds(i * length, length)],
+            copied.at[i],
+        )
+        for i in range(chunks)
+    ]
+    for copy in copies:
+        copy.start()
+
+    full = 2 * half
+    square_ref[...] = jnp.zeros(square_ref.shape, F32)
+    square_ref[:full, :full] = stiffness_ref[...]
+    comps = strain_map_ref.shape[0]
+    square_ref[full : full + comps, :full] = strain_map_ref[...]
+    square_ref[full + 8 : full + 9, :full] = template_ref[...]
+    stiff = square_ref[:full, :]
+    same = lax.broadcasted_iota(jnp.int32, (full, LANES), 0) == lane_ids(full)
+    kdiag = jnp.sum(jnp.where(same, stiff, 0.0), axis=1, keepdims=True)
+    template = jnp.sum(
+        jnp.where(same, square_ref[full + 8 : full + 9, :], 0.0), axis=1, keepdims=True
+    )
+    lane = lane_ids(half)
+    columns = jnp.zeros((half, LANES), F32)
+    for i, col in enumerate((kdiag[:half], kdiag[half:], template[:half], template[half:])):
+        columns = jnp.where(lane == i, col, columns)
+    cols_ref[...] = columns
+    off = jnp.where(same, 0.0, stiff)
+    strain_rows = square_ref[full : full + 8, :]
+    moved = pltpu.roll(off, LANES - half, 1)
+    moved_rows = pltpu.roll(strain_rows, LANES - half, 1)
+    stacked = jnp.concatenate(
+        [off[:half], moved[half:], moved[:half], off[half:], strain_rows, moved_rows], 0
+    )
+    rows = stacked.shape[0]
+    lane = lane_ids(rows)
+    stacked = jnp.where(lane < half, stacked, 0.0)
+    high, low = halves(stacked)
+    high = high.astype(F32)
+    lhs_ref[:, :LANES] = (high + pltpu.roll(high, half, 1)).astype(BF16)
+    lhs_ref[:, LANES:] = low
+
+    slot = lane_ids(parts) // SLOT
+    for chunk in range(chunks):
+        copies[chunk].wait()
+        held = jnp.zeros((parts, LANES), F32)
+        for i in range(per):
+            start = (chunk * per + i) * parts
+            moved = pltpu.roll(buffer_ref[start : start + parts, :], 2 + SLOT * i, 1)
+            held = jnp.where(slot == i, moved, held)
+        at = chunk * per
+        for turn, shift in enumerate((LANES - 1, LANES - 3)):
+            slots_ref[pl.ds(0, parts, stride=2), :] = held
+            slots_ref[pl.ds(1, parts, stride=2), :] = pltpu.roll(held, shift, 1)
+            turned_ref[...] = jnp.transpose(slots_ref[...])
+            if turn == 0:
+                pair = turned_ref[pl.ds(1, per, stride=SLOT), :]
+                up_ref[at : at + per, :] = pair
+                down_ref[at : at + per, :] = pair
+            else:
+                pair = turned_ref[pl.ds(0, per, stride=SLOT), :]
+                up_ref[half + at : half + at + per, :] = pair
+                down_ref[half + at : half + at + per, :] = pair
+                down_ref[UP_ROWS + at : UP_ROWS + at + per, :] = turned_ref[
+                    pl.ds(1, per, stride=SLOT), :
+                ]
+    for ref in (up_ref, down_ref):
+        ref[ROW_AT : ROW_AT + 1, :] = modulus_ref[...]
+        ref[ROW_AT + 1 : ROW_AT + 2, :] = mass_ref[...]
+        ref[ROW_AT + 2 : UP_ROWS, :] = jnp.zeros((UP_ROWS - ROW_AT - 2, LANES), F32)
 
 
 def main_kernel(
-    info_ref, load_ref, own_ref, left_ref, right_ref, lhs_ref, cols_ref,
-    strain_ref, dots_out_ref, field_ref, inv_ref, border_ref, dots_ref,
+    load_ref, own_ref, left_ref, right_ref, lhs_ref, cols_ref, strain_out_ref, dots_out_ref,
+    strain_ref, field_ref, inv_ref, border_ref, dots_ref, copied,
 ):
-    half = lhs_ref.shape[1] // 3
-    parts = 64
+    half, parts = 48, 64
     freqs = parts // 2
-    groups = parts // PER_PATCH
-    base = groups * half
-    freq_group = info_ref[0]
-    is_last = info_ref[1]
+    freq_group = lax.axis_index("freq")
+    is_last = lax.axis_index("elem") == lax.axis_size("elem") - 1
     first_order = (freq_group * freqs + 1).astype(F32)
     lanes = lane_ids()
-    place = lanes % SLOT
+    even = lanes % 2 == 0
 
     def shift_of(order):
         return MASS_COEF * (order * (1.0 / (4 * freqs))) ** 2
@@ -88,81 +142,99 @@
     kd_top, kd_low, mt_top, mt_low = (cols[:, i : i + 1] for i in range(4))
 
     def rows_of(at):
-        own, left, right = (r[base + at : base + at + 1, :] for r in (own_ref, left_ref, right_ref))
+        own, left, right = (
+            r[ROW_AT + at : ROW_AT + at + 1, :] for r in (own_ref, left_ref, right_ref)
+        )
         prev = jnp.where(lanes == 0, earlier(left), earlier(own))
-        right_prev = jnp.where(lanes == 0, earlier(own), earlier(right))
-        own2, prev2 = pltpu.roll(own, 2, 1), pltpu.roll(prev, 2, 1)
-        near = lanes < 2
-        lower = pattern(jnp.where(near, pltpu.roll(left, 2, 1), own2))
-        lower_prev = pattern(jnp.where(near, pltpu.roll(left, 3, 1), prev2))
-        upper = pattern(jnp.where(near, own2, pltpu.roll(right, 2, 1)))
-        upper_prev = pattern(jnp.where(near, prev2, pltpu.roll(right_prev, 2, 1)))
-        return (own, prev), (lower, lower_prev), (upper, upper_prev)
-
-    mod_main, mod_lower, mod_upper = rows_of(0)
-    mass_main, mass_lower, mass_upper = rows_of(1)
+
+        def sides(*upper_lower):
+            (upper, i), (lower, j) = upper_lower
+            upper, lower = upper[:, i : i + 1], lower[:, j : j + 1]
+            return jnp.where(even, upper, lower)
+
+        zero = jnp.zeros_like(own)
+        pairs = [
+            (sides((own, 126), (own, 1)), sides((own, 125), (own, 0))),
+            (sides((own, 127), (own, 0)), sides((own, 126), (left, 127))),
+            (sides((right, 0), (left, 127)), sides((own, 127), (left, 126))),
+            (sides((right, 1), (left, 126)), sides((right, 0), (left, 125))),
+            (sides((right, 2), (zero, 0)), sides((right, 1), (zero, 0))),
+        ]
+        return (own, prev), pairs
+
+    mod_main, mod_pairs = rows_of(0)
+    mass_main, mass_pairs = rows_of(1)
 
     def diagonals(mod, mass):
         return kd_top * mod[0] + kd_low * mod[1], mt_top * mass[0] + mt_low * mass[1]
 
-    lhs = lhs_ref[...]
-
-    def products(left, right):
-        left_high, left_low = halves(left)
-        right_high, right_low = halves(right)
-        high = jnp.concatenate([left_high, right_high], 1)
-        low = jnp.concatenate([left_low, right_low], 1)
-        result = jnp.dot(lhs, jnp.concatenate([high, low, high], 0), preferred_element_type=F32)
+    lhs = lhs_ref[:, :DEPTH]
+    blank = jnp.zeros((DEPTH - 3 * half, 2 * LANES), BF16)
+
+    def products(*fields):
+        split = [halves(field) for field in fields]
+        high = jnp.concatenate([h for h, _ in split], 1)
+        low = jnp.concatenate([l for _, l in split], 1)
+        gap = blank[:, : high.shape[1]]
+        result = jnp.dot(
+            lhs, jnp.concatenate([high, low, gap, high], 0), preferred_element_type=F32
+        )
         cut = [half * i for i in range(5)] + [4 * half + 8, 4 * half + 16]
         return [
             [result[cut[i] : cut[i + 1], LANES * k : LANES * (k + 1)] for i in range(6)]
-            for k in range(2)
+            for k in range(len(fields))
         ]
 
-    stiff_lower, mass_diag_lower = diagonals(mod_lower, mass_lower)
-    stiff_upper, mass_diag_upper = diagonals(mod_upper, mass_upper)
-    fixed = jnp.logical_and(is_last == 1, place >= 2)
-    for group in range(groups):
-        order = first_order + (group * (PER_PATCH // 2) + lanes // (2 * SLOT)).astype(F32)
-        shift = shift_of(order)
-        diag_lower = stiff_lower + shift * mass_diag_lower
-        diag_upper = stiff_upper + shift * mass_diag_upper
-        inv_lower = jnp.where(diag_lower > 0, 1.0 / diag_lower, 0.0)
-        inv_upper = jnp.where(
-            jnp.logical_and(diag_upper > 0, jnp.logical_not(fixed)), 1.0 / diag_upper, 0.0
-        )
-        rows = slice(group * half, (group + 1) * half)
-        own, left, right = own_ref[rows, :], left_ref[rows, :], right_ref[rows, :]
-        lower = jnp.where(place < 2, left, own) * inv_lower
-        upper = jnp.where(place < 2, own, right) * inv_upper
-        for stage in range(3):
-            lower_p, upper_p = products(lower, upper)
-            l11, l22, l12, l21, _, _ = lower_p
-            u11, u22, u12, u21, _, u_strain = upper_p
-            from_above = later(mod_upper[1] * u12)
-            at = stage * groups + group
-            if stage < 2:
-                from_below = earlier(mod_lower[0] * l21)
-                border = jnp.where(
-                    place == 1, from_above, jnp.where(place == 2, from_below, 0.0)
-                )
-                lower = -inv_lower * (
-                    mod_lower[0] * l11 + mod_lower[1] * l22 + later(mod_lower[1] * l12) + from_below
-                )
-                tail = u_strain
-                upper_next = -inv_upper * (
-                    mod_upper[0] * u11 + mod_upper[1] * u22 + from_above
-                    + earlier(mod_upper[0] * u21)
-                )
-            else:
-                border = jnp.where(place == 1, from_above, 0.0)
-                energy = jnp.sum(mod_upper[1] * upper * u22, axis=0, keepdims=True)
-                row = lax.broadcasted_iota(jnp.int32, (8, LANES), 0)
-                tail = jnp.where(row == 6, energy, u_strain)
-                upper_next = None
-            border_ref[at, :half, :] = border
-            border_ref[at, half:, :] = jnp.where(place == 1, later(tail), 0.0)
-            upper = upper_next
+    order = first_order + (lanes // 4).astype(F32)
+    beyond = jnp.logical_and(even, is_last)
+    inverses = []
+    for i, (mod, mass) in enumerate(zip(mod_pairs, mass_pairs)):
+        stiff, weight = diagonals(mod, mass)
+        diag = stiff + shift_of(order) * weight
+        good = diag > 0
+        if i >= 2:
+            good = jnp.logical_and(good, jnp.logical_not(beyond))
+        inverses.append(jnp.where(good, 1.0 / diag, 0.0))
+
+    def met(at):
+        inward = later(right_ref[at : at + half, :])
+        return jnp.where(even, inward, earlier(left_ref[at : at + half, :]))
+
+    rims = [
+        own_ref[half : 2 * half, :],
+        own_ref[:half, :],
+        met(0),
+        met(half),
+        jnp.where(even, later(right_ref[UP_ROWS:, :]), 0.0),
+    ]
+    rims = [field * inv for field, inv in zip(rims, inverses)]
+
+    def rim_stage(stage, rims):
+        first = stage
+        z = {}
+        for i in range(first, len(rims), 2):
+            names = list(range(i, min(i + 2, len(rims))))
+            for name, value in zip(names, products(*(rims[name] for name in names))):
+                z[name] = value
+        at_edge = mod_pairs[1]
+        outer = z[2]
+        if stage < 2:
+            border = jnp.where(even, at_edge[0] * outer[2], at_edge[1] * outer[3])
+            tail = outer[5]
+        else:
+            border = jnp.where(even, at_edge[0] * outer[2], 0.0)
+            energy = jnp.sum(at_edge[0] * rims[2] * outer[1], axis=0, keepdims=True)
+            row = lax.broadcasted_iota(jnp.int32, (8, LANES), 0)
+            tail = jnp.where(row == 6, energy, outer[5])
+        border_ref[stage, :half, :] = border
+        border_ref[stage, half:, :] = jnp.where(even, tail, 0.0)
+        nexts = [None] * len(rims)
+        for i in range(first + 1, len(rims) - 1):
+            above = jnp.where(even, z[i + 1][2], z[i - 1][2])
+            below = jnp.where(even, z[i - 1][3], z[i + 1][3])
+            top, low = mod_pairs[i]
+            nexts[i] = -inverses[i] * (top * (z[i][0] + above) + low * (z[i][1] + below))
+        return nexts[: len(rims) - 1]
 
     stiff_main, mass_diag_main = diagonals(mod_main, mass_main)
     mod_own, mod_prev = mod_main
@@ -171,10 +243,7 @@
     rim = jnp.logical_or(lanes == 0, lanes == 127)
 
     def borders(stage, f, k):
-        part = 2 * f + k
-        group = part // PER_PATCH
-        i = part % PER_PATCH
-        moved = pltpu.roll(border_ref[stage * groups + group], (126 + LANES - SLOT * i) % LANES, 1)
+        moved = pltpu.roll(border_ref[stage], LANES - 1 - 2 * (2 * f + k), 1)
         moved = jnp.where(rim, moved, 0.0)
         return moved[:half], moved[half:]
 
@@ -241,9 +310,17 @@
         dots_ref[pl.ds(5 * freqs + f, 1), :] = -(jnp.sum(total, axis=0, keepdims=True) + extra)
         return carry
 
-    lax.fori_loop(0, freqs, first, 0, unroll=UNROLL)
-    lax.fori_loop(0, freqs, second, 0, unroll=UNROLL)
-    lax.fori_loop(0, freqs, third, 0, unroll=UNROLL)
+    rows = 2 * freqs * 8
+    copies = []
+    for stage, step in enumerate((first, second, third)):
+        rims = rim_stage(stage, rims)
+        lax.fori_loop(0, freqs, step, 0, unroll=UNROLL)
+        block = pl.ds(stage * rows, rows)
+        copy = pltpu.make_async_copy(
+            strain_ref.at[block], strain_out_ref.at[block], copied.at[stage]
+        )
+        copy.start()
+        copies.append(copy)
 
     dots_ref[DOTS * freqs :, :] = jnp.zeros((256 - DOTS * freqs, LANES), F32)
     sums = lax.dot_general(
@@ -254,6 +331,8 @@
     pair = jnp.where(row % 2 == 0, sums[:, :LANES], sums[:, LANES:])
     for i in range(dots_out_ref.shape[0] // 8):
         dots_out_ref[8 * i : 8 * i + 8, :] = pair
+    for copy in copies:
+        copy.wait()
 
 
 def coefficients(h):
@@ -297,8 +376,12 @@
     return result
 
 
-def combine_kernel(info_ref, dots_ref, strain_ref, out0_ref, out1_ref, out2_ref, out3_ref):
-    freq_group = info_ref[0]
+def combine_kernel(
+    dots_ref, strain_in_ref, out0_ref, out1_ref, out2_ref, out3_ref, strain_ref, copied
+):
+    copy = pltpu.make_async_copy(strain_in_ref, strain_ref, copied)
+    copy.start()
+    freq_group = lax.axis_index("freq")
     freqs, comps = 32, 6
     total = jnp.zeros((8, LANES), F32)
     for i in range(dots_ref.shape[0] // 8):
@@ -314,6 +397,7 @@
     quarter = LANES // 4
     cell = lane_ids(freqs) // quarter
     outs = (out0_ref, out1_ref, out2_ref, out3_ref)
+    copy.wait()
     for k in range(2):
         spectra = [
             sum(
@@ -334,11 +418,11 @@
 
 
 def final_kernel(
-    info_ref, curves_ref, part0_ref, part1_ref, part2_ref, part3_ref,
+    curves_ref, part0_ref, part1_ref, part2_ref, part3_ref,
     table_high_ref, table_low_ref, modulus_ref, soil_ref,
     modulus_out_ref, strain_out_ref, spectra_ref,
 ):
-    freq_group = info_ref[0]
+    freq_group = lax.axis_index("freq")
     parts, freqs = 64, 32
     for step, part_ref in enumerate((part0_ref, part1_ref, part2_ref, part3_ref)):
         start = pl.multiple_of((freq_group + 4 - step) % 4 * parts, parts)
@@ -388,58 +472,60 @@
     parts = 2 * freq_dev
     groups = lax.axis_size("freq")
     slabs = lax.axis_size("elem")
-    freq_group = lax.axis_index("freq")
-    is_last = (lax.axis_index("elem") == slabs - 1).astype(jnp.int32)
-    info = jnp.stack([freq_group.astype(jnp.int32), is_last])
     rows = load.reshape(half * parts, nodes)
     modulus_row, mass_row = modulus.reshape(1, nodes), element_mass.reshape(1, nodes)
-    edge_rows = parts // PER_PATCH * half + 8
-    edges = pl.pallas_call(
+    edge_up, edge_down, lhs, cols = pl.pallas_call(
         edges_kernel,
-        out_shape=jax.ShapeDtypeStruct((edge_rows, LANES), F32),
-        in_specs=[VMEM] * 3,
-        out_specs=VMEM,
+        out_shape=[
+            jax.ShapeDtypeStruct((UP_ROWS, LANES), F32),
+            jax.ShapeDtypeStruct((DOWN_ROWS, LANES), F32),
+            jax.ShapeDtypeStruct((4 * half + 16, 2 * LANES), BF16),
+            jax.ShapeDtypeStruct((half, LANES), F32),
+        ],
+        in_specs=[HBM] + [VMEM] * 5,
+        out_specs=[VMEM] * 4,
+        scratch_shapes=[
+            pltpu.VMEM((half * parts, LANES), F32),
+            pltpu.VMEM((LANES, LANES), F32),
+            pltpu.VMEM((LANES, LANES), F32),
+            pltpu.VMEM((LANES, LANES), F32),
+            pltpu.SemaphoreType.DMA((3,)),
+        ],
         name="edges",
-    )(rows, modulus_row, mass_row)
-    from_left = lax.ppermute(edges, "elem", [(i, i + 1) for i in range(slabs - 1)])
-    from_right = lax.ppermute(edges, "elem", [(i + 1, i) for i in range(slabs - 1)])
-
-    kdiag = jnp.diagonal(stiffness)
-    off = stiffness * (1.0 - jnp.eye(2 * half, dtype=F32))
-    comps = strain_map.shape[0]
-    strain_rows = jnp.pad(strain_map, ((0, 8 - comps), (0, 0)))
-    stacked = jnp.concatenate(
-        [off[:half, :half], off[half:, half:], off[:half, half:], off[half:, :half],
-         strain_rows[:, :half], strain_rows[:, half:]], 0
-    )
-    high, low = halves(stacked)
-    lhs = jnp.concatenate([high, high, low], 1)
-    cols = jnp.stack([kdiag[:half], kdiag[half:], mass_template[:half], mass_template[half:]], 1)
+    )(rows, modulus_row, mass_row, stiffness, mass_template.reshape(1, -1), strain_map)
+    from_left = lax.ppermute(edge_up, "elem", [(i, i + 1) for i in range(slabs - 1)])
+    from_right = lax.ppermute(edge_down, "elem", [(i + 1, i) for i in range(slabs - 1)])
     strains, dots = pl.pallas_call(
         main_kernel,
         out_shape=[
             jax.ShapeDtypeStruct((3 * parts * 8, LANES), F32),
             jax.ShapeDtypeStruct((2 * slabs, LANES), F32),
         ],
-        in_specs=[SMEM] + [VMEM] * 6,
-        out_specs=[VMEM] * 2,
+        in_specs=[VMEM] * 6,
+        out_specs=[HBM, VMEM],
         scratch_shapes=[
+            pltpu.VMEM((3 * parts * 8, LANES), F32),
             pltpu.VMEM((parts, half, LANES), F32),
             pltpu.VMEM((freq_dev, half, LANES), F32),
-            pltpu.VMEM((3 * parts // PER_PATCH, half + 8, LANES), F32),
+            pltpu.VMEM((3, half + 8, LANES), F32),
             pltpu.VMEM((256, LANES), F32),
+            pltpu.SemaphoreType.DMA((3,)),
         ],
         compiler_params=pltpu.CompilerParams(vmem_limit_bytes=32 * 1024 * 1024),
         name="krylov",
-    )(info, rows, edges, from_left, from_right, lhs, cols)
+    )(rows, edge_down, from_left, from_right, lhs, cols)
     dots = lax.all_to_all(dots.reshape(slabs, 2, LANES), "elem", 0, 0).reshape(-1, LANES)
     outs = pl.pallas_call(
         combine_kernel,
         out_shape=[jax.ShapeDtypeStruct((2 * parts, LANES), F32)] * groups,
-        in_specs=[SMEM] + [VMEM] * 2,
+        in_specs=[VMEM, HBM],
         out_specs=[VMEM] * groups,
+        scratch_shapes=[
+            pltpu.VMEM((3 * parts * 8, LANES), F32),
+            pltpu.SemaphoreType.DMA,
+        ],
         name="combine",
-    )(info, dots, strains)
+    )(dots, strains)
     received = [outs[0]] + [
         lax.ppermute(outs[step], "freq", [(i, (i + step) % groups) for i in range(groups)])
         for step in range(1, groups)
@@ -449,12 +535,12 @@
     new_modulus, peak_strain = pl.pallas_call(
         final_kernel,
         out_shape=[jax.ShapeDtypeStruct((1, quarter), F32)] * 2,
-        in_specs=[SMEM] * 2 + [VMEM] * 8,
+        in_specs=[SMEM] + [VMEM] * 8,
         out_specs=[VMEM] * 2,
         scratch_shapes=[pltpu.VMEM((groups * parts, 2 * LANES), F32)],
         compiler_params=pltpu.CompilerParams(vmem_limit_bytes=32 * 1024 * 1024),
         name="response",
-    )(info, curves, *received, jnp.asarray(table_high), jnp.asarray(table_low),
+    )(curves, *received, jnp.asarray(table_high), jnp.asarray(table_low),
       modulus_row, soil_type.reshape(1, quarter))
     return new_modulus.reshape(quarter), peak_strain.reshape(quarter)
 

time: 52.7 us -> 54.6 us (1.036)
  waiting for transfers between devices: 2.9 us -> 4.4 us
    unnamed x30 -> x22, local copies, waits for them, and re-layouts: 2.64 us -> 4.26 us
    ppermute x2, waiting for transfers between devices: 0.01 us -> 1.51 us  [the longest x1 1.51 us: per_device(): lax.ppermute(edge_up, 'elem', [(i, i + 1) for i in range(slabs - 1)])]
    gather x1 -> x0, local copies, waits for them, and re-layouts: 1.25 us -> none  [per_device(): kdiag = jnp.diagonal(stiffness)]
    pallas_call x1, Pallas kernels: 7.14 us -> 6.3 us  [per_device(): pl.pallas_call(main_kernel, out_shape=[jax.ShapeDtypeStruct((3 * parts *...]
    pallas_call x1, Pallas kernels: 3.23 us -> 3.9 us  [per_device(): pl.pallas_call(edges_kernel, out_shape=[jax.ShapeDtypeStruct((UP_ROWS, LA...]
  transfers between devices with their start and end apart: 5 -> 5, of which waited for: 3 -> 4; matrix products, arithmetic and copies ran while one was open for 4% -> 0% of each run, Pallas kernels for 0% -> 0%
where the time goes in v3:
time: 54.6 us; the launch traced here: 53.7 us
  blocking collectives  17.2 us (32%)
  Pallas kernels  14.7 us (27%)
  starting transfers between devices  12.4 us (23%)
  waiting for transfers between devices  4.4 us (8%)
  local copies, waits for them, and re-layouts  4.26 us (8%)
  between operations  0.76 us (1%)
    all_to_all x1, blocking collectives, per_device(): lax.all_to_all(dots.reshape(slabs, 2, LANES), 'elem', 0, 0)  17.2 us
    pallas_call x1, Pallas kernels, per_device(): pl.pallas_call(main_kernel, out_shape=[jax.ShapeDtypeStruct((3 * parts *...  6.3 us
    ppermute x3, starting transfers between devices, per_device(): lax.ppermute(outs[step], 'freq', [(i, (i + step) % groups) for i in range...  5.73 us
    unnamed x22, local copies, waits for them, and re-layouts  4.26 us
    pallas_call x1, Pallas kernels, per_device(): pl.pallas_call(edges_kernel, out_shape=[jax.ShapeDtypeStruct((UP_ROWS, LA...  3.9 us
    ppermute x1, starting transfers between devices, per_device(): lax.ppermute(edge_down, 'elem', [(i + 1, i) for i in range(slabs - 1)])  3.46 us
    ppermute x1, starting transfers between devices, per_device(): lax.ppermute(edge_up, 'elem', [(i, i + 1) for i in range(slabs - 1)])  3.18 us
    ppermute x3, waiting for transfers between devices, per_device(): lax.ppermute(outs[step], 'freq', [(i, (i + step) % groups) for i in range...  2.89 us
  transfers between devices with their start and end apart: 5, of which 4 were waited for; matrix products, arithmetic and copies ran while one was open for 0% of the time, Pallas kernels for 0%

profile of v3, /device:TPU:1, one launch (start us, length us, event | category | flops | bytes accessed | tf_op | source)
XLA Modules:
  0.0 53.7 jit_solution(7919285424509887119)
XLA Ops:
  0.7 3.9 %edges.1 = (f32[104,128]{1,0:T(8,128)}, f32[152,128]{1,0:T(8,128)}, bf16[208,256]{1,0:T(8,128)(2,1)}, f32[48,128]{1,0:T(8,128)}) custom-call(f32[3072,128]{1,0:T(8,128)} %bitcast.9, f32[1,128]{1,0:T(1,128)} %bitcast.12, f32[1,128]{1,0:T(1,128)} %bitcast.16, f32[96,96]{1,0:T(8,128)} %stiffness_ref.1, f32[1,96]{1,0:T(1,128)} %bitcast.17, f32[6,96]{1,0:T(8,128)} %strain_map_ref.1), custom_call_target="tpu_custom_call" | custom-call | tf_op jit(solution)/shard_map/edges/pallas_call | solution.py:477
  4.6 0.0 copy-start.2
  4.6 0.0 copy-start.3
  4.6 3.5 %collective-permute-start.1 = (f32[152,128]{1,0:T(8,128)}, f32[152,128]{1,0:T(8,128)S(1)}, u32[]{:S(2)}, u32[]{:S(2)}) collective-permute-start(f32[152,128]{1,0:T(8,128)} %get-tuple-element.14.own_ref), channel_id=1, source_target_pairs={{4,0},{8,4},{12,8},{16,12},{20,16},{24,20},{28,24},{32,28},{36,32}... | collective-permute-start | bytes 233480 | tf_op jit(solution)/shard_map/ppermute | solution.py:497
  8.1 3.2 %collective-permute-start = (f32[104,128]{1,0:T(8,128)}, f32[104,128]{1,0:T(8,128)S(1)}, u32[]{:S(2)}, u32[]{:S(2)}) collective-permute-start(f32[104,128]{1,0:T(8,128)} %get-tuple-element.15), channel_id=1, source_target_pairs={{0,4},{4,8},{8,12},{12,16},{16,20},{20,24},{24,28},{28,32},{32,36}... | collective-permute-start | bytes 159752 | tf_op jit(solution)/shard_map/ppermute | solution.py:496
  11.3 1.5 %collective-permute-done.left_ref = f32[104,128]{1,0:T(8,128)S(1)} collective-permute-done((f32[104,128]{1,0:T(8,128)}, f32[104,128]{1,0:T(8,128)S(1)}, u32[]{:S(2)}, u32[]{:S(2)}) %collective-permute-start) | collective-permute-done | bytes 53280 | tf_op jit(solution)/shard_map/ppermute | solution.py:496
  12.8 0.0 collective-permute-done.1.right_ref
  12.8 0.0 copy-done
  12.8 0.9 %copy-done.4 = bf16[208,256]{1,0:T(8,128)(2,1)S(1)} copy-done((bf16[208,256]{1,0:T(8,128)(2,1)S(1)}, bf16[208,256]{1,0:T(8,128)(2,1)}, u32[]{:S(2)}) %copy-start.4) | copy-done | bytes 106520
  13.7 0.9 %copy-done.5 = f32[152,128]{1,0:T(8,128)S(1)} copy-done((f32[152,128]{1,0:T(8,128)S(1)}, f32[152,128]{1,0:T(8,128)}, u32[]{:S(2)}) %copy-start.5) | copy-done | bytes 77848
  14.6 0.7 %copy-done.7 = f32[48,128]{1,0:T(8,128)S(1)} copy-done((f32[48,128]{1,0:T(8,128)S(1)}, f32[48,128]{1,0:T(8,128)}, u32[]{:S(2)}) %copy-start.7) | copy-done | bytes 24600
  15.3 6.3 %krylov.1 = (f32[1536,128]{1,0:T(8,128)S(1)}, f32[64,128]{1,0:T(8,128)S(1)}) custom-call(f32[3072,128]{1,0:T(8,128)S(1)} %bitcast.10, f32[152,128]{1,0:T(8,128)S(1)} %copy-done.5, f32[104,128]{1,0:T(8,128)S(1)} %collective-permute-done.left_ref, f32[152,128]{1,0:T(8,128)S(1)} %collective-permute-done.1.right_ref, bf16[208,256]{1,0:T(8,128)(2,1)S(1)} %copy-done.4, ...), custom_call_target="tpu_custom_call" | custom-call | tf_op jit(solution)/shard_map/krylov/pallas_call | solution.py:498
  21.6 0.9 %copy-done.1 = f32[1536,128]{1,0:T(8,128)} copy-done((f32[1536,128]{1,0:T(8,128)}, f32[1536,128]{1,0:T(8,128)S(1)}, u32[]{:S(2)}) %copy-start.1) | copy-done | bytes 786456
  22.5 17.2 %all_to_all.5 = f32[32,2,128]{2,1,0:T(2,128)} all-to-all(f32[32,2,128]{2,1,0:T(2,128)S(1)} %bitcast.11), channel_id=1, replica_groups=mesh['elem'=32,'freq'=4] {'elem'}, dimensions={0} | all-to-all | bytes 65536 | tf_op jit(solution)/shard_map/all_to_all | solution.py:517
  39.7 2.8 %combine.1 = (f32[128,128]{1,0:T(8,128)}, f32[128,128]{1,0:T(8,128)}, f32[128,128]{1,0:T(8,128)}, f32[128,128]{1,0:T(8,128)}) custom-call(f32[64,128]{1,0:T(8,128)} %bitcast.15, f32[1536,128]{1,0:T(8,128)} %copy-done.1), custom_call_target="tpu_custom_call" | custom-call | tf_op jit(solution)/shard_map/combine/pallas_call | solution.py:518
  42.6 1.7 %collective-permute-start.2 = (f32[128,128]{1,0:T(8,128)}, f32[128,128]{1,0:T(8,128)S(1)}, u32[]{:S(2)}, u32[]{:S(2)}) collective-permute-start(f32[128,128]{1,0:T(8,128)} %get-tuple-element.21), channel_id=1, source_target_pairs={{0,1},{1,2},{2,3},{3,0},{4,5},{5,6},{6,7},{7,4},{8,9},{9,10},{10,1... | collective-permute-start | bytes 196616 | tf_op jit(solution)/shard_map/ppermute | solution.py:530
  44.3 3.3 %collective-permute-start.3 = (f32[128,128]{1,0:T(8,128)}, f32[128,128]{1,0:T(8,128)S(1)}, u32[]{:S(2)}, u32[]{:S(2)}) collective-permute-start(f32[128,128]{1,0:T(8,128)} %get-tuple-element.22), channel_id=1, source_target_pairs={{0,2},{1,3},{2,0},{3,1},{4,6},{5,7},{6,4},{7,5},{8,10},{9,11},{10,... | collective-permute-start | bytes 196616 | tf_op jit(solution)/shard_map/ppermute | solution.py:530
  47.6 0.7 %collective-permute-start.4 = (f32[128,128]{1,0:T(8,128)}, f32[128,128]{1,0:T(8,128)S(1)}, u32[]{:S(2)}, u32[]{:S(2)}) collective-permute-start(f32[128,128]{1,0:T(8,128)} %get-tuple-element.23), channel_id=1, source_target_pairs={{0,3},{1,0},{2,1},{3,2},{4,7},{5,4},{6,5},{7,6},{8,11},{9,8},{10,9... | collective-permute-start | bytes 196616 | tf_op jit(solution)/shard_map/ppermute | solution.py:530
  48.3 0.4 collective-permute-done.2.part1_ref
  48.7 2.0 %collective-permute-done.3.part2_ref = f32[128,128]{1,0:T(8,128)S(1)} collective-permute-done((f32[128,128]{1,0:T(8,128)}, f32[128,128]{1,0:T(8,128)S(1)}, u32[]{:S(2)}, u32[]{:S(2)}) %collective-permute-start.3) | collective-permute-done | bytes 65568 | tf_op jit(solution)/shard_map/ppermute | solution.py:530
  50.7 0.5 collective-permute-done.4.part3_ref
  51.2 0.0 copy-done.9
  51.2 0.8 %copy-done.6 = f32[128,128]{1,0:T(8,128)S(1)} copy-done((f32[128,128]{1,0:T(8,128)S(1)}, f32[128,128]{1,0:T(8,128)}, u32[]{:S(2)}) %copy-start.6) | copy-done | bytes 65560
  52.1 1.7 %response.1 = (f32[1,32]{1,0:T(1,128)}, f32[1,32]{1,0:T(1,128)}) custom-call(f32[4,16]{1,0:T(4,128)S(1)} %copy-done.8, f32[128,128]{1,0:T(8,128)S(1)} %copy-done.6, f32[128,128]{1,0:T(8,128)S(1)} %collective-permute-done.2.part1_ref, f32[128,128]{1,0:T(8,128)S(1)} %collective-permute-done.3.part2_ref, f32[128,128]{1,0:T(8,128)S(1)} %collective-permute-done.4.part3_ref, ...), custom_call_target="tpu_custom_call" | custom-call | tf_op jit(solution)/shard_map/response/pallas_call | solution.py:535
  (13 shorter events, 0.0 us)
Async XLA Ops:
  0.6 12.1 %copy-start = (f32[48,32,2,128]{3,2,1,0:T(2,128)S(1)}, f32[48,32,2,128]{3,2,1,0:T(2,128)}, u32[]{:S(2)}) copy-start(f32[48,32,2,128]{3,2,1,0:T(2,128)} %param.10) | copy-start | bytes 4718596
  0.6 50.5 %copy-start.8 = (f32[4,16]{1,0:T(4,128)S(1)}, f32[4,16]{1,0:T(4,128)}, u32[]{:S(2)}) copy-start(f32[4,16]{1,0:T(4,128)} %curves_ref.1) | copy-start | bytes 772
  0.7 50.5 %copy-start.9 = (f32[128]{0:T(128)S(1)}, f32[128]{0:T(128)}, u32[]{:S(2)}) copy-start(f32[128]{0:T(128)} %param.13) | copy-start | bytes 1540
  0.7 50.5 %copy-start.10 = (s32[32]{0:T(128)S(1)}, s32[32]{0:T(128)}, u32[]{:S(2)}) copy-start(s32[32]{0:T(128)} %param.17) | copy-start | bytes 388
  4.6 46.6 %copy-start.2 = (bf16[512,256]{1,0:T(8,128)(2,1)S(1)}, bf16[512,256]{1,0:T(8,128)(2,1)}, u32[]{:S(2)}) copy-start(bf16[512,256]{1,0:T(8,128)(2,1)} %constant.5.clone.table_low_ref) | copy-start | bytes 786436
  4.6 46.6 %copy-start.3 = (bf16[512,256]{1,0:T(8,128)(2,1)S(1)}, bf16[512,256]{1,0:T(8,128)(2,1)}, u32[]{:S(2)}) copy-start(bf16[512,256]{1,0:T(8,128)(2,1)} %constant.4.clone.table_high_ref) | copy-start | bytes 786436
  4.6 8.2 %collective-permute-start.1 = (f32[152,128]{1,0:T(8,128)}, f32[152,128]{1,0:T(8,128)S(1)}, u32[]{:S(2)}, u32[]{:S(2)}) collective-permute-start(f32[152,128]{1,0:T(8,128)} %get-tuple-element.14.own_ref), channel_id=1, source_target_pairs={{4,0},{8,4},{12,8},{16,12},{20,16},{24,20},{28,24},{32,28},{36,32}... | collective-permute-start | bytes 233480 | tf_op jit(solution)/shard_map/ppermute | solution.py:497
  8.1 4.7 %collective-permute-start = (f32[104,128]{1,0:T(8,128)}, f32[104,128]{1,0:T(8,128)S(1)}, u32[]{:S(2)}, u32[]{:S(2)}) collective-permute-start(f32[104,128]{1,0:T(8,128)} %get-tuple-element.15), channel_id=1, source_target_pairs={{0,4},{4,8},{8,12},{12,16},{16,20},{20,24},{24,28},{28,32},{32,36}... | collective-permute-start | bytes 159752 | tf_op jit(solution)/shard_map/ppermute | solution.py:496
  12.8 0.9 %copy-start.4 = (bf16[208,256]{1,0:T(8,128)(2,1)S(1)}, bf16[208,256]{1,0:T(8,128)(2,1)}, u32[]{:S(2)}) copy-start(bf16[208,256]{1,0:T(8,128)(2,1)} %get-tuple-element.16.lhs_ref) | copy-start | bytes 319492
  13.7 0.9 %copy-start.5 = (f32[152,128]{1,0:T(8,128)S(1)}, f32[152,128]{1,0:T(8,128)}, u32[]{:S(2)}) copy-start(f32[152,128]{1,0:T(8,128)} %get-tuple-element.14.own_ref) | copy-start | bytes 233476
  14.6 0.7 %copy-start.7 = (f32[48,128]{1,0:T(8,128)S(1)}, f32[48,128]{1,0:T(8,128)}, u32[]{:S(2)}) copy-start(f32[48,128]{1,0:T(8,128)} %get-tuple-element.17.cols_ref) | copy-start | bytes 73732
  21.6 0.9 %copy-start.1 = (f32[1536,128]{1,0:T(8,128)}, f32[1536,128]{1,0:T(8,128)S(1)}, u32[]{:S(2)}) copy-start(f32[1536,128]{1,0:T(8,128)S(1)} %get-tuple-element.19.strain_in_ref) | copy-start | bytes 2359300
  42.6 6.2 %collective-permute-start.2 = (f32[128,128]{1,0:T(8,128)}, f32[128,128]{1,0:T(8,128)S(1)}, u32[]{:S(2)}, u32[]{:S(2)}) collective-permute-start(f32[128,128]{1,0:T(8,128)} %get-tuple-element.21), channel_id=1, source_target_pairs={{0,1},{1,2},{2,3},{3,0},{4,5},{5,6},{6,7},{7,4},{8,9},{9,10},{10,1... | collective-permute-start | bytes 196616 | tf_op jit(solution)/shard_map/ppermute | solution.py:530
  44.3 6.4 %collective-permute-start.3 = (f32[128,128]{1,0:T(8,128)}, f32[128,128]{1,0:T(8,128)S(1)}, u32[]{:S(2)}, u32[]{:S(2)}) collective-permute-start(f32[128,128]{1,0:T(8,128)} %get-tuple-element.22), channel_id=1, source_target_pairs={{0,2},{1,3},{2,0},{3,1},{4,6},{5,7},{6,4},{7,5},{8,10},{9,11},{10,... | collective-permute-start | bytes 196616 | tf_op jit(solution)/shard_map/ppermute | solution.py:530
  47.6 3.6 %collective-permute-start.4 = (f32[128,128]{1,0:T(8,128)}, f32[128,128]{1,0:T(8,128)S(1)}, u32[]{:S(2)}, u32[]{:S(2)}) collective-permute-start(f32[128,128]{1,0:T(8,128)} %get-tuple-element.23), channel_id=1, source_target_pairs={{0,3},{1,0},{2,1},{3,2},{4,7},{5,4},{6,5},{7,6},{8,11},{9,8},{10,9... | collective-permute-start | bytes 196616 | tf_op jit(solution)/shard_map/ppermute | solution.py:530
  51.2 0.8 %copy-start.6 = (f32[128,128]{1,0:T(8,128)S(1)}, f32[128,128]{1,0:T(8,128)}, u32[]{:S(2)}) copy-start(f32[128,128]{1,0:T(8,128)} %get-tuple-element.20.part0_ref) | copy-start | bytes 196612

commit v4 on v3

--- a/solution.py
+++ b/solution.py
@@ -45,12 +45,14 @@
 
 def edges_kernel(
     load_ref, modulus_ref, mass_ref, stiffness_ref, template_ref, strain_map_ref,
-    up_ref, down_ref, lhs_ref, cols_ref,
-    buffer_ref, slots_ref, turned_ref, square_ref, copied,
+    up_ref, down_ref, own_ref, lhs_ref, cols_ref,
+    buffer_ref, slots_ref, turned_ref, square_ref, small_ref, copied,
 ):
     half, parts, chunks = 48, 64, 3
     per = half // chunks
     length = per * parts
+    full = 2 * half
+    comps = strain_map_ref.shape[0]
     copies = [
         pltpu.make_async_copy(
             load_ref.at[pl.ds(i * length, length)], buffer_ref.at[pl.ds(i * length, length)],
@@ -58,13 +60,17 @@
         )
         for i in range(chunks)
     ]
-    for copy in copies:
+    smalls = [
+        pltpu.make_async_copy(source, target, copied.at[chunks + i])
+        for i, (source, target) in enumerate((
+            (modulus_ref, small_ref.at[0]), (mass_ref, small_ref.at[1]),
+        ))
+    ]
+    square_ref[...] = jnp.zeros(square_ref.shape, F32)
+    for copy in copies + smalls:
         copy.start()
 
-    full = 2 * half
-    square_ref[...] = jnp.zeros(square_ref.shape, F32)
     square_ref[:full, :full] = stiffness_ref[...]
-    comps = strain_map_ref.shape[0]
     square_ref[full : full + comps, :full] = strain_map_ref[...]
     square_ref[full + 8 : full + 9, :full] = template_ref[...]
     stiff = square_ref[:full, :]
@@ -108,24 +114,27 @@
             turned_ref[...] = jnp.transpose(slots_ref[...])
             if turn == 0:
                 pair = turned_ref[pl.ds(1, per, stride=SLOT), :]
-                up_ref[at : at + per, :] = pair
-                down_ref[at : at + per, :] = pair
+                for ref in (up_ref, down_ref, own_ref):
+                    ref[at : at + per, :] = pair
             else:
                 pair = turned_ref[pl.ds(0, per, stride=SLOT), :]
-                up_ref[half + at : half + at + per, :] = pair
-                down_ref[half + at : half + at + per, :] = pair
+                for ref in (up_ref, down_ref, own_ref):
+                    ref[half + at : half + at + per, :] = pair
                 down_ref[UP_ROWS + at : UP_ROWS + at + per, :] = turned_ref[
                     pl.ds(1, per, stride=SLOT), :
                 ]
-    for ref in (up_ref, down_ref):
-        ref[ROW_AT : ROW_AT + 1, :] = modulus_ref[...]
-        ref[ROW_AT + 1 : ROW_AT + 2, :] = mass_ref[...]
+    for copy in smalls:
+        copy.wait()
+    for ref in (up_ref, down_ref, own_ref):
+        ref[ROW_AT : ROW_AT + 1, :] = small_ref[0]
+        ref[ROW_AT + 1 : ROW_AT + 2, :] = small_ref[1]
         ref[ROW_AT + 2 : UP_ROWS, :] = jnp.zeros((UP_ROWS - ROW_AT - 2, LANES), F32)
 
 
 def main_kernel(
-    load_ref, own_ref, left_ref, right_ref, lhs_ref, cols_ref, strain_out_ref, dots_out_ref,
-    strain_ref, field_ref, inv_ref, border_ref, dots_ref, copied,
+    load_ref, own_ref, left_ref, right_ref, lhs_ref, cols_ref,
+    out0_ref, out1_ref, out2_ref, out3_ref, dots_out_ref,
+    strain_ref, field_ref, inv_ref, border_ref, dots_ref,
 ):
     half, parts = 48, 64
     freqs = parts // 2
@@ -310,17 +319,33 @@
         dots_ref[pl.ds(5 * freqs + f, 1), :] = -(jnp.sum(total, axis=0, keepdims=True) + extra)
         return carry
 
-    rows = 2 * freqs * 8
-    copies = []
+    quarter = LANES // 4
+    cell = lane_ids(8) // quarter
+    outs = (out0_ref, out1_ref, out2_ref, out3_ref)
+
+    def pack(stage, block):
+        def comp(k, c):
+            start = (((stage * 2 + k) * freqs) + block * 8) * 8 + c
+            return strain_ref[pl.ds(start, 8, stride=8), :]
+
+        comps = {(k, c): comp(k, c) for k in range(2) for c in range(6)}
+        places = [
+            (stage * parts + k * freqs, [(k, c) for c in range(4)]) for k in range(2)
+        ] + [(3 * parts + stage * freqs, [(0, 4), (0, 5), (1, 4), (1, 5)])]
+        for step in range(4):
+            dest = (freq_group + step) % 4
+            for row, names in places:
+                held = None
+                for i, name in enumerate(names):
+                    moved = pltpu.roll(comps[name], quarter * ((i + 4 - dest) % 4), 1)
+                    held = moved if held is None else jnp.where(cell == i, moved, held)
+                outs[step][row + block * 8 : row + block * 8 + 8, :] = held
+
     for stage, step in enumerate((first, second, third)):
         rims = rim_stage(stage, rims)
         lax.fori_loop(0, freqs, step, 0, unroll=UNROLL)
-        block = pl.ds(stage * rows, rows)
-        copy = pltpu.make_async_copy(
-            strain_ref.at[block], strain_out_ref.at[block], copied.at[stage]
-        )
-        copy.start()
-        copies.append(copy)
+        for block in range(freqs // 8):
+            pack(stage, block)
 
     dots_ref[DOTS * freqs :, :] = jnp.zeros((256 - DOTS * freqs, LANES), F32)
     sums = lax.dot_general(
@@ -331,8 +356,6 @@
     pair = jnp.where(row % 2 == 0, sums[:, :LANES], sums[:, LANES:])
     for i in range(dots_out_ref.shape[0] // 8):
         dots_out_ref[8 * i : 8 * i + 8, :] = pair
-    for copy in copies:
-        copy.wait()
 
 
 def coefficients(h):
@@ -376,60 +399,41 @@
     return result
 
 
-def combine_kernel(
-    dots_ref, strain_in_ref, out0_ref, out1_ref, out2_ref, out3_ref, strain_ref, copied
+def final_kernel(
+    curves_ref, dots_ref, part0_ref, part1_ref, part2_ref, part3_ref,
+    table_high_ref, table_low_ref, modulus_ref, soil_ref,
+    modulus_out_ref, strain_out_ref, spectra_ref,
 ):
-    copy = pltpu.make_async_copy(strain_in_ref, strain_ref, copied)
-    copy.start()
     freq_group = lax.axis_index("freq")
-    freqs, comps = 32, 6
+    parts, freqs = 64, 32
     total = jnp.zeros((8, LANES), F32)
     for i in range(dots_ref.shape[0] // 8):
         total = total + dots_ref[8 * i : 8 * i + 8, :]
     square = jnp.concatenate([total, jnp.zeros((LANES - 8, LANES), F32)], 0)
     turned = jnp.transpose(square)
-    odd = lane_ids(LANES) % 2 == 1
-    even_sums = jnp.sum(jnp.where(odd, 0.0, turned), axis=1, keepdims=True)
-    odd_sums = jnp.sum(jnp.where(odd, turned, 0.0), axis=1, keepdims=True)
-    h = [even_sums[freqs * i : freqs * (i + 1)] for i in range(4)]
-    h += [odd_sums[freqs * i : freqs * (i + 1)] for i in range(2)]
-    weights = [jnp.broadcast_to(c, (freqs, LANES)) for c in coefficients(h)]
-    quarter = LANES // 4
-    cell = lane_ids(freqs) // quarter
-    outs = (out0_ref, out1_ref, out2_ref, out3_ref)
-    copy.wait()
-    for k in range(2):
-        spectra = [
-            sum(
-                weights[j] * strain_ref[pl.ds((2 * j + k) * freqs * 8 + c, freqs, stride=8), :]
+    beside = pltpu.roll(turned, 127, 1)
+    h = [turned[freqs * i : freqs * (i + 1)] for i in range(4)]
+    h += [beside[freqs * i : freqs * (i + 1)] for i in range(2)]
+    coefs = coefficients(h)
+    lanes = lane_ids(freqs)
+    for step, part_ref in enumerate((part0_ref, part1_ref, part2_ref, part3_ref)):
+        source = (freq_group + 4 - step) % 4
+        weights = [
+            jnp.sum(jnp.where(lanes == 2 * source, c, 0.0), axis=1, keepdims=True) for c in coefs
+        ]
+
+        def joined(base, per_stage):
+            return sum(
+                weights[j] * part_ref[base + j * per_stage : base + j * per_stage + freqs, :]
                 for j in range(3)
             )
-            for c in range(comps)
-        ]
-        for step in range(4):
-            dest = (freq_group + step) % 4
-            for side in range(2):
-                held = jnp.zeros((freqs, LANES), F32)
-                for c in range(4 * side, min(comps, 4 * side + 4)):
-                    moved = pltpu.roll(spectra[c], quarter * ((c + 4 - dest) % 4), 1)
-                    held = jnp.where(cell == c % 4, moved, held)
-                start = (2 * side + k) * freqs
-                outs[step][start : start + freqs, :] = held
-
-
-def final_kernel(
-    curves_ref, part0_ref, part1_ref, part2_ref, part3_ref,
-    table_high_ref, table_low_ref, modulus_ref, soil_ref,
-    modulus_out_ref, strain_out_ref, spectra_ref,
-):
-    freq_group = lax.axis_index("freq")
-    parts, freqs = 64, 32
-    for step, part_ref in enumerate((part0_ref, part1_ref, part2_ref, part3_ref)):
-        start = pl.multiple_of((freq_group + 4 - step) % 4 * parts, parts)
-        for side in range(2):
-            spectra_ref[pl.ds(start, parts), side * LANES : (side + 1) * LANES] = part_ref[
-                side * parts : (side + 1) * parts, :
-            ]
+
+        rest = joined(3 * parts, freqs)
+        for k in range(2):
+            start = pl.multiple_of(source * parts + k * freqs, freqs)
+            spectra_ref[pl.ds(start, freqs), :LANES] = joined(k * freqs, parts)
+            side = pltpu.roll(rest, 64, 1) if k else rest
+            spectra_ref[pl.ds(start, freqs), LANES:] = jnp.where(lanes < 64, side, 0.0)
     high, low = halves(spectra_ref[...])
     table_high, table_low = table_high_ref[...], table_low_ref[...]
     history = (
@@ -474,73 +478,64 @@
     slabs = lax.axis_size("elem")
     rows = load.reshape(half * parts, nodes)
     modulus_row, mass_row = modulus.reshape(1, nodes), element_mass.reshape(1, nodes)
-    edge_up, edge_down, lhs, cols = pl.pallas_call(
+    edge_up, edge_down, edge_own, lhs, cols = pl.pallas_call(
         edges_kernel,
         out_shape=[
-            jax.ShapeDtypeStruct((UP_ROWS, LANES), F32),
-            jax.ShapeDtypeStruct((DOWN_ROWS, LANES), F32),
-            jax.ShapeDtypeStruct((4 * half + 16, 2 * LANES), BF16),
-            jax.ShapeDtypeStruct((half, LANES), F32),
+            pltpu.VMEM((UP_ROWS, LANES), F32),
+            pltpu.VMEM((DOWN_ROWS, LANES), F32),
+            pltpu.VMEM((UP_ROWS, LANES), F32),
+            pltpu.VMEM((4 * half + 16, 2 * LANES), BF16),
+            pltpu.VMEM((half, LANES), F32),
         ],
-        in_specs=[HBM] + [VMEM] * 5,
-        out_specs=[VMEM] * 4,
+        in_specs=[HBM] * 3 + [VMEM] * 3,
+        out_specs=[VMEM] * 5,
         scratch_shapes=[
             pltpu.VMEM((half * parts, LANES), F32),
             pltpu.VMEM((LANES, LANES), F32),
             pltpu.VMEM((LANES, LANES), F32),
             pltpu.VMEM((LANES, LANES), F32),
-            pltpu.SemaphoreType.DMA((3,)),
+            pltpu.VMEM((2, 1, LANES), F32),
+            pltpu.SemaphoreType.DMA((5,)),
         ],
         name="edges",
     )(rows, modulus_row, mass_row, stiffness, mass_template.reshape(1, -1), strain_map)
     from_left = lax.ppermute(edge_up, "elem", [(i, i + 1) for i in range(slabs - 1)])
     from_right = lax.ppermute(edge_down, "elem", [(i + 1, i) for i in range(slabs - 1)])
-    strains, dots = pl.pallas_call(
+    packed = 9 * freq_dev
+    outs = pl.pallas_call(
         main_kernel,
-        out_shape=[
-            jax.ShapeDtypeStruct((3 * parts * 8, LANES), F32),
-            jax.ShapeDtypeStruct((2 * slabs, LANES), F32),
-        ],
+        out_shape=[jax.ShapeDtypeStruct((packed, LANES), F32)] * 4
+        + [jax.ShapeDtypeStruct((2 * slabs * groups, LANES), F32)],
         in_specs=[VMEM] * 6,
-        out_specs=[HBM, VMEM],
+        out_specs=[VMEM] * 5,
         scratch_shapes=[
             pltpu.VMEM((3 * parts * 8, LANES), F32),
             pltpu.VMEM((parts, half, LANES), F32),
             pltpu.VMEM((freq_dev, half, LANES), F32),
             pltpu.VMEM((3, half + 8, LANES), F32),
             pltpu.VMEM((256, LANES), F32),
-            pltpu.SemaphoreType.DMA((3,)),
         ],
         compiler_params=pltpu.CompilerParams(vmem_limit_bytes=32 * 1024 * 1024),
         name="krylov",
-    )(rows, edge_down, from_left, from_right, lhs, cols)
-    dots = lax.all_to_all(dots.reshape(slabs, 2, LANES), "elem", 0, 0).reshape(-1, LANES)
-    outs = pl.pallas_call(
-        combine_kernel,
-        out_shape=[jax.ShapeDtypeStruct((2 * parts, LANES), F32)] * groups,
-        in_specs=[VMEM, HBM],
-        out_specs=[VMEM] * groups,
-        scratch_shapes=[
-            pltpu.VMEM((3 * parts * 8, LANES), F32),
-            pltpu.SemaphoreType.DMA,
-        ],
-        name="combine",
-    )(dots, strains)
+    )(rows, edge_own, from_left, from_right, lhs, cols)
     received = [outs[0]] + [
         lax.ppermute(outs[step], "freq", [(i, (i + step) % groups) for i in range(groups)])
         for step in range(1, groups)
     ]
+    dots = lax.all_to_all(
+        outs[4].reshape(slabs * groups, 2, LANES), ("elem", "freq"), 0, 0
+    ).reshape(-1, LANES)
     table_high, table_low = time_table(freq_dev * groups)
     quarter = nodes // groups
     new_modulus, peak_strain = pl.pallas_call(
         final_kernel,
         out_shape=[jax.ShapeDtypeStruct((1, quarter), F32)] * 2,
-        in_specs=[SMEM] + [VMEM] * 8,
+        in_specs=[SMEM] + [VMEM] * 9,
         out_specs=[VMEM] * 2,
         scratch_shapes=[pltpu.VMEM((groups * parts, 2 * LANES), F32)],
         compiler_params=pltpu.CompilerParams(vmem_limit_bytes=32 * 1024 * 1024),
         name="response",
-    )(curves, *received, jnp.asarray(table_high), jnp.asarray(table_low),
+    )(curves, dots, *received, jnp.asarray(table_high), jnp.asarray(table_low),
       modulus_row, soil_type.reshape(1, quarter))
     return new_modulus.reshape(quarter), peak_strain.reshape(quarter)
 

time: 54.6 us -> 46.8 us (0.86); the launches traced: 53.7 us -> 46.6 us
  local copies, waits for them, and re-layouts: 4.26 us -> 0.03 us
  blocking collectives: 17.2 us -> 20.7 us
  waiting for transfers between devices: 4.4 us -> 1.2 us
  Pallas kernels: 14.7 us -> 11.6 us
    unnamed x22 -> x12, local copies, waits for them, and re-layouts: 4.26 us -> 0.03 us
    all_to_all x1, blocking collectives: 17.2 us -> 20.7 us  [per_device(): lax.all_to_all(outs[4].reshape(slabs * groups, 2, LANES), ('elem', 'freq'...]
    pallas_call x3 -> x2, Pallas kernels: 13 us -> 9.57 us  [the longest x1 6.37 us: per_device(): pl.pallas_call(main_kernel, out_shape=[jax.ShapeDtypeStruct((packed, LANE...]
    ppermute x3, waiting for transfers between devices: 2.89 us -> 0.01 us  [per_device(): lax.ppermute(outs[step], 'freq', [(i, (i + step) % groups) for i in range...]
  transfers between devices with their start and end apart: 5 -> 5, of which waited for: 4 -> 1; matrix products, arithmetic and copies ran while one was open for 0% -> 0% of each run, Pallas kernels for 0% -> 0%
where the time goes in v4:
time: 46.8 us; the launch traced here: 46.6 us
  blocking collectives  20.7 us (44%)
  starting transfers between devices  12.3 us (26%)
  Pallas kernels  11.6 us (25%)
  waiting for transfers between devices  1.2 us (3%)
  between operations  0.76 us (2%)
    all_to_all x1, blocking collectives, per_device(): lax.all_to_all(outs[4].reshape(slabs * groups, 2, LANES), ('elem', 'freq'...  20.7 us
    pallas_call x1, Pallas kernels, per_device(): pl.pallas_call(main_kernel, out_shape=[jax.ShapeDtypeStruct((packed, LANE...  6.37 us
    ppermute x3, starting transfers between devices, per_device(): lax.ppermute(outs[step], 'freq', [(i, (i + step) % groups) for i in range...  5.74 us
    ppermute x1, starting transfers between devices, per_device(): lax.ppermute(edge_down, 'elem', [(i + 1, i) for i in range(slabs - 1)])  3.33 us
    pallas_call x1, Pallas kernels, per_device(): pl.pallas_call(edges_kernel, out_shape=[pltpu.VMEM((UP_ROWS, LANES), F32)...  3.2 us
    ppermute x1, starting transfers between devices, per_device(): lax.ppermute(edge_up, 'elem', [(i, i + 1) for i in range(slabs - 1)])  3.19 us
    pallas_call x1, Pallas kernels, per_device(): pl.pallas_call(final_kernel, out_shape=[jax.ShapeDtypeStruct((1, quarter)...  2.05 us
    ppermute x1, waiting for transfers between devices, per_device(): lax.ppermute(edge_up, 'elem', [(i, i + 1) for i in range(slabs - 1)])  1.19 us
  transfers between devices with their start and end apart: 5, of which 1 were waited for; matrix products, arithmetic and copies ran while one was open for 0% of the time, Pallas kernels for 0%

profile of v4, /device:TPU:1, one launch (start us, length us, event | category | flops | bytes accessed | tf_op | source)
XLA Modules:
  0.0 46.6 jit_solution(4941789525783111711)
XLA Ops:
  0.6 0.0 copy-start
  0.6 0.0 copy-start.1
  0.7 0.0 copy-start.2
  0.7 0.0 copy-start.3
  0.7 0.0 copy-start.4
  0.7 0.0 copy-start.5
  0.7 3.2 %edges.1 = (f32[104,128]{1,0:T(8,128)S(1)}, f32[152,128]{1,0:T(8,128)S(1)}, f32[104,128]{1,0:T(8,128)S(1)}, bf16[208,256]{1,0:T(8,128)(2,1)S(1)}, f32[48,128]{1,0:T(8,128)S(1)}) custom-call(f32[3072,128]{1,0:T(8,128)} %bitcast.9, f32[1,128]{1,0:T(1,128)} %bitcast.13, f32[1,128]{1,0:T(1,128)} %bitcast.16, f32[96,96]{1,0:T(8,128)} %stiffness_ref.1, ...), custom_call_target="tpu_custom_call" | custom-call | tf_op jit(solution)/shard_map/edges/pallas_call | solution.py:481
  3.9 3.3 %collective-permute-start.1 = (f32[152,128]{1,0:T(8,128)S(1)}, f32[152,128]{1,0:T(8,128)S(1)}, u32[]{:S(2)}, u32[]{:S(2)}) collective-permute-start(f32[152,128]{1,0:T(8,128)S(1)} %get-tuple-element.16), channel_id=1, source_target_pairs={{4,0},{8,4},{12,8},{16,12},{20,16},{24,20},{28,24},{32,28},{36,32}... | collective-permute-start | bytes 233480 | tf_op jit(solution)/shard_map/ppermute | solution.py:503
  7.2 3.2 %collective-permute-start = (f32[104,128]{1,0:T(8,128)S(1)}, f32[104,128]{1,0:T(8,128)S(1)}, u32[]{:S(2)}, u32[]{:S(2)}) collective-permute-start(f32[104,128]{1,0:T(8,128)S(1)} %get-tuple-element.15), channel_id=1, source_target_pairs={{0,4},{4,8},{8,12},{12,16},{16,20},{20,24},{24,28},{28,32},{32,36}... | collective-permute-start | bytes 159752 | tf_op jit(solution)/shard_map/ppermute | solution.py:502
  10.4 1.2 %collective-permute-done.left_ref = f32[104,128]{1,0:T(8,128)S(1)} collective-permute-done((f32[104,128]{1,0:T(8,128)S(1)}, f32[104,128]{1,0:T(8,128)S(1)}, u32[]{:S(2)}, u32[]{:S(2)}) %collective-permute-start) | collective-permute-done | bytes 53280 | tf_op jit(solution)/shard_map/ppermute | solution.py:502
  11.6 0.0 collective-permute-done.1.right_ref
  11.6 0.0 copy-done
  11.6 6.4 %krylov.1 = (f32[288,128]{1,0:T(8,128)S(1)}, f32[288,128]{1,0:T(8,128)S(1)}, f32[288,128]{1,0:T(8,128)S(1)}, f32[288,128]{1,0:T(8,128)S(1)}, f32[256,128]{1,0:T(8,128)S(1)}) custom-call(f32[3072,128]{1,0:T(8,128)S(1)} %bitcast.10, f32[104,128]{1,0:T(8,128)S(1)} %get-tuple-element.14.own_ref, f32[104,128]{1,0:T(8,128)S(1)} %collective-permute-done.left_ref, ...), custom_call_target="tpu_custom_call" | custom-call | tf_op jit(solution)/shard_map/krylov/pallas_call | solution.py:505
  18.0 1.7 %collective-permute-start.2 = (f32[288,128]{1,0:T(8,128)S(1)}, f32[288,128]{1,0:T(8,128)S(1)}, u32[]{:S(2)}, u32[]{:S(2)}) collective-permute-start(f32[288,128]{1,0:T(8,128)S(1)} %get-tuple-element.21), channel_id=1, source_target_pairs={{0,1},{1,2},{2,3},{3,0},{4,5},{5,6},{6,7},{7,4},{8,9},{9,10},{10,1... | collective-permute-start | bytes 442376 | tf_op jit(solution)/shard_map/ppermute | solution.py:522
  19.7 3.3 %collective-permute-start.3 = (f32[288,128]{1,0:T(8,128)S(1)}, f32[288,128]{1,0:T(8,128)S(1)}, u32[]{:S(2)}, u32[]{:S(2)}) collective-permute-start(f32[288,128]{1,0:T(8,128)S(1)} %get-tuple-element.22), channel_id=1, source_target_pairs={{0,2},{1,3},{2,0},{3,1},{4,6},{5,7},{6,4},{7,5},{8,10},{9,11},{10,... | collective-permute-start | bytes 442376 | tf_op jit(solution)/shard_map/ppermute | solution.py:522
  23.0 0.7 %collective-permute-start.4 = (f32[288,128]{1,0:T(8,128)S(1)}, f32[288,128]{1,0:T(8,128)S(1)}, u32[]{:S(2)}, u32[]{:S(2)}) collective-permute-start(f32[288,128]{1,0:T(8,128)S(1)} %get-tuple-element.23), channel_id=1, source_target_pairs={{0,3},{1,0},{2,1},{3,2},{4,7},{5,4},{6,5},{7,6},{8,11},{9,8},{10,9... | collective-permute-start | bytes 442376 | tf_op jit(solution)/shard_map/ppermute | solution.py:522
  23.8 20.7 %all_to_all.5 = f32[128,2,128]{2,1,0:T(2,128)S(1)} all-to-all(f32[128,2,128]{2,1,0:T(2,128)S(1)} %bitcast.12), channel_id=1, replica_groups=mesh['elem'=32,'freq'=4] {'elem','freq'}, dimensions={0} | all-to-all | bytes 262144 | tf_op jit(solution)/shard_map/all_to_all | solution.py:525
  44.5 0.0 collective-permute-done.2.part1_ref
  44.5 0.0 collective-permute-done.3.part2_ref
  44.5 0.0 collective-permute-done.4.part3_ref
  44.5 0.0 copy-done.1
  44.5 0.0 copy-done.2
  44.5 0.0 copy-done.3
  44.6 2.1 %response.1 = (f32[1,32]{1,0:T(1,128)}, f32[1,32]{1,0:T(1,128)}) custom-call(f32[4,16]{1,0:T(4,128)S(1)} %copy-done.3, f32[256,128]{1,0:T(8,128)S(1)} %bitcast.11, f32[288,128]{1,0:T(8,128)S(1)} %get-tuple-element.20.part0_ref, f32[288,128]{1,0:T(8,128)S(1)} %collective-permute-done.2.part1_ref, f32[288,128]{1,0:T(8,128)S(1)} %collective-permute-done.3.part2_ref, ...), custom_call_target="tpu_custom_call" | custom-call | tf_op jit(solution)/shard_map/response/pallas_call | solution.py:530
  (2 shorter events, 0.0 us)
Async XLA Ops:
  0.6 11.0 %copy-start = (f32[48,32,2,128]{3,2,1,0:T(2,128)S(1)}, f32[48,32,2,128]{3,2,1,0:T(2,128)}, u32[]{:S(2)}) copy-start(f32[48,32,2,128]{3,2,1,0:T(2,128)} %param.10) | copy-start | bytes 4718596
  0.6 43.9 %copy-start.1 = (bf16[512,256]{1,0:T(8,128)(2,1)S(1)}, bf16[512,256]{1,0:T(8,128)(2,1)}, u32[]{:S(2)}) copy-start(bf16[512,256]{1,0:T(8,128)(2,1)} %constant.5.clone.table_low_ref) | copy-start | bytes 786436
  0.7 43.9 %copy-start.2 = (bf16[512,256]{1,0:T(8,128)(2,1)S(1)}, bf16[512,256]{1,0:T(8,128)(2,1)}, u32[]{:S(2)}) copy-start(bf16[512,256]{1,0:T(8,128)(2,1)} %constant.4.clone.table_high_ref) | copy-start | bytes 786436
  0.7 43.9 %copy-start.3 = (f32[4,16]{1,0:T(4,128)S(1)}, f32[4,16]{1,0:T(4,128)}, u32[]{:S(2)}) copy-start(f32[4,16]{1,0:T(4,128)} %curves_ref.1) | copy-start | bytes 772
  0.7 43.9 %copy-start.4 = (f32[128]{0:T(128)S(1)}, f32[128]{0:T(128)}, u32[]{:S(2)}) copy-start(f32[128]{0:T(128)} %param.13) | copy-start | bytes 1540
  0.7 43.9 %copy-start.5 = (s32[32]{0:T(128)S(1)}, s32[32]{0:T(128)}, u32[]{:S(2)}) copy-start(s32[32]{0:T(128)} %param.17) | copy-start | bytes 388
  3.9 7.7 %collective-permute-start.1 = (f32[152,128]{1,0:T(8,128)S(1)}, f32[152,128]{1,0:T(8,128)S(1)}, u32[]{:S(2)}, u32[]{:S(2)}) collective-permute-start(f32[152,128]{1,0:T(8,128)S(1)} %get-tuple-element.16), channel_id=1, source_target_pairs={{4,0},{8,4},{12,8},{16,12},{20,16},{24,20},{28,24},{32,28},{36,32}... | collective-permute-start | bytes 233480 | tf_op jit(solution)/shard_map/ppermute | solution.py:503
  7.2 4.4 %collective-permute-start = (f32[104,128]{1,0:T(8,128)S(1)}, f32[104,128]{1,0:T(8,128)S(1)}, u32[]{:S(2)}, u32[]{:S(2)}) collective-permute-start(f32[104,128]{1,0:T(8,128)S(1)} %get-tuple-element.15), channel_id=1, source_target_pairs={{0,4},{4,8},{8,12},{12,16},{16,20},{20,24},{24,28},{28,32},{32,36}... | collective-permute-start | bytes 159752 | tf_op jit(solution)/shard_map/ppermute | solution.py:502
  18.0 26.5 %collective-permute-start.2 = (f32[288,128]{1,0:T(8,128)S(1)}, f32[288,128]{1,0:T(8,128)S(1)}, u32[]{:S(2)}, u32[]{:S(2)}) collective-permute-start(f32[288,128]{1,0:T(8,128)S(1)} %get-tuple-element.21), channel_id=1, source_target_pairs={{0,1},{1,2},{2,3},{3,0},{4,5},{5,6},{6,7},{7,4},{8,9},{9,10},{10,1... | collective-permute-start | bytes 442376 | tf_op jit(solution)/shard_map/ppermute | solution.py:522
  19.7 24.8 %collective-permute-start.3 = (f32[288,128]{1,0:T(8,128)S(1)}, f32[288,128]{1,0:T(8,128)S(1)}, u32[]{:S(2)}, u32[]{:S(2)}) collective-permute-start(f32[288,128]{1,0:T(8,128)S(1)} %get-tuple-element.22), channel_id=1, source_target_pairs={{0,2},{1,3},{2,0},{3,1},{4,6},{5,7},{6,4},{7,5},{8,10},{9,11},{10,... | collective-permute-start | bytes 442376 | tf_op jit(solution)/shard_map/ppermute | solution.py:522
  23.0 21.5 %collective-permute-start.4 = (f32[288,128]{1,0:T(8,128)S(1)}, f32[288,128]{1,0:T(8,128)S(1)}, u32[]{:S(2)}, u32[]{:S(2)}) collective-permute-start(f32[288,128]{1,0:T(8,128)S(1)} %get-tuple-element.23), channel_id=1, source_target_pairs={{0,3},{1,0},{2,1},{3,2},{4,7},{5,4},{6,5},{7,6},{8,11},{9,8},{10,9... | collective-permute-start | bytes 442376 | tf_op jit(solution)/shard_map/ppermute | solution.py:522

commit v5 on v4

--- a/solution.py
+++ b/solution.py
@@ -22,8 +22,8 @@
 VMEM = pl.BlockSpec(memory_space=pltpu.VMEM)
 SMEM = pl.BlockSpec(memory_space=pltpu.SMEM)
 HBM = pl.BlockSpec(memory_space=pltpu.HBM)
-PAIR_ROWS, ROW_AT = 96, 96
-UP_ROWS, DOWN_ROWS = 104, 152
+OWN_ROWS, OWN_AT = 104, 96
+SENT_ROWS, SENT_AT = 80, 72
 
 
 def lane_ids(rows=1):
@@ -45,8 +45,8 @@
 
 def edges_kernel(
     load_ref, modulus_ref, mass_ref, stiffness_ref, template_ref, strain_map_ref,
-    up_ref, down_ref, own_ref, lhs_ref, cols_ref,
-    buffer_ref, slots_ref, turned_ref, square_ref, small_ref, copied,
+    first_ref, second_ref, own_ref, lhs_ref, cols_ref, buffer_ref,
+    slots_ref, turned_ref, square_ref, small_ref, third_ref, copied,
 ):
     half, parts, chunks = 48, 64, 3
     per = half // chunks
@@ -66,9 +66,9 @@
             (modulus_ref, small_ref.at[0]), (mass_ref, small_ref.at[1]),
         ))
     ]
-    square_ref[...] = jnp.zeros(square_ref.shape, F32)
     for copy in copies + smalls:
         copy.start()
+    square_ref[...] = jnp.zeros(square_ref.shape, F32)
 
     square_ref[:full, :full] = stiffness_ref[...]
     square_ref[full : full + comps, :full] = strain_map_ref[...]
@@ -113,33 +113,44 @@
             slots_ref[pl.ds(1, parts, stride=2), :] = pltpu.roll(held, shift, 1)
             turned_ref[...] = jnp.transpose(slots_ref[...])
             if turn == 0:
-                pair = turned_ref[pl.ds(1, per, stride=SLOT), :]
-                for ref in (up_ref, down_ref, own_ref):
-                    ref[at : at + per, :] = pair
+                own_ref[at : at + per, :] = turned_ref[pl.ds(1, per, stride=SLOT), :]
             else:
-                pair = turned_ref[pl.ds(0, per, stride=SLOT), :]
-                for ref in (up_ref, down_ref, own_ref):
-                    ref[half + at : half + at + per, :] = pair
-                down_ref[UP_ROWS + at : UP_ROWS + at + per, :] = turned_ref[
-                    pl.ds(1, per, stride=SLOT), :
-                ]
+                own_ref[half + at : half + at + per, :] = turned_ref[pl.ds(0, per, stride=SLOT), :]
+                third_ref[at : at + per, :] = turned_ref[pl.ds(1, per, stride=SLOT), :]
     for copy in smalls:
         copy.wait()
-    for ref in (up_ref, down_ref, own_ref):
-        ref[ROW_AT : ROW_AT + 1, :] = small_ref[0]
-        ref[ROW_AT + 1 : ROW_AT + 2, :] = small_ref[1]
-        ref[ROW_AT + 2 : UP_ROWS, :] = jnp.zeros((UP_ROWS - ROW_AT - 2, LANES), F32)
+    own_ref[OWN_AT : OWN_AT + 1, :] = small_ref[0]
+    own_ref[OWN_AT + 1 : OWN_AT + 2, :] = small_ref[1]
+    own_ref[OWN_AT + 2 :, :] = jnp.zeros((OWN_ROWS - OWN_AT - 2, LANES), F32)
+    even = lane_ids() % 2 == 0
+    outer, inner = own_ref[:half, :], own_ref[half : 2 * half, :]
+    third = third_ref[...]
+    up = [jnp.where(even, outer, earlier(inner)), jnp.zeros((half // 2, LANES), F32)]
+    down = [
+        jnp.where(even, later(inner), outer),
+        jnp.where(even, later(third[half // 2 :]), third[: half // 2]),
+    ]
+    even_device = lax.axis_index("elem") % 2 == 0
+    for ref, ahead in ((first_ref, even_device), (second_ref, jnp.logical_not(even_device))):
+        ref[:half, :] = jnp.where(ahead, up[0], down[0])
+        ref[half:SENT_AT, :] = jnp.where(ahead, up[1], down[1])
+        ref[SENT_AT:, :] = own_ref[OWN_AT:, :]
 
 
 def main_kernel(
-    load_ref, own_ref, left_ref, right_ref, lhs_ref, cols_ref,
+    load_ref, own_ref, first_ref, second_ref, lhs_ref, cols_ref,
     out0_ref, out1_ref, out2_ref, out3_ref, dots_out_ref,
     strain_ref, field_ref, inv_ref, border_ref, dots_ref,
 ):
     half, parts = 48, 64
     freqs = parts // 2
     freq_group = lax.axis_index("freq")
-    is_last = lax.axis_index("elem") == lax.axis_size("elem") - 1
+    slab = lax.axis_index("elem")
+    is_last = slab == lax.axis_size("elem") - 1
+    ahead = slab % 2 == 0
+    met_first, met_second = first_ref[...], second_ref[...]
+    from_right = jnp.where(ahead, met_first, met_second)
+    from_left = jnp.where(ahead, met_second, met_first)
     first_order = (freq_group * freqs + 1).astype(F32)
     lanes = lane_ids()
     even = lanes % 2 == 0
@@ -151,9 +162,8 @@
     kd_top, kd_low, mt_top, mt_low = (cols[:, i : i + 1] for i in range(4))
 
     def rows_of(at):
-        own, left, right = (
-            r[ROW_AT + at : ROW_AT + at + 1, :] for r in (own_ref, left_ref, right_ref)
-        )
+        own = own_ref[OWN_AT + at : OWN_AT + at + 1, :]
+        left, right = (r[SENT_AT + at : SENT_AT + at + 1] for r in (from_left, from_right))
         prev = jnp.where(lanes == 0, earlier(left), earlier(own))
 
         def sides(*upper_lower):
@@ -205,16 +215,13 @@
             good = jnp.logical_and(good, jnp.logical_not(beyond))
         inverses.append(jnp.where(good, 1.0 / diag, 0.0))
 
-    def met(at):
-        inward = later(right_ref[at : at + half, :])
-        return jnp.where(even, inward, earlier(left_ref[at : at + half, :]))
-
+    third = from_right[half:SENT_AT]
     rims = [
         own_ref[half : 2 * half, :],
         own_ref[:half, :],
-        met(0),
-        met(half),
-        jnp.where(even, later(right_ref[UP_ROWS:, :]), 0.0),
+        jnp.where(even, later(from_right[:half]), earlier(from_left[:half])),
+        jnp.where(even, from_right[:half], from_left[:half]),
+        jnp.where(even, jnp.concatenate([later(third), third], 0), 0.0),
     ]
     rims = [field * inv for field, inv in zip(rims, inverses)]
 
@@ -333,7 +340,7 @@
             (stage * parts + k * freqs, [(k, c) for c in range(4)]) for k in range(2)
         ] + [(3 * parts + stage * freqs, [(0, 4), (0, 5), (1, 4), (1, 5)])]
         for step in range(4):
-            dest = (freq_group + step) % 4
+            dest = lax.bitwise_xor(freq_group, step)
             for row, names in places:
                 held = None
                 for i, name in enumerate(names):
@@ -417,7 +424,7 @@
     coefs = coefficients(h)
     lanes = lane_ids(freqs)
     for step, part_ref in enumerate((part0_ref, part1_ref, part2_ref, part3_ref)):
-        source = (freq_group + 4 - step) % 4
+        source = lax.bitwise_xor(freq_group, step)
         weights = [
             jnp.sum(jnp.where(lanes == 2 * source, c, 0.0), axis=1, keepdims=True) for c in coefs
         ]
@@ -478,29 +485,32 @@
     slabs = lax.axis_size("elem")
     rows = load.reshape(half * parts, nodes)
     modulus_row, mass_row = modulus.reshape(1, nodes), element_mass.reshape(1, nodes)
-    edge_up, edge_down, edge_own, lhs, cols = pl.pallas_call(
+    first, second, own, lhs, cols, rows = pl.pallas_call(
         edges_kernel,
         out_shape=[
-            pltpu.VMEM((UP_ROWS, LANES), F32),
-            pltpu.VMEM((DOWN_ROWS, LANES), F32),
-            pltpu.VMEM((UP_ROWS, LANES), F32),
+            pltpu.VMEM((SENT_ROWS, LANES), F32),
+            pltpu.VMEM((SENT_ROWS, LANES), F32),
+            pltpu.VMEM((OWN_ROWS, LANES), F32),
             pltpu.VMEM((4 * half + 16, 2 * LANES), BF16),
             pltpu.VMEM((half, LANES), F32),
+            pltpu.VMEM((half * parts, LANES), F32),
         ],
         in_specs=[HBM] * 3 + [VMEM] * 3,
-        out_specs=[VMEM] * 5,
+        out_specs=[VMEM] * 6,
         scratch_shapes=[
-            pltpu.VMEM((half * parts, LANES), F32),
             pltpu.VMEM((LANES, LANES), F32),
             pltpu.VMEM((LANES, LANES), F32),
             pltpu.VMEM((LANES, LANES), F32),
             pltpu.VMEM((2, 1, LANES), F32),
+            pltpu.VMEM((half, LANES), F32),
             pltpu.SemaphoreType.DMA((5,)),
         ],
         name="edges",
     )(rows, modulus_row, mass_row, stiffness, mass_template.reshape(1, -1), strain_map)
-    from_left = lax.ppermute(edge_up, "elem", [(i, i + 1) for i in range(slabs - 1)])
-    from_right = lax.ppermute(edge_down, "elem", [(i + 1, i) for i in range(slabs - 1)])
+    met_first = lax.ppermute(first, "elem", [(i, i ^ 1) for i in range(slabs)])
+    met_second = lax.ppermute(
+        second, "elem", [(i, i + 1 if i % 2 else i - 1) for i in range(1, slabs - 1)]
+    )
     packed = 9 * freq_dev
     outs = pl.pallas_call(
         main_kernel,
@@ -517,9 +527,9 @@
         ],
         compiler_params=pltpu.CompilerParams(vmem_limit_bytes=32 * 1024 * 1024),
         name="krylov",
-    )(rows, edge_own, from_left, from_right, lhs, cols)
+    )(rows, own, met_first, met_second, lhs, cols)
     received = [outs[0]] + [
-        lax.ppermute(outs[step], "freq", [(i, (i + step) % groups) for i in range(groups)])
+        lax.ppermute(outs[step], "freq", [(i, i ^ step) for i in range(groups)])
         for step in range(1, groups)
     ]
     dots = lax.all_to_all(

time: 46.8 us -> 45.2 us (0.966)
  starting transfers between devices: 12.3 us -> 9.79 us
  waiting for transfers between devices: 1.2 us -> 2.11 us
    ppermute x5, starting transfers between devices: 12.3 us -> 9.79 us  [the longest x3 5.1 us: per_device(): lax.ppermute(outs[step], 'freq', [(i, i ^ step) for i in range(groups)])]
    ppermute x5, waiting for transfers between devices: 1.2 us -> 2.11 us  [the longest x1 2.1 us: per_device(): lax.ppermute(second, 'elem', [(i, i + 1 if i % 2 else i - 1) for i in ran...]
where the time goes in v5:
time: 45.2 us; the launch traced here: 45 us
  blocking collectives  20.8 us (46%)
  Pallas kernels  11.5 us (25%)
  starting transfers between devices  9.79 us (22%)
  waiting for transfers between devices  2.11 us (5%)
  between operations  0.75 us (2%)
    all_to_all x1, blocking collectives, per_device(): lax.all_to_all(outs[4].reshape(slabs * groups, 2, LANES), ('elem', 'freq'...  20.8 us
    pallas_call x1, Pallas kernels, per_device(): pl.pallas_call(main_kernel, out_shape=[jax.ShapeDtypeStruct((packed, LANE...  6.26 us
    ppermute x3, starting transfers between devices, per_device(): lax.ppermute(outs[step], 'freq', [(i, i ^ step) for i in range(groups)])  5.1 us
    pallas_call x1, Pallas kernels, per_device(): pl.pallas_call(edges_kernel, out_shape=[pltpu.VMEM((SENT_ROWS, LANES), F3...  3.19 us
    ppermute x1, starting transfers between devices, per_device(): lax.ppermute(second, 'elem', [(i, i + 1 if i % 2 else i - 1) for i in ran...  3.19 us
    ppermute x1, waiting for transfers between devices, per_device(): lax.ppermute(second, 'elem', [(i, i + 1 if i % 2 else i - 1) for i in ran...  2.1 us
    pallas_call x1, Pallas kernels, per_device(): pl.pallas_call(final_kernel, out_shape=[jax.ShapeDtypeStruct((1, quarter)...  2.06 us
    ppermute x1, starting transfers between devices, per_device(): met_first = lax.ppermute(first, 'elem', [(i, i ^ 1) for i in range(slabs)])  1.5 us
  transfers between devices with their start and end apart: 5, of which 1 were waited for; matrix products, arithmetic and copies ran while one was open for 0% of the time, Pallas kernels for 0%

profile of v5, /device:TPU:1, one launch (start us, length us, event | category | flops | bytes accessed | tf_op | source)
XLA Modules:
  0.0 45.0 jit_solution(3591428814325123328)
XLA Ops:
  0.6 0.0 copy-start
  0.6 0.0 copy-start.1
  0.7 0.0 copy-start.2
  0.7 0.0 copy-start.3
  0.7 0.0 copy-start.4
  0.7 3.2 %edges.1 = (f32[80,128]{1,0:T(8,128)S(1)}, f32[80,128]{1,0:T(8,128)S(1)}, f32[104,128]{1,0:T(8,128)S(1)}, bf16[208,256]{1,0:T(8,128)(2,1)S(1)}, f32[48,128]{1,0:T(8,128)S(1)}, /*index=5*/f32[3072,128]{1,0:T(8,128)S(1)}) custom-call(f32[3072,128]{1,0:T(8,128)} %bitcast.14, f32[1,128]{1,0:T(1,128)} %bitcast.11, f32[1,128]{1,0:T(1,128)} %bitcast.15, ...), custom_call_target="tpu_custom_call" | custom-call | tf_op jit(solution)/shard_map/edges/pallas_call | solution.py:488
  3.9 1.5 %collective-permute-start = (f32[80,128]{1,0:T(8,128)S(1)}, f32[80,128]{1,0:T(8,128)S(1)}, u32[]{:S(2)}, u32[]{:S(2)}) collective-permute-start(f32[80,128]{1,0:T(8,128)S(1)} %get-tuple-element.17), channel_id=1, source_target_pairs={{0,4},{4,0},{8,12},{12,8},{16,20},{20,16},{24,28},{28,24},{32,36},... | collective-permute-start | bytes 122888 | tf_op jit(solution)/shard_map/ppermute | solution.py:510
  5.4 3.2 %collective-permute-start.1 = (f32[80,128]{1,0:T(8,128)S(1)}, f32[80,128]{1,0:T(8,128)S(1)}, u32[]{:S(2)}, u32[]{:S(2)}) collective-permute-start(f32[80,128]{1,0:T(8,128)S(1)} %get-tuple-element.18), channel_id=1, source_target_pairs={{4,8},{8,4},{12,16},{16,12},{20,24},{24,20},{28,32},{32,28},{36,40... | collective-permute-start | bytes 122888 | tf_op jit(solution)/shard_map/ppermute | solution.py:511
  8.6 0.0 collective-permute-done.first_ref
  8.6 2.1 %collective-permute-done.1.second_ref = f32[80,128]{1,0:T(8,128)S(1)} collective-permute-done((f32[80,128]{1,0:T(8,128)S(1)}, f32[80,128]{1,0:T(8,128)S(1)}, u32[]{:S(2)}, u32[]{:S(2)}) %collective-permute-start.1) | collective-permute-done | bytes 40992 | tf_op jit(solution)/shard_map/ppermute | solution.py:511
  10.7 6.3 %krylov.1 = (f32[288,128]{1,0:T(8,128)S(1)}, f32[288,128]{1,0:T(8,128)S(1)}, f32[288,128]{1,0:T(8,128)S(1)}, f32[288,128]{1,0:T(8,128)S(1)}, f32[256,128]{1,0:T(8,128)S(1)}) custom-call(f32[3072,128]{1,0:T(8,128)S(1)} %get-tuple-element.15.load_ref, f32[104,128]{1,0:T(8,128)S(1)} %get-tuple-element.16.own_ref, f32[80,128]{1,0:T(8,128)S(1)} %collective-permute-done.first_ref, ...), custom_call_target="tpu_custom_call" | custom-call | tf_op jit(solution)/shard_map/krylov/pallas_call | solution.py:515
  17.0 1.8 %collective-permute-start.2 = (f32[288,128]{1,0:T(8,128)S(1)}, f32[288,128]{1,0:T(8,128)S(1)}, u32[]{:S(2)}, u32[]{:S(2)}) collective-permute-start(f32[288,128]{1,0:T(8,128)S(1)} %get-tuple-element.23), channel_id=1, source_target_pairs={{0,1},{1,0},{2,3},{3,2},{4,5},{5,4},{6,7},{7,6},{8,9},{9,8},{10,11... | collective-permute-start | bytes 442376 | tf_op jit(solution)/shard_map/ppermute | solution.py:532
  18.8 3.3 %collective-permute-start.3 = (f32[288,128]{1,0:T(8,128)S(1)}, f32[288,128]{1,0:T(8,128)S(1)}, u32[]{:S(2)}, u32[]{:S(2)}) collective-permute-start(f32[288,128]{1,0:T(8,128)S(1)} %get-tuple-element.24), channel_id=1, source_target_pairs={{0,2},{1,3},{2,0},{3,1},{4,6},{5,7},{6,4},{7,5},{8,10},{9,11},{10,... | collective-permute-start | bytes 442376 | tf_op jit(solution)/shard_map/ppermute | solution.py:532
  22.1 0.0 collective-permute-start.4
  22.1 20.8 %all_to_all.5 = f32[128,2,128]{2,1,0:T(2,128)S(1)} all-to-all(f32[128,2,128]{2,1,0:T(2,128)S(1)} %bitcast.10), channel_id=1, replica_groups=mesh['elem'=32,'freq'=4] {'elem','freq'}, dimensions={0} | all-to-all | bytes 262144 | tf_op jit(solution)/shard_map/all_to_all | solution.py:535
  42.9 0.0 collective-permute-done.2.part1_ref
  42.9 0.0 collective-permute-done.3.part2_ref
  42.9 0.0 collective-permute-done.4.part3_ref
  42.9 0.0 copy-done
  42.9 0.0 copy-done.1
  42.9 0.0 copy-done.2
  42.9 0.0 copy-done.3
  42.9 0.0 copy-done.4
  42.9 2.1 %response.1 = (f32[1,32]{1,0:T(1,128)}, f32[1,32]{1,0:T(1,128)}) custom-call(f32[4,16]{1,0:T(4,128)S(1)} %copy-done.2, f32[256,128]{1,0:T(8,128)S(1)} %bitcast.9, f32[288,128]{1,0:T(8,128)S(1)} %get-tuple-element.22.part0_ref, f32[288,128]{1,0:T(8,128)S(1)} %collective-permute-done.2.part1_ref, f32[288,128]{1,0:T(8,128)S(1)} %collective-permute-done.3.part2_ref, ...), custom_call_target="tpu_custom_call" | custom-call | tf_op jit(solution)/shard_map/response/pallas_call | solution.py:540
Async XLA Ops:
  0.6 42.3 %copy-start = (bf16[512,256]{1,0:T(8,128)(2,1)S(1)}, bf16[512,256]{1,0:T(8,128)(2,1)}, u32[]{:S(2)}) copy-start(bf16[512,256]{1,0:T(8,128)(2,1)} %constant.5.clone.table_low_ref) | copy-start | bytes 786436
  0.6 42.3 %copy-start.1 = (bf16[512,256]{1,0:T(8,128)(2,1)S(1)}, bf16[512,256]{1,0:T(8,128)(2,1)}, u32[]{:S(2)}) copy-start(bf16[512,256]{1,0:T(8,128)(2,1)} %constant.4.clone.table_high_ref) | copy-start | bytes 786436
  0.7 42.3 %copy-start.2 = (f32[4,16]{1,0:T(4,128)S(1)}, f32[4,16]{1,0:T(4,128)}, u32[]{:S(2)}) copy-start(f32[4,16]{1,0:T(4,128)} %curves_ref.1) | copy-start | bytes 772
  0.7 42.3 %copy-start.3 = (f32[128]{0:T(128)S(1)}, f32[128]{0:T(128)}, u32[]{:S(2)}) copy-start(f32[128]{0:T(128)} %param.13) | copy-start | bytes 1540
  0.7 42.3 %copy-start.4 = (s32[32]{0:T(128)S(1)}, s32[32]{0:T(128)}, u32[]{:S(2)}) copy-start(s32[32]{0:T(128)} %param.17) | copy-start | bytes 388
  3.9 4.7 %collective-permute-start = (f32[80,128]{1,0:T(8,128)S(1)}, f32[80,128]{1,0:T(8,128)S(1)}, u32[]{:S(2)}, u32[]{:S(2)}) collective-permute-start(f32[80,128]{1,0:T(8,128)S(1)} %get-tuple-element.17), channel_id=1, source_target_pairs={{0,4},{4,0},{8,12},{12,8},{16,20},{20,16},{24,28},{28,24},{32,36},... | collective-permute-start | bytes 122888 | tf_op jit(solution)/shard_map/ppermute | solution.py:510
  5.4 5.3 %collective-permute-start.1 = (f32[80,128]{1,0:T(8,128)S(1)}, f32[80,128]{1,0:T(8,128)S(1)}, u32[]{:S(2)}, u32[]{:S(2)}) collective-permute-start(f32[80,128]{1,0:T(8,128)S(1)} %get-tuple-element.18), channel_id=1, source_target_pairs={{4,8},{8,4},{12,16},{16,12},{20,24},{24,20},{28,32},{32,28},{36,40... | collective-permute-start | bytes 122888 | tf_op jit(solution)/shard_map/ppermute | solution.py:511
  17.0 25.9 %collective-permute-start.2 = (f32[288,128]{1,0:T(8,128)S(1)}, f32[288,128]{1,0:T(8,128)S(1)}, u32[]{:S(2)}, u32[]{:S(2)}) collective-permute-start(f32[288,128]{1,0:T(8,128)S(1)} %get-tuple-element.23), channel_id=1, source_target_pairs={{0,1},{1,0},{2,3},{3,2},{4,5},{5,4},{6,7},{7,6},{8,9},{9,8},{10,11... | collective-permute-start | bytes 442376 | tf_op jit(solution)/shard_map/ppermute | solution.py:532
  18.8 24.1 %collective-permute-start.3 = (f32[288,128]{1,0:T(8,128)S(1)}, f32[288,128]{1,0:T(8,128)S(1)}, u32[]{:S(2)}, u32[]{:S(2)}) collective-permute-start(f32[288,128]{1,0:T(8,128)S(1)} %get-tuple-element.24), channel_id=1, source_target_pairs={{0,2},{1,3},{2,0},{3,1},{4,6},{5,7},{6,4},{7,5},{8,10},{9,11},{10,... | collective-permute-start | bytes 442376 | tf_op jit(solution)/shard_map/ppermute | solution.py:532
  22.1 20.8 %collective-permute-start.4 = (f32[288,128]{1,0:T(8,128)S(1)}, f32[288,128]{1,0:T(8,128)S(1)}, u32[]{:S(2)}, u32[]{:S(2)}) collective-permute-start(f32[288,128]{1,0:T(8,128)S(1)} %get-tuple-element.25), channel_id=1, source_target_pairs={{0,3},{1,2},{2,1},{3,0},{4,7},{5,6},{6,5},{7,4},{8,11},{9,10},{10,... | collective-permute-start | bytes 442376 | tf_op jit(solution)/shard_map/ppermute | solution.py:532

commit v6 on v5

--- a/solution.py
+++ b/solution.py
@@ -46,33 +46,37 @@
 def edges_kernel(
     load_ref, modulus_ref, mass_ref, stiffness_ref, template_ref, strain_map_ref,
     first_ref, second_ref, own_ref, lhs_ref, cols_ref, buffer_ref,
-    slots_ref, turned_ref, square_ref, small_ref, third_ref, copied,
+    slots_ref, turned_ref, square_ref, small_ref, third_ref, small_template_ref, small_stiff_ref, small_map_ref, copied,
 ):
     half, parts, chunks = 48, 64, 3
     per = half // chunks
-    length = per * parts
+    pieces = 3
+    piece = half * parts // pieces
     full = 2 * half
     comps = strain_map_ref.shape[0]
     copies = [
         pltpu.make_async_copy(
-            load_ref.at[pl.ds(i * length, length)], buffer_ref.at[pl.ds(i * length, length)],
+            load_ref.at[pl.ds(i * piece, piece)], buffer_ref.at[pl.ds(i * piece, piece)],
             copied.at[i],
         )
-        for i in range(chunks)
+        for i in range(pieces)
     ]
     smalls = [
-        pltpu.make_async_copy(source, target, copied.at[chunks + i])
+        pltpu.make_async_copy(source, target, copied.at[pieces + i])
         for i, (source, target) in enumerate((
             (modulus_ref, small_ref.at[0]), (mass_ref, small_ref.at[1]),
+            (template_ref, small_template_ref), (stiffness_ref, small_stiff_ref), (strain_map_ref, small_map_ref),
         ))
     ]
-    for copy in copies + smalls:
+    for copy in smalls[2:] + copies + smalls[:2]:
         copy.start()
     square_ref[...] = jnp.zeros(square_ref.shape, F32)
 
-    square_ref[:full, :full] = stiffness_ref[...]
-    square_ref[full : full + comps, :full] = strain_map_ref[...]
-    square_ref[full + 8 : full + 9, :full] = template_ref[...]
+    for copy in smalls[2:]:
+        copy.wait()
+    square_ref[:full, :full] = small_stiff_ref[...]
+    square_ref[full : full + comps, :full] = small_map_ref[...]
+    square_ref[full + 8 : full + 9, :full] = small_template_ref[...]
     stiff = square_ref[:full, :]
     same = lax.broadcasted_iota(jnp.int32, (full, LANES), 0) == lane_ids(full)
     kdiag = jnp.sum(jnp.where(same, stiff, 0.0), axis=1, keepdims=True)
@@ -101,7 +105,8 @@
 
     slot = lane_ids(parts) // SLOT
     for chunk in range(chunks):
-        copies[chunk].wait()
+        for copy in copies[chunk * pieces // chunks : (chunk + 1) * pieces // chunks]:
+            copy.wait()
         held = jnp.zeros((parts, LANES), F32)
         for i in range(per):
             start = (chunk * per + i) * parts
@@ -117,7 +122,7 @@
             else:
                 own_ref[half + at : half + at + per, :] = turned_ref[pl.ds(0, per, stride=SLOT), :]
                 third_ref[at : at + per, :] = turned_ref[pl.ds(1, per, stride=SLOT), :]
-    for copy in smalls:
+    for copy in smalls[:2]:
         copy.wait()
     own_ref[OWN_AT : OWN_AT + 1, :] = small_ref[0]
     own_ref[OWN_AT + 1 : OWN_AT + 2, :] = small_ref[1]
@@ -137,8 +142,79 @@
         ref[SENT_AT:, :] = own_ref[OWN_AT:, :]
 
 
+def shift_of(order, total):
+    return MASS_COEF * (order * (1.0 / total)) ** 2
+
+
+def columns_of(cols):
+    return [cols[:, i : i + 1] for i in range(4)]
+
+
+def diagonals(columns, mod, mass):
+    kd_top, kd_low, mt_top, mt_low = columns
+    return kd_top * mod[0] + kd_low * mod[1], mt_top * mass[0] + mt_low * mass[1]
+
+
+def products(lhs, *fields):
+    half = fields[0].shape[0]
+    split = [halves(field) for field in fields]
+    high = jnp.concatenate([h for h, _ in split], 1)
+    low = jnp.concatenate([l for _, l in split], 1)
+    gap = jnp.zeros((DEPTH - 3 * half, high.shape[1]), BF16)
+    result = jnp.dot(lhs, jnp.concatenate([high, low, gap, high], 0), preferred_element_type=F32)
+    cut = [half * i for i in range(5)] + [4 * half + 8, 4 * half + 16]
+    return [
+        [result[cut[i] : cut[i + 1], LANES * k : LANES * (k + 1)] for i in range(6)]
+        for k in range(len(fields))
+    ]
+
+
+def image_of(mod, z):
+    lanes = lane_ids()
+    own, prev = mod
+    up = jnp.where(lanes == 127, 0.0, own)
+    down = jnp.where(lanes == 0, 0.0, prev)
+    return own * z[0] + prev * z[1] + later(down * z[2]) + earlier(up * z[3])
+
+
+def strain_of(z):
+    return z[4] + jnp.where(lane_ids() == 127, 0.0, later(z[5]))
+
+
+def inner_kernel(
+    load_ref, own_ref, lhs_ref, cols_ref, image_ref, field_ref, inv_ref, strain_ref
+):
+    half, parts = 48, 64
+    freqs = parts // 2
+    first_order = (lax.axis_index("freq") * freqs + 1).astype(F32)
+    lanes = lane_ids()
+
+    def row(at):
+        own = own_ref[OWN_AT + at : OWN_AT + at + 1, :]
+        return own, jnp.where(lanes == 0, 0.0, earlier(own))
+
+    mod, mass = row(0), row(1)
+    stiff, weight = diagonals(columns_of(cols_ref[...]), mod, mass)
+    lhs = lhs_ref[:, :DEPTH]
+
+    def step(f, carry):
+        shift = shift_of(first_order + f.astype(F32), 4 * freqs)
+        inv = jnp.where(lanes == 0, 0.0, 1.0 / (stiff + shift * weight))
+        inv_ref[f] = inv
+        loads = [load_ref[pl.ds(2 * f + k, half, stride=parts), :] for k in range(2)]
+        for k, z in enumerate(products(lhs, *(inv * b for b in loads))):
+            field_ref[2 * f + k] = loads[k]
+            image_ref[2 * f + k] = image_of(mod, z)
+            start = pl.multiple_of((k * freqs + f) * 8, 8)
+            strain_ref[pl.ds(start, 8), :] = strain_of(z)
+        return carry
+
+    lax.fori_loop(0, freqs, step, 0, unroll=UNROLL)
+
+
 def main_kernel(
-    load_ref, own_ref, first_ref, second_ref, lhs_ref, cols_ref,
+    image_ref, load_ref, inner_inv_ref, inner_strain_ref,
+    own_ref, first_ref, second_ref, lhs_ref, cols_ref,
     out0_ref, out1_ref, out2_ref, out3_ref, dots_out_ref,
     strain_ref, field_ref, inv_ref, border_ref, dots_ref,
 ):
@@ -155,12 +231,7 @@
     lanes = lane_ids()
     even = lanes % 2 == 0
 
-    def shift_of(order):
-        return MASS_COEF * (order * (1.0 / (4 * freqs))) ** 2
-
-    cols = cols_ref[...]
-    kd_top, kd_low, mt_top, mt_low = (cols[:, i : i + 1] for i in range(4))
-
+    columns = columns_of(cols_ref[...])
     def rows_of(at):
         own = own_ref[OWN_AT + at : OWN_AT + at + 1, :]
         left, right = (r[SENT_AT + at : SENT_AT + at + 1] for r in (from_left, from_right))
@@ -184,32 +255,14 @@
     mod_main, mod_pairs = rows_of(0)
     mass_main, mass_pairs = rows_of(1)
 
-    def diagonals(mod, mass):
-        return kd_top * mod[0] + kd_low * mod[1], mt_top * mass[0] + mt_low * mass[1]
-
     lhs = lhs_ref[:, :DEPTH]
-    blank = jnp.zeros((DEPTH - 3 * half, 2 * LANES), BF16)
-
-    def products(*fields):
-        split = [halves(field) for field in fields]
-        high = jnp.concatenate([h for h, _ in split], 1)
-        low = jnp.concatenate([l for _, l in split], 1)
-        gap = blank[:, : high.shape[1]]
-        result = jnp.dot(
-            lhs, jnp.concatenate([high, low, gap, high], 0), preferred_element_type=F32
-        )
-        cut = [half * i for i in range(5)] + [4 * half + 8, 4 * half + 16]
-        return [
-            [result[cut[i] : cut[i + 1], LANES * k : LANES * (k + 1)] for i in range(6)]
-            for k in range(len(fields))
-        ]
 
     order = first_order + (lanes // 4).astype(F32)
     beyond = jnp.logical_and(even, is_last)
     inverses = []
     for i, (mod, mass) in enumerate(zip(mod_pairs, mass_pairs)):
-        stiff, weight = diagonals(mod, mass)
-        diag = stiff + shift_of(order) * weight
+        stiff, weight = diagonals(columns, mod, mass)
+        diag = stiff + shift_of(order, 4 * freqs) * weight
         good = diag > 0
         if i >= 2:
             good = jnp.logical_and(good, jnp.logical_not(beyond))
@@ -230,11 +283,18 @@
         z = {}
         for i in range(first, len(rims), 2):
             names = list(range(i, min(i + 2, len(rims))))
-            for name, value in zip(names, products(*(rims[name] for name in names))):
+            for name, value in zip(names, products(lhs, *(rims[name] for name in names))):
                 z[name] = value
         at_edge = mod_pairs[1]
         outer = z[2]
-        if stage < 2:
+        if stage == 0:
+            node = z[1]
+            own_part = at_edge[0] * node[0] + at_edge[1] * (node[1] + outer[3])
+            border = jnp.where(even, at_edge[0] * outer[2], own_part)
+            border_ref[3, :half, :] = at_edge[0] * node[3]
+            border_ref[4, :half, :] = inverses[1]
+            tail = outer[5]
+        elif stage == 1:
             border = jnp.where(even, at_edge[0] * outer[2], at_edge[1] * outer[3])
             tail = outer[5]
         else:
@@ -243,7 +303,7 @@
             row = lax.broadcasted_iota(jnp.int32, (8, LANES), 0)
             tail = jnp.where(row == 6, energy, outer[5])
         border_ref[stage, :half, :] = border
-        border_ref[stage, half:, :] = jnp.where(even, tail, 0.0)
+        border_ref[stage, half:, :] = jnp.where(even, tail, z[1][4] if stage == 0 else 0.0)
         nexts = [None] * len(rims)
         for i in range(first + 1, len(rims) - 1):
             above = jnp.where(even, z[i + 1][2], z[i - 1][2])
@@ -252,9 +312,7 @@
             nexts[i] = -inverses[i] * (top * (z[i][0] + above) + low * (z[i][1] + below))
         return nexts[: len(rims) - 1]
 
-    stiff_main, mass_diag_main = diagonals(mod_main, mass_main)
     mod_own, mod_prev = mod_main
-    mod_sent_up = jnp.where(lanes == 127, 0.0, mod_own)
     mod_sent_down = jnp.where(lanes == 0, 0.0, mod_prev)
     rim = jnp.logical_or(lanes == 0, lanes == 127)
 
@@ -263,9 +321,6 @@
         moved = jnp.where(rim, moved, 0.0)
         return moved[:half], moved[half:]
 
-    def strain_of(top, low, added):
-        return top + jnp.where(lanes == 127, 0.0, later(low)) + added
-
     def put_dot(which, f, pairs):
         total = sum(a * b for a, b in pairs)
         dots_ref[pl.ds(which * freqs + f, 1), :] = jnp.sum(total, axis=0, keepdims=True)
@@ -274,25 +329,30 @@
         start = ((stage * 2 + k) * freqs + f) * 8
         strain_ref[pl.ds(pl.multiple_of(start, 8), 8), :] = value
 
+    def moved_to(which, lane, place, f, k):
+        shift = (lane + 2 * LANES - 1 - 2 * (2 * f + k)) % LANES
+        return jnp.where(lanes == lane, pltpu.roll(border_ref[which, :half, :], shift, 1), place)
+
     def images(f, stage, fields):
         result = []
-        for k, z in enumerate(products(*fields)):
-            z11, z22, z12, z21, s_top, s_low = z
+        for k, z in enumerate(products(lhs, *fields)):
             added, added_strain = borders(stage, f, k)
-            image = (
-                mod_own * z11 + mod_prev * z22 + later(mod_sent_down * z12)
-                + earlier(mod_sent_up * z21) + added
-            )
-            put_strain(stage, f, k, strain_of(s_top, s_low, added_strain))
-            result.append(-image)
+            put_strain(stage, f, k, strain_of(z) + added_strain)
+            result.append(-(image_of(mod_main, z) + added))
         return result
 
     def first(f, carry):
-        inv = 1.0 / (stiff_main + shift_of(first_order + f.astype(F32)) * mass_diag_main)
+        inv = moved_to(4, 0, inner_inv_ref[f], f, 0)
         inv_ref[f] = inv
-        loads = [load_ref[pl.ds(2 * f + k, half, stride=parts), :] for k in range(2)]
+        loads = [load_ref[2 * f + k] for k in range(2)]
         fields = [inv * b for b in loads]
-        image = images(f, 0, fields)
+        image = []
+        for k in range(2):
+            added, added_strain = borders(0, f, k)
+            added = added + moved_to(3, 1, 0.0, f, k)
+            image.append(-(image_ref[2 * f + k] + added))
+            start = pl.multiple_of((k * freqs + f) * 8, 8)
+            put_strain(0, f, k, inner_strain_ref[pl.ds(start, 8), :] + added_strain)
         nexts = [inv * t for t in image]
         for k in range(2):
             field_ref[2 * f + k] = nexts[k]
@@ -315,12 +375,12 @@
     def third(f, carry):
         fields = [field_ref[2 * f + k] for k in range(2)]
         total, extra = 0.0, 0.0
-        for k, z in enumerate(products(*fields)):
-            z11, z22, z12, _, s_top, s_low = z
+        for k, z in enumerate(products(lhs, *fields)):
+            z11, z22, z12 = z[:3]
             added, added_strain = borders(2, f, k)
             twice = 2.0 * (later(mod_sent_down * z12) + added)
             total = total + fields[k] * (mod_own * z11 + mod_sent_down * z22 + twice)
-            strain = strain_of(s_top, s_low, added_strain)
+            strain = strain_of(z) + added_strain
             put_strain(2, f, k, strain)
             extra = extra + strain[6:7]
         dots_ref[pl.ds(5 * freqs + f, 1), :] = -(jnp.sum(total, axis=0, keepdims=True) + extra)
@@ -495,7 +555,7 @@
             pltpu.VMEM((half, LANES), F32),
             pltpu.VMEM((half * parts, LANES), F32),
         ],
-        in_specs=[HBM] * 3 + [VMEM] * 3,
+        in_specs=[HBM] * 6,
         out_specs=[VMEM] * 6,
         scratch_shapes=[
             pltpu.VMEM((LANES, LANES), F32),
@@ -503,7 +563,10 @@
             pltpu.VMEM((LANES, LANES), F32),
             pltpu.VMEM((2, 1, LANES), F32),
             pltpu.VMEM((half, LANES), F32),
-            pltpu.SemaphoreType.DMA((5,)),
+            pltpu.VMEM((1, 2 * half), F32),
+            pltpu.VMEM((2 * half, 2 * half), F32),
+            pltpu.VMEM(strain_map.shape, F32),
+            pltpu.SemaphoreType.DMA((3+6,)),
         ],
         name="edges",
     )(rows, modulus_row, mass_row, stiffness, mass_template.reshape(1, -1), strain_map)
@@ -511,23 +574,36 @@
     met_second = lax.ppermute(
         second, "elem", [(i, i + 1 if i % 2 else i - 1) for i in range(1, slabs - 1)]
     )
+    inner = pl.pallas_call(
+        inner_kernel,
+        out_shape=[
+            pltpu.VMEM((parts, half, LANES), F32),
+            pltpu.VMEM((parts, half, LANES), F32),
+            pltpu.VMEM((freq_dev, half, LANES), F32),
+            pltpu.VMEM((parts * 8, LANES), F32),
+        ],
+        in_specs=[VMEM] * 4,
+        out_specs=[VMEM] * 4,
+        compiler_params=pltpu.CompilerParams(vmem_limit_bytes=32 * 1024 * 1024),
+        name="inner",
+    )(rows, own, lhs, cols)
     packed = 9 * freq_dev
     outs = pl.pallas_call(
         main_kernel,
         out_shape=[jax.ShapeDtypeStruct((packed, LANES), F32)] * 4
         + [jax.ShapeDtypeStruct((2 * slabs * groups, LANES), F32)],
-        in_specs=[VMEM] * 6,
+        in_specs=[VMEM] * 9,
         out_specs=[VMEM] * 5,
         scratch_shapes=[
             pltpu.VMEM((3 * parts * 8, LANES), F32),
             pltpu.VMEM((parts, half, LANES), F32),
             pltpu.VMEM((freq_dev, half, LANES), F32),
-            pltpu.VMEM((3, half + 8, LANES), F32),
+            pltpu.VMEM((5, half + 8, LANES), F32),
             pltpu.VMEM((256, LANES), F32),
         ],
         compiler_params=pltpu.CompilerParams(vmem_limit_bytes=32 * 1024 * 1024),
         name="krylov",
-    )(rows, own, met_first, met_second, lhs, cols)
+    )(*inner, own, met_first, met_second, lhs, cols)
     received = [outs[0]] + [
         lax.ppermute(outs[step], "freq", [(i, i ^ step) for i in range(groups)])
         for step in range(1, groups)

time: 45.2 us -> 43.1 us (0.954)
  waiting for transfers between devices: 2.11 us -> 0.01 us
    pallas_call x0 -> x1, Pallas kernels: none -> 2.11 us  [per_device(): pl.pallas_call(inner_kernel, out_shape=[pltpu.VMEM((parts, half, LANES),...]
    ppermute x1, waiting for transfers between devices: 2.1 us -> 0.01 us  [per_device(): lax.ppermute(second, 'elem', [(i, i + 1 if i % 2 else i - 1) for i in ran...]
    pallas_call x1, Pallas kernels: 6.26 us -> 4.99 us  [per_device(): pl.pallas_call(main_kernel, out_shape=[jax.ShapeDtypeStruct((packed, LANE...]
    pallas_call x1, Pallas kernels: 3.19 us -> 2.42 us  [per_device(): pl.pallas_call(edges_kernel, out_shape=[pltpu.VMEM((SENT_ROWS, LANES), F3...]
  transfers between devices with their start and end apart: 5 -> 5, of which waited for: 1 -> 0; matrix products, arithmetic and copies ran while one was open for 0% -> 0% of each run, Pallas kernels for 0% -> 5%
where the time goes in v6:
time: 43.1 us; the launch traced here: 42.9 us
  blocking collectives  20.8 us (48%)
  Pallas kernels  11.6 us (27%)
  starting transfers between devices  9.72 us (23%)
  between operations  0.76 us (2%)
    all_to_all x1, blocking collectives, per_device(): lax.all_to_all(outs[4].reshape(slabs * groups, 2, LANES), ('elem', 'freq'...  20.8 us
    ppermute x3, starting transfers between devices, per_device(): lax.ppermute(outs[step], 'freq', [(i, i ^ step) for i in range(groups)])  5.04 us
    pallas_call x1, Pallas kernels, per_device(): pl.pallas_call(main_kernel, out_shape=[jax.ShapeDtypeStruct((packed, LANE...  4.99 us
    ppermute x1, starting transfers between devices, per_device(): lax.ppermute(second, 'elem', [(i, i + 1 if i % 2 else i - 1) for i in ran...  3.19 us
    pallas_call x1, Pallas kernels, per_device(): pl.pallas_call(edges_kernel, out_shape=[pltpu.VMEM((SENT_ROWS, LANES), F3...  2.42 us
    pallas_call x1, Pallas kernels, per_device(): pl.pallas_call(inner_kernel, out_shape=[pltpu.VMEM((parts, half, LANES),...  2.11 us
    pallas_call x1, Pallas kernels, per_device(): pl.pallas_call(final_kernel, out_shape=[jax.ShapeDtypeStruct((1, quarter)...  2.06 us
    ppermute x1, starting transfers between devices, per_device(): met_first = lax.ppermute(first, 'elem', [(i, i ^ 1) for i in range(slabs)])  1.5 us
  transfers between devices with their start and end apart: 5, of which 0 were waited for; matrix products, arithmetic and copies ran while one was open for 0% of the time, Pallas kernels for 5%

profile of v6, /device:TPU:1, one launch (start us, length us, event | category | flops | bytes accessed | tf_op | source)
XLA Modules:
  0.0 42.9 jit_solution(6546874197862047478)
XLA Ops:
  0.6 2.4 %edges.1 = (f32[80,128]{1,0:T(8,128)S(1)}, f32[80,128]{1,0:T(8,128)S(1)}, f32[104,128]{1,0:T(8,128)S(1)}, bf16[208,256]{1,0:T(8,128)(2,1)S(1)}, f32[48,128]{1,0:T(8,128)S(1)}, /*index=5*/f32[3072,128]{1,0:T(8,128)S(1)}) custom-call(f32[3072,128]{1,0:T(8,128)} %bitcast.14, f32[1,128]{1,0:T(1,128)} %bitcast.11, f32[1,128]{1,0:T(1,128)} %bitcast.15, ...), custom_call_target="tpu_custom_call" | custom-call | tf_op jit(solution)/shard_map/edges/pallas_call | solution.py:548
  3.1 1.5 %collective-permute-start = (f32[80,128]{1,0:T(8,128)S(1)}, f32[80,128]{1,0:T(8,128)S(1)}, u32[]{:S(2)}, u32[]{:S(2)}) collective-permute-start(f32[80,128]{1,0:T(8,128)S(1)} %get-tuple-element.27), channel_id=1, source_target_pairs={{0,4},{4,0},{8,12},{12,8},{16,20},{20,16},{24,28},{28,24},{32,36},... | collective-permute-start | bytes 122888 | tf_op jit(solution)/shard_map/ppermute | solution.py:573
  4.6 3.2 %collective-permute-start.1 = (f32[80,128]{1,0:T(8,128)S(1)}, f32[80,128]{1,0:T(8,128)S(1)}, u32[]{:S(2)}, u32[]{:S(2)}) collective-permute-start(f32[80,128]{1,0:T(8,128)S(1)} %get-tuple-element.28), channel_id=1, source_target_pairs={{4,8},{8,4},{12,16},{16,12},{20,24},{24,20},{28,32},{32,28},{36,40... | collective-permute-start | bytes 122888 | tf_op jit(solution)/shard_map/ppermute | solution.py:574
  7.8 2.1 %inner.1 = (f32[64,48,128]{2,1,0:T(8,128)S(1)}, f32[64,48,128]{2,1,0:T(8,128)S(1)}, f32[32,48,128]{2,1,0:T(8,128)S(1)}, f32[512,128]{1,0:T(8,128)S(1)}) custom-call(f32[3072,128]{1,0:T(8,128)S(1)} %get-tuple-element.19.load_ref, f32[104,128]{1,0:T(8,128)S(1)} %get-tuple-element.20.own_ref, bf16[208,256]{1,0:T(8,128)(2,1)S(1)} %get-tuple-element.21.lhs_ref, ...), custom_call_target="tpu_custom_call" | custom-call | tf_op jit(solution)/shard_map/inner/pallas_call | solution.py:577
  9.9 0.0 collective-permute-done.first_ref
  9.9 0.0 collective-permute-done.1.second_ref
  9.9 0.0 copy-start
  9.9 0.0 copy-start.1
  9.9 0.0 copy-start.2
  9.9 0.0 copy-start.3
  9.9 0.0 copy-start.4
  10.0 5.0 %krylov.1 = (f32[288,128]{1,0:T(8,128)S(1)}, f32[288,128]{1,0:T(8,128)S(1)}, f32[288,128]{1,0:T(8,128)S(1)}, f32[288,128]{1,0:T(8,128)S(1)}, f32[256,128]{1,0:T(8,128)S(1)}) custom-call(f32[64,48,128]{2,1,0:T(8,128)S(1)} %get-tuple-element.23.image_ref, f32[64,48,128]{2,1,0:T(8,128)S(1)} %get-tuple-element.24.load_ref, ...), custom_call_target="tpu_custom_call" | custom-call | tf_op jit(solution)/shard_map/krylov/pallas_call | solution.py:591
  15.0 1.7 %collective-permute-start.2 = (f32[288,128]{1,0:T(8,128)S(1)}, f32[288,128]{1,0:T(8,128)S(1)}, u32[]{:S(2)}, u32[]{:S(2)}) collective-permute-start(f32[288,128]{1,0:T(8,128)S(1)} %get-tuple-element.31), channel_id=1, source_target_pairs={{0,1},{1,0},{2,3},{3,2},{4,5},{5,4},{6,7},{7,6},{8,9},{9,8},{10,11... | collective-permute-start | bytes 442376 | tf_op jit(solution)/shard_map/ppermute | solution.py:608
  16.7 3.3 %collective-permute-start.3 = (f32[288,128]{1,0:T(8,128)S(1)}, f32[288,128]{1,0:T(8,128)S(1)}, u32[]{:S(2)}, u32[]{:S(2)}) collective-permute-start(f32[288,128]{1,0:T(8,128)S(1)} %get-tuple-element.32), channel_id=1, source_target_pairs={{0,2},{1,3},{2,0},{3,1},{4,6},{5,7},{6,4},{7,5},{8,10},{9,11},{10,... | collective-permute-start | bytes 442376 | tf_op jit(solution)/shard_map/ppermute | solution.py:608
  20.0 0.0 collective-permute-start.4
  20.0 20.8 %all_to_all.5 = f32[128,2,128]{2,1,0:T(2,128)S(1)} all-to-all(f32[128,2,128]{2,1,0:T(2,128)S(1)} %bitcast.10), channel_id=1, replica_groups=mesh['elem'=32,'freq'=4] {'elem','freq'}, dimensions={0} | all-to-all | bytes 262144 | tf_op jit(solution)/shard_map/all_to_all | solution.py:611
  40.8 0.0 collective-permute-done.2.part1_ref
  40.8 0.0 collective-permute-done.3.part2_ref
  40.8 0.0 collective-permute-done.4.part3_ref
  40.8 0.0 copy-done
  40.8 0.0 copy-done.1
  40.8 0.0 copy-done.2
  40.8 0.0 copy-done.3
  40.9 2.1 %response.1 = (f32[1,32]{1,0:T(1,128)}, f32[1,32]{1,0:T(1,128)}) custom-call(f32[4,16]{1,0:T(4,128)S(1)} %copy-done.2, f32[256,128]{1,0:T(8,128)S(1)} %bitcast.9, f32[288,128]{1,0:T(8,128)S(1)} %get-tuple-element.30.part0_ref, f32[288,128]{1,0:T(8,128)S(1)} %collective-permute-done.2.part1_ref, f32[288,128]{1,0:T(8,128)S(1)} %collective-permute-done.3.part2_ref, ...), custom_call_target="tpu_custom_call" | custom-call | tf_op jit(solution)/shard_map/response/pallas_call | solution.py:616
  (1 shorter events, 0.0 us)
Async XLA Ops:
  3.1 6.8 %collective-permute-start = (f32[80,128]{1,0:T(8,128)S(1)}, f32[80,128]{1,0:T(8,128)S(1)}, u32[]{:S(2)}, u32[]{:S(2)}) collective-permute-start(f32[80,128]{1,0:T(8,128)S(1)} %get-tuple-element.27), channel_id=1, source_target_pairs={{0,4},{4,0},{8,12},{12,8},{16,20},{20,16},{24,28},{28,24},{32,36},... | collective-permute-start | bytes 122888 | tf_op jit(solution)/shard_map/ppermute | solution.py:573
  4.6 5.3 %collective-permute-start.1 = (f32[80,128]{1,0:T(8,128)S(1)}, f32[80,128]{1,0:T(8,128)S(1)}, u32[]{:S(2)}, u32[]{:S(2)}) collective-permute-start(f32[80,128]{1,0:T(8,128)S(1)} %get-tuple-element.28), channel_id=1, source_target_pairs={{4,8},{8,4},{12,16},{16,12},{20,24},{24,20},{28,32},{32,28},{36,40... | collective-permute-start | bytes 122888 | tf_op jit(solution)/shard_map/ppermute | solution.py:574
  9.9 30.9 %copy-start = (bf16[512,256]{1,0:T(8,128)(2,1)S(1)}, bf16[512,256]{1,0:T(8,128)(2,1)}, u32[]{:S(2)}) copy-start(bf16[512,256]{1,0:T(8,128)(2,1)} %constant.5.clone.table_low_ref) | copy-start | bytes 786436
  9.9 30.9 %copy-start.1 = (bf16[512,256]{1,0:T(8,128)(2,1)S(1)}, bf16[512,256]{1,0:T(8,128)(2,1)}, u32[]{:S(2)}) copy-start(bf16[512,256]{1,0:T(8,128)(2,1)} %constant.4.clone.table_high_ref) | copy-start | bytes 786436
  9.9 30.9 %copy-start.2 = (f32[4,16]{1,0:T(4,128)S(1)}, f32[4,16]{1,0:T(4,128)}, u32[]{:S(2)}) copy-start(f32[4,16]{1,0:T(4,128)} %curves_ref.1) | copy-start | bytes 772
  9.9 30.9 %copy-start.3 = (f32[128]{0:T(128)S(1)}, f32[128]{0:T(128)}, u32[]{:S(2)}) copy-start(f32[128]{0:T(128)} %param.13) | copy-start | bytes 1540
  9.9 30.9 %copy-start.4 = (s32[32]{0:T(128)S(1)}, s32[32]{0:T(128)}, u32[]{:S(2)}) copy-start(s32[32]{0:T(128)} %param.17) | copy-start | bytes 388
  15.0 25.9 %collective-permute-start.2 = (f32[288,128]{1,0:T(8,128)S(1)}, f32[288,128]{1,0:T(8,128)S(1)}, u32[]{:S(2)}, u32[]{:S(2)}) collective-permute-start(f32[288,128]{1,0:T(8,128)S(1)} %get-tuple-element.31), channel_id=1, source_target_pairs={{0,1},{1,0},{2,3},{3,2},{4,5},{5,4},{6,7},{7,6},{8,9},{9,8},{10,11... | collective-permute-start | bytes 442376 | tf_op jit(solution)/shard_map/ppermute | solution.py:608
  16.7 24.1 %collective-permute-start.3 = (f32[288,128]{1,0:T(8,128)S(1)}, f32[288,128]{1,0:T(8,128)S(1)}, u32[]{:S(2)}, u32[]{:S(2)}) collective-permute-start(f32[288,128]{1,0:T(8,128)S(1)} %get-tuple-element.32), channel_id=1, source_target_pairs={{0,2},{1,3},{2,0},{3,1},{4,6},{5,7},{6,4},{7,5},{8,10},{9,11},{10,... | collective-permute-start | bytes 442376 | tf_op jit(solution)/shard_map/ppermute | solution.py:608
  20.0 20.8 %collective-permute-start.4 = (f32[288,128]{1,0:T(8,128)S(1)}, f32[288,128]{1,0:T(8,128)S(1)}, u32[]{:S(2)}, u32[]{:S(2)}) collective-permute-start(f32[288,128]{1,0:T(8,128)S(1)} %get-tuple-element.33), channel_id=1, source_target_pairs={{0,3},{1,2},{2,1},{3,0},{4,7},{5,6},{6,5},{7,4},{8,11},{9,10},{10,... | collective-permute-start | bytes 442376 | tf_op jit(solution)/shard_map/ppermute | solution.py:608

commit v7 on v6

--- a/solution.py
+++ b/solution.py
@@ -16,6 +16,7 @@
 SLOT = 8
 DEPTH = 176
 UNROLL = 32
+STEPS = (0, 1, 3, 2)
 DOTS = 6
 F32 = jnp.float32
 BF16 = jnp.bfloat16
@@ -93,7 +94,7 @@
     moved = pltpu.roll(off, LANES - half, 1)
     moved_rows = pltpu.roll(strain_rows, LANES - half, 1)
     stacked = jnp.concatenate(
-        [off[:half], moved[half:], moved[:half], off[half:], strain_rows, moved_rows], 0
+        [off[:half], moved[half:], moved[:half], strain_rows, moved_rows, off[half:]], 0
     )
     rows = stacked.shape[0]
     lane = lane_ids(rows)
@@ -162,9 +163,9 @@
     low = jnp.concatenate([l for _, l in split], 1)
     gap = jnp.zeros((DEPTH - 3 * half, high.shape[1]), BF16)
     result = jnp.dot(lhs, jnp.concatenate([high, low, gap, high], 0), preferred_element_type=F32)
-    cut = [half * i for i in range(5)] + [4 * half + 8, 4 * half + 16]
+    cut = [0, half, 2 * half, 3 * half, 3 * half + 8, 3 * half + 16, lhs.shape[0]]
     return [
-        [result[cut[i] : cut[i + 1], LANES * k : LANES * (k + 1)] for i in range(6)]
+        [result[cut[i] : cut[i + 1], LANES * k : LANES * (k + 1)] for i in (0, 1, 2, 5, 3, 4)]
         for k in range(len(fields))
     ]
 
@@ -214,7 +215,7 @@
 
 def main_kernel(
     image_ref, load_ref, inner_inv_ref, inner_strain_ref,
-    own_ref, first_ref, second_ref, lhs_ref, cols_ref,
+    own_ref, second_ref, first_ref, lhs_ref, cols_ref,
     out0_ref, out1_ref, out2_ref, out3_ref, dots_out_ref,
     strain_ref, field_ref, inv_ref, border_ref, dots_ref,
 ):
@@ -375,7 +376,7 @@
     def third(f, carry):
         fields = [field_ref[2 * f + k] for k in range(2)]
         total, extra = 0.0, 0.0
-        for k, z in enumerate(products(lhs, *fields)):
+        for k, z in enumerate(products(lhs[: 3 * half + 16], *fields)):
             z11, z22, z12 = z[:3]
             added, added_strain = borders(2, f, k)
             twice = 2.0 * (later(mod_sent_down * z12) + added)
@@ -400,7 +401,7 @@
             (stage * parts + k * freqs, [(k, c) for c in range(4)]) for k in range(2)
         ] + [(3 * parts + stage * freqs, [(0, 4), (0, 5), (1, 4), (1, 5)])]
         for step in range(4):
-            dest = lax.bitwise_xor(freq_group, step)
+            dest = lax.bitwise_xor(freq_group, STEPS[step])
             for row, names in places:
                 held = None
                 for i, name in enumerate(names):
@@ -484,7 +485,7 @@
     coefs = coefficients(h)
     lanes = lane_ids(freqs)
     for step, part_ref in enumerate((part0_ref, part1_ref, part2_ref, part3_ref)):
-        source = lax.bitwise_xor(freq_group, step)
+        source = lax.bitwise_xor(freq_group, STEPS[step])
         weights = [
             jnp.sum(jnp.where(lanes == 2 * source, c, 0.0), axis=1, keepdims=True) for c in coefs
         ]
@@ -603,9 +604,9 @@
         ],
         compiler_params=pltpu.CompilerParams(vmem_limit_bytes=32 * 1024 * 1024),
         name="krylov",
-    )(*inner, own, met_first, met_second, lhs, cols)
+    )(*inner, own, met_second, met_first, lhs, cols)
     received = [outs[0]] + [
-        lax.ppermute(outs[step], "freq", [(i, i ^ step) for i in range(groups)])
+        lax.ppermute(outs[step], "freq", [(i, i ^ STEPS[step]) for i in range(groups)])
         for step in range(1, groups)
     ]
     dots = lax.all_to_all(

time: 43.1 us -> 41.7 us (0.968)
  blocking collectives: 20.8 us -> 19.5 us
    ppermute x1, starting transfers between devices: 1.5 us -> 0.09 us  [per_device(): met_first = lax.ppermute(first, 'elem', [(i, i ^ 1) for i in range(slabs)])]
    ppermute x1, starting transfers between devices: 3.19 us -> 4.59 us  [per_device(): lax.ppermute(second, 'elem', [(i, i + 1 if i % 2 else i - 1) for i in ran...]
    all_to_all x1, blocking collectives: 20.8 us -> 19.5 us  [per_device(): lax.all_to_all(outs[4].reshape(slabs * groups, 2, LANES), ('elem', 'freq'...]
where the time goes in v7:
time: 41.7 us; the launch traced here: 41.5 us
  blocking collectives  19.5 us (47%)
  Pallas kernels  11.5 us (28%)
  starting transfers between devices  9.72 us (23%)
  between operations  0.77 us (2%)
    all_to_all x1, blocking collectives, per_device(): lax.all_to_all(outs[4].reshape(slabs * groups, 2, LANES), ('elem', 'freq'...  19.5 us
    ppermute x3, starting transfers between devices, per_device(): lax.ppermute(outs[step], 'freq', [(i, i ^ STEPS[step]) for i in range(gro...  5.04 us
    pallas_call x1, Pallas kernels, per_device(): pl.pallas_call(main_kernel, out_shape=[jax.ShapeDtypeStruct((packed, LANE...  4.93 us
    ppermute x1, starting transfers between devices, per_device(): lax.ppermute(second, 'elem', [(i, i + 1 if i % 2 else i - 1) for i in ran...  4.59 us
    pallas_call x1, Pallas kernels, per_device(): pl.pallas_call(edges_kernel, out_shape=[pltpu.VMEM((SENT_ROWS, LANES), F3...  2.42 us
    pallas_call x1, Pallas kernels, per_device(): pl.pallas_call(inner_kernel, out_shape=[pltpu.VMEM((parts, half, LANES),...  2.12 us
    pallas_call x1, Pallas kernels, per_device(): pl.pallas_call(final_kernel, out_shape=[jax.ShapeDtypeStruct((1, quarter)...  2.06 us
  transfers between devices with their start and end apart: 5, of which 0 were waited for; matrix products, arithmetic and copies ran while one was open for 0% of the time, Pallas kernels for 5%

profile of v7, /device:TPU:1, one launch (start us, length us, event | category | flops | bytes accessed | tf_op | source)
XLA Modules:
  0.0 41.5 jit_solution(11241247223966017086)
XLA Ops:
  0.6 2.4 %edges.1 = (f32[80,128]{1,0:T(8,128)S(1)}, f32[80,128]{1,0:T(8,128)S(1)}, f32[104,128]{1,0:T(8,128)S(1)}, bf16[208,256]{1,0:T(8,128)(2,1)S(1)}, f32[48,128]{1,0:T(8,128)S(1)}, /*index=5*/f32[3072,128]{1,0:T(8,128)S(1)}) custom-call(f32[3072,128]{1,0:T(8,128)} %bitcast.14, f32[1,128]{1,0:T(1,128)} %bitcast.11, f32[1,128]{1,0:T(1,128)} %bitcast.15, ...), custom_call_target="tpu_custom_call" | custom-call | tf_op jit(solution)/shard_map/edges/pallas_call | solution.py:549
  3.1 4.6 %collective-permute-start = (f32[80,128]{1,0:T(8,128)S(1)}, f32[80,128]{1,0:T(8,128)S(1)}, u32[]{:S(2)}, u32[]{:S(2)}) collective-permute-start(f32[80,128]{1,0:T(8,128)S(1)} %get-tuple-element.27), channel_id=1, source_target_pairs={{4,8},{8,4},{12,16},{16,12},{20,24},{24,20},{28,32},{32,28},{36,40... | collective-permute-start | bytes 122888 | tf_op jit(solution)/shard_map/ppermute | solution.py:575
  7.7 0.1 collective-permute-start.1
  7.8 2.1 %inner.1 = (f32[64,48,128]{2,1,0:T(8,128)S(1)}, f32[64,48,128]{2,1,0:T(8,128)S(1)}, f32[32,48,128]{2,1,0:T(8,128)S(1)}, f32[512,128]{1,0:T(8,128)S(1)}) custom-call(f32[3072,128]{1,0:T(8,128)S(1)} %get-tuple-element.19.load_ref, f32[104,128]{1,0:T(8,128)S(1)} %get-tuple-element.20.own_ref, bf16[208,256]{1,0:T(8,128)(2,1)S(1)} %get-tuple-element.21.lhs_ref, ...), custom_call_target="tpu_custom_call" | custom-call | tf_op jit(solution)/shard_map/inner/pallas_call | solution.py:578
  9.9 0.0 collective-permute-done.second_ref
  9.9 0.0 collective-permute-done.1.first_ref
  9.9 0.0 copy-start
  9.9 0.0 copy-start.1
  9.9 0.0 copy-start.2
  9.9 0.0 copy-start.3
  9.9 0.0 copy-start.4
  10.0 4.9 %krylov.1 = (f32[288,128]{1,0:T(8,128)S(1)}, f32[288,128]{1,0:T(8,128)S(1)}, f32[288,128]{1,0:T(8,128)S(1)}, f32[288,128]{1,0:T(8,128)S(1)}, f32[256,128]{1,0:T(8,128)S(1)}) custom-call(f32[64,48,128]{2,1,0:T(8,128)S(1)} %get-tuple-element.23.image_ref, f32[64,48,128]{2,1,0:T(8,128)S(1)} %get-tuple-element.24.load_ref, ...), custom_call_target="tpu_custom_call" | custom-call | tf_op jit(solution)/shard_map/krylov/pallas_call | solution.py:592
  14.9 1.7 %collective-permute-start.2 = (f32[288,128]{1,0:T(8,128)S(1)}, f32[288,128]{1,0:T(8,128)S(1)}, u32[]{:S(2)}, u32[]{:S(2)}) collective-permute-start(f32[288,128]{1,0:T(8,128)S(1)} %get-tuple-element.31), channel_id=1, source_target_pairs={{0,1},{1,0},{2,3},{3,2},{4,5},{5,4},{6,7},{7,6},{8,9},{9,8},{10,11... | collective-permute-start | bytes 442376 | tf_op jit(solution)/shard_map/ppermute | solution.py:609
  16.6 2.2 %collective-permute-start.3 = (f32[288,128]{1,0:T(8,128)S(1)}, f32[288,128]{1,0:T(8,128)S(1)}, u32[]{:S(2)}, u32[]{:S(2)}) collective-permute-start(f32[288,128]{1,0:T(8,128)S(1)} %get-tuple-element.32), channel_id=1, source_target_pairs={{0,3},{1,2},{2,1},{3,0},{4,7},{5,6},{6,5},{7,4},{8,11},{9,10},{10,... | collective-permute-start | bytes 442376 | tf_op jit(solution)/shard_map/ppermute | solution.py:609
  18.9 1.1 %collective-permute-start.4 = (f32[288,128]{1,0:T(8,128)S(1)}, f32[288,128]{1,0:T(8,128)S(1)}, u32[]{:S(2)}, u32[]{:S(2)}) collective-permute-start(f32[288,128]{1,0:T(8,128)S(1)} %get-tuple-element.33), channel_id=1, source_target_pairs={{0,2},{1,3},{2,0},{3,1},{4,6},{5,7},{6,4},{7,5},{8,10},{9,11},{10,... | collective-permute-start | bytes 442376 | tf_op jit(solution)/shard_map/ppermute | solution.py:609
  19.9 19.5 %all_to_all.5 = f32[128,2,128]{2,1,0:T(2,128)S(1)} all-to-all(f32[128,2,128]{2,1,0:T(2,128)S(1)} %bitcast.10), channel_id=1, replica_groups=mesh['elem'=32,'freq'=4] {'elem','freq'}, dimensions={0} | all-to-all | bytes 262144 | tf_op jit(solution)/shard_map/all_to_all | solution.py:612
  39.4 0.0 collective-permute-done.2.part1_ref
  39.4 0.0 collective-permute-done.3.part2_ref
  39.4 0.0 collective-permute-done.4.part3_ref
  39.4 0.0 copy-done
  39.4 0.0 copy-done.1
  39.4 0.0 copy-done.2
  39.5 0.0 copy-done.3
  39.5 2.1 %response.1 = (f32[1,32]{1,0:T(1,128)}, f32[1,32]{1,0:T(1,128)}) custom-call(f32[4,16]{1,0:T(4,128)S(1)} %copy-done.2, f32[256,128]{1,0:T(8,128)S(1)} %bitcast.9, f32[288,128]{1,0:T(8,128)S(1)} %get-tuple-element.30.part0_ref, f32[288,128]{1,0:T(8,128)S(1)} %collective-permute-done.2.part1_ref, f32[288,128]{1,0:T(8,128)S(1)} %collective-permute-done.3.part2_ref, ...), custom_call_target="tpu_custom_call" | custom-call | tf_op jit(solution)/shard_map/response/pallas_call | solution.py:617
  (1 shorter events, 0.0 us)
Async XLA Ops:
  3.1 6.8 %collective-permute-start = (f32[80,128]{1,0:T(8,128)S(1)}, f32[80,128]{1,0:T(8,128)S(1)}, u32[]{:S(2)}, u32[]{:S(2)}) collective-permute-start(f32[80,128]{1,0:T(8,128)S(1)} %get-tuple-element.27), channel_id=1, source_target_pairs={{4,8},{8,4},{12,16},{16,12},{20,24},{24,20},{28,32},{32,28},{36,40... | collective-permute-start | bytes 122888 | tf_op jit(solution)/shard_map/ppermute | solution.py:575
  7.7 2.2 %collective-permute-start.1 = (f32[80,128]{1,0:T(8,128)S(1)}, f32[80,128]{1,0:T(8,128)S(1)}, u32[]{:S(2)}, u32[]{:S(2)}) collective-permute-start(f32[80,128]{1,0:T(8,128)S(1)} %get-tuple-element.28), channel_id=1, source_target_pairs={{0,4},{4,0},{8,12},{12,8},{16,20},{20,16},{24,28},{28,24},{32,36},... | collective-permute-start | bytes 122888 | tf_op jit(solution)/shard_map/ppermute | solution.py:574
  9.9 29.5 %copy-start = (bf16[512,256]{1,0:T(8,128)(2,1)S(1)}, bf16[512,256]{1,0:T(8,128)(2,1)}, u32[]{:S(2)}) copy-start(bf16[512,256]{1,0:T(8,128)(2,1)} %constant.5.clone.table_low_ref) | copy-start | bytes 786436
  9.9 29.5 %copy-start.1 = (bf16[512,256]{1,0:T(8,128)(2,1)S(1)}, bf16[512,256]{1,0:T(8,128)(2,1)}, u32[]{:S(2)}) copy-start(bf16[512,256]{1,0:T(8,128)(2,1)} %constant.4.clone.table_high_ref) | copy-start | bytes 786436
  9.9 29.5 %copy-start.2 = (f32[4,16]{1,0:T(4,128)S(1)}, f32[4,16]{1,0:T(4,128)}, u32[]{:S(2)}) copy-start(f32[4,16]{1,0:T(4,128)} %curves_ref.1) | copy-start | bytes 772
  9.9 29.5 %copy-start.3 = (f32[128]{0:T(128)S(1)}, f32[128]{0:T(128)}, u32[]{:S(2)}) copy-start(f32[128]{0:T(128)} %param.13) | copy-start | bytes 1540
  9.9 29.5 %copy-start.4 = (s32[32]{0:T(128)S(1)}, s32[32]{0:T(128)}, u32[]{:S(2)}) copy-start(s32[32]{0:T(128)} %param.17) | copy-start | bytes 388
  14.9 24.5 %collective-permute-start.2 = (f32[288,128]{1,0:T(8,128)S(1)}, f32[288,128]{1,0:T(8,128)S(1)}, u32[]{:S(2)}, u32[]{:S(2)}) collective-permute-start(f32[288,128]{1,0:T(8,128)S(1)} %get-tuple-element.31), channel_id=1, source_target_pairs={{0,1},{1,0},{2,3},{3,2},{4,5},{5,4},{6,7},{7,6},{8,9},{9,8},{10,11... | collective-permute-start | bytes 442376 | tf_op jit(solution)/shard_map/ppermute | solution.py:609
  16.6 22.8 %collective-permute-start.3 = (f32[288,128]{1,0:T(8,128)S(1)}, f32[288,128]{1,0:T(8,128)S(1)}, u32[]{:S(2)}, u32[]{:S(2)}) collective-permute-start(f32[288,128]{1,0:T(8,128)S(1)} %get-tuple-element.32), channel_id=1, source_target_pairs={{0,3},{1,2},{2,1},{3,0},{4,7},{5,6},{6,5},{7,4},{8,11},{9,10},{10,... | collective-permute-start | bytes 442376 | tf_op jit(solution)/shard_map/ppermute | solution.py:609
  18.9 20.6 %collective-permute-start.4 = (f32[288,128]{1,0:T(8,128)S(1)}, f32[288,128]{1,0:T(8,128)S(1)}, u32[]{:S(2)}, u32[]{:S(2)}) collective-permute-start(f32[288,128]{1,0:T(8,128)S(1)} %get-tuple-element.33), channel_id=1, source_target_pairs={{0,2},{1,3},{2,0},{3,1},{4,6},{5,7},{6,4},{7,5},{8,10},{9,11},{10,... | collective-permute-start | bytes 442376 | tf_op jit(solution)/shard_map/ppermute | solution.py:609

commit v8 on v7

--- a/solution.py
+++ b/solution.py
@@ -416,12 +416,12 @@
             pack(stage, block)
 
     dots_ref[DOTS * freqs :, :] = jnp.zeros((256 - DOTS * freqs, LANES), F32)
-    sums = lax.dot_general(
-        jnp.ones((8, LANES), F32), dots_ref[...], (((1,), (1,)), ((), ())),
-        precision=lax.Precision.HIGHEST, preferred_element_type=F32,
-    )
+    sums = [
+        jnp.sum(jnp.transpose(dots_ref[i : i + LANES, :]), axis=0, keepdims=True)
+        for i in (0, LANES)
+    ]
     row = lax.broadcasted_iota(jnp.int32, (8, LANES), 0)
-    pair = jnp.where(row % 2 == 0, sums[:, :LANES], sums[:, LANES:])
+    pair = jnp.where(row % 2 == 0, sums[0], sums[1])
     for i in range(dots_out_ref.shape[0] // 8):
         dots_out_ref[8 * i : 8 * i + 8, :] = pair
 
@@ -468,10 +468,18 @@
 
 
 def final_kernel(
-    curves_ref, dots_ref, part0_ref, part1_ref, part2_ref, part3_ref,
-    table_high_ref, table_low_ref, modulus_ref, soil_ref,
-    modulus_out_ref, strain_out_ref, spectra_ref,
+    curves_in_ref, dots_ref, part0_ref, part1_ref, part2_ref, part3_ref,
+    table_high_ref, table_low_ref, modulus_in_ref, soil_in_ref,
+    modulus_out_ref, strain_out_ref, spectra_ref, curves_ref, modulus_ref, soil_ref, copied,
 ):
+    copies = [
+        pltpu.make_async_copy(source, target, copied.at[i])
+        for i, (source, target) in enumerate((
+            (curves_in_ref, curves_ref), (modulus_in_ref, modulus_ref), (soil_in_ref, soil_ref),
+        ))
+    ]
+    for copy in copies:
+        copy.start()
     freq_group = lax.axis_index("freq")
     parts, freqs = 64, 32
     total = jnp.zeros((8, LANES), F32)
@@ -515,6 +523,8 @@
     peak = jnp.max(squares, axis=0, keepdims=True)[:, : LANES // 4] * (1.0 / (4 * freqs))
     peak_strain = STRAIN_FACTOR * jnp.sqrt(peak + EPSILON)
     position = (jnp.log(peak_strain) * (1.0 / np.log(10.0)) - LOG_LOW) / LOG_STEP
+    for copy in copies:
+        copy.wait()
     soil = soil_ref[...]
     ratio = jnp.zeros_like(position)
     for level in range(curves_ref.shape[1]):
@@ -617,9 +627,15 @@
     new_modulus, peak_strain = pl.pallas_call(
         final_kernel,
         out_shape=[jax.ShapeDtypeStruct((1, quarter), F32)] * 2,
-        in_specs=[SMEM] + [VMEM] * 9,
+        in_specs=[HBM] + [VMEM] * 7 + [HBM] * 2,
         out_specs=[VMEM] * 2,
-        scratch_shapes=[pltpu.VMEM((groups * parts, 2 * LANES), F32)],
+        scratch_shapes=[
+            pltpu.VMEM((groups * parts, 2 * LANES), F32),
+            pltpu.SMEM(curves.shape, F32),
+            pltpu.VMEM((1, nodes), F32),
+            pltpu.VMEM((1, quarter), jnp.int32),
+            pltpu.SemaphoreType.DMA((3,)),
+        ],
         compiler_params=pltpu.CompilerParams(vmem_limit_bytes=32 * 1024 * 1024),
         name="response",
     )(curves, dots, *received, jnp.asarray(table_high), jnp.asarray(table_low),

time: 41.7 us -> 41.1 us (0.986)
  Pallas kernels: 11.5 us -> 10.9 us
    pallas_call x1, Pallas kernels: 2.06 us -> 1.58 us  [per_device(): pl.pallas_call(final_kernel, out_shape=[jax.ShapeDtypeStruct((1, quarter)...]
where the time goes in v8:
time: 41.1 us; the launch traced here: 40.9 us
  blocking collectives  19.5 us (47%)
  Pallas kernels  10.9 us (27%)
  starting transfers between devices  9.72 us (24%)
  between operations  0.77 us (2%)
    all_to_all x1, blocking collectives, per_device(): lax.all_to_all(outs[4].reshape(slabs * groups, 2, LANES), ('elem', 'freq'...  19.5 us
    ppermute x3, starting transfers between devices, per_device(): lax.ppermute(outs[step], 'freq', [(i, i ^ STEPS[step]) for i in range(gro...  5.04 us
    pallas_call x1, Pallas kernels, per_device(): pl.pallas_call(main_kernel, out_shape=[jax.ShapeDtypeStruct((packed, LANE...  4.82 us
    ppermute x1, starting transfers between devices, per_device(): lax.ppermute(second, 'elem', [(i, i + 1 if i % 2 else i - 1) for i in ran...  4.59 us
    pallas_call x1, Pallas kernels, per_device(): pl.pallas_call(edges_kernel, out_shape=[pltpu.VMEM((SENT_ROWS, LANES), F3...  2.42 us
    pallas_call x1, Pallas kernels, per_device(): pl.pallas_call(inner_kernel, out_shape=[pltpu.VMEM((parts, half, LANES),...  2.12 us
    pallas_call x1, Pallas kernels, per_device(): pl.pallas_call(final_kernel, out_shape=[jax.ShapeDtypeStruct((1, quarter)...  1.58 us
  transfers between devices with their start and end apart: 5, of which 0 were waited for; matrix products, arithmetic and copies ran while one was open for 0% of the time, Pallas kernels for 5%

profile of v8, /device:TPU:1, one launch (start us, length us, event | category | flops | bytes accessed | tf_op | source)
XLA Modules:
  0.0 40.9 jit_solution(14351194888643915638)
XLA Ops:
  0.6 2.4 %edges.1 = (f32[80,128]{1,0:T(8,128)S(1)}, f32[80,128]{1,0:T(8,128)S(1)}, f32[104,128]{1,0:T(8,128)S(1)}, bf16[208,256]{1,0:T(8,128)(2,1)S(1)}, f32[48,128]{1,0:T(8,128)S(1)}, /*index=5*/f32[3072,128]{1,0:T(8,128)S(1)}) custom-call(f32[3072,128]{1,0:T(8,128)} %bitcast.14, f32[1,128]{1,0:T(1,128)} %bitcast.11, f32[1,128]{1,0:T(1,128)} %bitcast.15, ...), custom_call_target="tpu_custom_call" | custom-call | tf_op jit(solution)/shard_map/edges/pallas_call | solution.py:559
  3.1 4.6 %collective-permute-start = (f32[80,128]{1,0:T(8,128)S(1)}, f32[80,128]{1,0:T(8,128)S(1)}, u32[]{:S(2)}, u32[]{:S(2)}) collective-permute-start(f32[80,128]{1,0:T(8,128)S(1)} %get-tuple-element.27), channel_id=1, source_target_pairs={{4,8},{8,4},{12,16},{16,12},{20,24},{24,20},{28,32},{32,28},{36,40... | collective-permute-start | bytes 122888 | tf_op jit(solution)/shard_map/ppermute | solution.py:585
  7.7 0.1 collective-permute-start.1
  7.8 2.1 %inner.1 = (f32[64,48,128]{2,1,0:T(8,128)S(1)}, f32[64,48,128]{2,1,0:T(8,128)S(1)}, f32[32,48,128]{2,1,0:T(8,128)S(1)}, f32[512,128]{1,0:T(8,128)S(1)}) custom-call(f32[3072,128]{1,0:T(8,128)S(1)} %get-tuple-element.19.load_ref, f32[104,128]{1,0:T(8,128)S(1)} %get-tuple-element.20.own_ref, bf16[208,256]{1,0:T(8,128)(2,1)S(1)} %get-tuple-element.21.lhs_ref, ...), custom_call_target="tpu_custom_call" | custom-call | tf_op jit(solution)/shard_map/inner/pallas_call | solution.py:588
  9.9 0.0 collective-permute-done.second_ref
  9.9 0.0 collective-permute-done.1.first_ref
  9.9 0.0 copy-start
  9.9 0.0 copy-start.1
  9.9 0.0 copy-start.2
  9.9 0.0 copy-start.3
  9.9 0.0 copy-start.4
  10.0 4.8 %krylov.1 = (f32[288,128]{1,0:T(8,128)S(1)}, f32[288,128]{1,0:T(8,128)S(1)}, f32[288,128]{1,0:T(8,128)S(1)}, f32[288,128]{1,0:T(8,128)S(1)}, f32[256,128]{1,0:T(8,128)S(1)}) custom-call(f32[64,48,128]{2,1,0:T(8,128)S(1)} %get-tuple-element.23.image_ref, f32[64,48,128]{2,1,0:T(8,128)S(1)} %get-tuple-element.24.load_ref, ...), custom_call_target="tpu_custom_call" | custom-call | tf_op jit(solution)/shard_map/krylov/pallas_call | solution.py:602
  14.8 1.7 %collective-permute-start.2 = (f32[288,128]{1,0:T(8,128)S(1)}, f32[288,128]{1,0:T(8,128)S(1)}, u32[]{:S(2)}, u32[]{:S(2)}) collective-permute-start(f32[288,128]{1,0:T(8,128)S(1)} %get-tuple-element.31), channel_id=1, source_target_pairs={{0,1},{1,0},{2,3},{3,2},{4,5},{5,4},{6,7},{7,6},{8,9},{9,8},{10,11... | collective-permute-start | bytes 442376 | tf_op jit(solution)/shard_map/ppermute | solution.py:619
  16.5 2.2 %collective-permute-start.3 = (f32[288,128]{1,0:T(8,128)S(1)}, f32[288,128]{1,0:T(8,128)S(1)}, u32[]{:S(2)}, u32[]{:S(2)}) collective-permute-start(f32[288,128]{1,0:T(8,128)S(1)} %get-tuple-element.32), channel_id=1, source_target_pairs={{0,3},{1,2},{2,1},{3,0},{4,7},{5,6},{6,5},{7,4},{8,11},{9,10},{10,... | collective-permute-start | bytes 442376 | tf_op jit(solution)/shard_map/ppermute | solution.py:619
  18.7 1.1 %collective-permute-start.4 = (f32[288,128]{1,0:T(8,128)S(1)}, f32[288,128]{1,0:T(8,128)S(1)}, u32[]{:S(2)}, u32[]{:S(2)}) collective-permute-start(f32[288,128]{1,0:T(8,128)S(1)} %get-tuple-element.33), channel_id=1, source_target_pairs={{0,2},{1,3},{2,0},{3,1},{4,6},{5,7},{6,4},{7,5},{8,10},{9,11},{10,... | collective-permute-start | bytes 442376 | tf_op jit(solution)/shard_map/ppermute | solution.py:619
  19.8 19.5 %all_to_all.5 = f32[128,2,128]{2,1,0:T(2,128)S(1)} all-to-all(f32[128,2,128]{2,1,0:T(2,128)S(1)} %bitcast.10), channel_id=1, replica_groups=mesh['elem'=32,'freq'=4] {'elem','freq'}, dimensions={0} | all-to-all | bytes 262144 | tf_op jit(solution)/shard_map/all_to_all | solution.py:622
  39.3 0.0 collective-permute-done.2.part1_ref
  39.3 0.0 collective-permute-done.3.part2_ref
  39.3 0.0 collective-permute-done.4.part3_ref
  39.3 0.0 copy-done
  39.3 0.0 copy-done.1
  39.3 0.0 copy-done.2
  39.3 0.0 copy-done.3
  39.4 1.6 %response.1 = (f32[1,32]{1,0:T(1,128)}, f32[1,32]{1,0:T(1,128)}) custom-call(f32[4,16]{1,0:T(4,128)S(1)} %copy-done.2, f32[256,128]{1,0:T(8,128)S(1)} %bitcast.9, f32[288,128]{1,0:T(8,128)S(1)} %get-tuple-element.30.part0_ref, f32[288,128]{1,0:T(8,128)S(1)} %collective-permute-done.2.part1_ref, f32[288,128]{1,0:T(8,128)S(1)} %collective-permute-done.3.part2_ref, ...), custom_call_target="tpu_custom_call" | custom-call | tf_op jit(solution)/shard_map/response/pallas_call | solution.py:627
  (1 shorter events, 0.0 us)
Async XLA Ops:
  3.1 6.8 %collective-permute-start = (f32[80,128]{1,0:T(8,128)S(1)}, f32[80,128]{1,0:T(8,128)S(1)}, u32[]{:S(2)}, u32[]{:S(2)}) collective-permute-start(f32[80,128]{1,0:T(8,128)S(1)} %get-tuple-element.27), channel_id=1, source_target_pairs={{4,8},{8,4},{12,16},{16,12},{20,24},{24,20},{28,32},{32,28},{36,40... | collective-permute-start | bytes 122888 | tf_op jit(solution)/shard_map/ppermute | solution.py:585
  7.7 2.2 %collective-permute-start.1 = (f32[80,128]{1,0:T(8,128)S(1)}, f32[80,128]{1,0:T(8,128)S(1)}, u32[]{:S(2)}, u32[]{:S(2)}) collective-permute-start(f32[80,128]{1,0:T(8,128)S(1)} %get-tuple-element.28), channel_id=1, source_target_pairs={{0,4},{4,0},{8,12},{12,8},{16,20},{20,16},{24,28},{28,24},{32,36},... | collective-permute-start | bytes 122888 | tf_op jit(solution)/shard_map/ppermute | solution.py:584
  9.9 29.4 %copy-start = (bf16[512,256]{1,0:T(8,128)(2,1)S(1)}, bf16[512,256]{1,0:T(8,128)(2,1)}, u32[]{:S(2)}) copy-start(bf16[512,256]{1,0:T(8,128)(2,1)} %constant.5.clone.table_low_ref) | copy-start | bytes 786436
  9.9 29.4 %copy-start.1 = (bf16[512,256]{1,0:T(8,128)(2,1)S(1)}, bf16[512,256]{1,0:T(8,128)(2,1)}, u32[]{:S(2)}) copy-start(bf16[512,256]{1,0:T(8,128)(2,1)} %constant.4.clone.table_high_ref) | copy-start | bytes 786436
  9.9 29.4 %copy-start.2 = (f32[4,16]{1,0:T(4,128)S(1)}, f32[4,16]{1,0:T(4,128)}, u32[]{:S(2)}) copy-start(f32[4,16]{1,0:T(4,128)} %curves_in_ref.1) | copy-start | bytes 772
  9.9 29.4 %copy-start.3 = (f32[128]{0:T(128)S(1)}, f32[128]{0:T(128)}, u32[]{:S(2)}) copy-start(f32[128]{0:T(128)} %param.13) | copy-start | bytes 1540
  9.9 29.4 %copy-start.4 = (s32[32]{0:T(128)S(1)}, s32[32]{0:T(128)}, u32[]{:S(2)}) copy-start(s32[32]{0:T(128)} %param.17) | copy-start | bytes 388
  14.8 24.5 %collective-permute-start.2 = (f32[288,128]{1,0:T(8,128)S(1)}, f32[288,128]{1,0:T(8,128)S(1)}, u32[]{:S(2)}, u32[]{:S(2)}) collective-permute-start(f32[288,128]{1,0:T(8,128)S(1)} %get-tuple-element.31), channel_id=1, source_target_pairs={{0,1},{1,0},{2,3},{3,2},{4,5},{5,4},{6,7},{7,6},{8,9},{9,8},{10,11... | collective-permute-start | bytes 442376 | tf_op jit(solution)/shard_map/ppermute | solution.py:619
  16.5 22.8 %collective-permute-start.3 = (f32[288,128]{1,0:T(8,128)S(1)}, f32[288,128]{1,0:T(8,128)S(1)}, u32[]{:S(2)}, u32[]{:S(2)}) collective-permute-start(f32[288,128]{1,0:T(8,128)S(1)} %get-tuple-element.32), channel_id=1, source_target_pairs={{0,3},{1,2},{2,1},{3,0},{4,7},{5,6},{6,5},{7,4},{8,11},{9,10},{10,... | collective-permute-start | bytes 442376 | tf_op jit(solution)/shard_map/ppermute | solution.py:619
  18.7 20.6 %collective-permute-start.4 = (f32[288,128]{1,0:T(8,128)S(1)}, f32[288,128]{1,0:T(8,128)S(1)}, u32[]{:S(2)}, u32[]{:S(2)}) collective-permute-start(f32[288,128]{1,0:T(8,128)S(1)} %get-tuple-element.33), channel_id=1, source_target_pairs={{0,2},{1,3},{2,0},{3,1},{4,6},{5,7},{6,4},{7,5},{8,10},{9,11},{10,... | collective-permute-start | bytes 442376 | tf_op jit(solution)/shard_map/ppermute | solution.py:619

commit v9 on v8

--- a/solution.py
+++ b/solution.py
@@ -1,3 +1,6 @@
+import functools
+import operator
+
 import jax
 import jax.numpy as jnp
 import numpy as np
@@ -323,7 +326,7 @@
         return moved[:half], moved[half:]
 
     def put_dot(which, f, pairs):
-        total = sum(a * b for a, b in pairs)
+        total = functools.reduce(operator.add, (a * b for a, b in pairs))
         dots_ref[pl.ds(which * freqs + f, 1), :] = jnp.sum(total, axis=0, keepdims=True)
 
     def put_strain(stage, f, k, value):
@@ -375,16 +378,17 @@
 
     def third(f, carry):
         fields = [field_ref[2 * f + k] for k in range(2)]
-        total, extra = 0.0, 0.0
+        totals, extras = [], []
         for k, z in enumerate(products(lhs[: 3 * half + 16], *fields)):
             z11, z22, z12 = z[:3]
             added, added_strain = borders(2, f, k)
             twice = 2.0 * (later(mod_sent_down * z12) + added)
-            total = total + fields[k] * (mod_own * z11 + mod_sent_down * z22 + twice)
+            totals.append(fields[k] * (mod_own * z11 + mod_sent_down * z22 + twice))
             strain = strain_of(z) + added_strain
             put_strain(2, f, k, strain)
-            extra = extra + strain[6:7]
-        dots_ref[pl.ds(5 * freqs + f, 1), :] = -(jnp.sum(total, axis=0, keepdims=True) + extra)
+            extras.append(strain[6:7])
+        energy = jnp.sum(totals[0] + totals[1], axis=0, keepdims=True) + extras[0] + extras[1]
+        dots_ref[pl.ds(5 * freqs + f, 1), :] = -energy
         return carry
 
     quarter = LANES // 4
@@ -400,6 +404,7 @@
         places = [
             (stage * parts + k * freqs, [(k, c) for c in range(4)]) for k in range(2)
         ] + [(3 * parts + stage * freqs, [(0, 4), (0, 5), (1, 4), (1, 5)])]
+        stores = []
         for step in range(4):
             dest = lax.bitwise_xor(freq_group, STEPS[step])
             for row, names in places:
@@ -407,7 +412,9 @@
                 for i, name in enumerate(names):
                     moved = pltpu.roll(comps[name], quarter * ((i + 4 - dest) % 4), 1)
                     held = moved if held is None else jnp.where(cell == i, moved, held)
-                outs[step][row + block * 8 : row + block * 8 + 8, :] = held
+                stores.append((step, row + block * 8, held))
+        for step, start, held in stores:
+            outs[step][start : start + 8, :] = held
 
     for stage, step in enumerate((first, second, third)):
         rims = rim_stage(stage, rims)
@@ -499,10 +506,10 @@
         ]
 
         def joined(base, per_stage):
-            return sum(
+            return functools.reduce(operator.add, (
                 weights[j] * part_ref[base + j * per_stage : base + j * per_stage + freqs, :]
                 for j in range(3)
-            )
+            ))
 
         rest = joined(3 * parts, freqs)
         for k in range(2):
@@ -512,10 +519,9 @@
             spectra_ref[pl.ds(start, freqs), LANES:] = jnp.where(lanes < 64, side, 0.0)
     high, low = halves(spectra_ref[...])
     table_high, table_low = table_high_ref[...], table_low_ref[...]
-    history = (
-        jnp.dot(table_high, low, preferred_element_type=F32)
-        + jnp.dot(table_low, high, preferred_element_type=F32)
-        + jnp.dot(table_high, high, preferred_element_type=F32)
+    history = jnp.dot(
+        jnp.concatenate([table_high, table_low, table_high], 1),
+        jnp.concatenate([high, high, low], 0), preferred_element_type=F32,
     )
     squares = history[:, :LANES] ** 2 + history[:, LANES:] ** 2
     squares = squares + pltpu.roll(squares, 64, 1)

time: 41.1 us -> 41.1 us (level)
  no operation moved by 1% of the time
where the time goes in v9:
time: 41.1 us; the launch traced here: 40.9 us
  blocking collectives  19.5 us (47%)
  Pallas kernels  10.9 us (27%)
  starting transfers between devices  9.72 us (24%)
  between operations  0.77 us (2%)
    all_to_all x1, blocking collectives, per_device(): lax.all_to_all(outs[4].reshape(slabs * groups, 2, LANES), ('elem', 'freq'...  19.5 us
    ppermute x3, starting transfers between devices, per_device(): lax.ppermute(outs[step], 'freq', [(i, i ^ STEPS[step]) for i in range(gro...  5.04 us
    pallas_call x1, Pallas kernels, per_device(): pl.pallas_call(main_kernel, out_shape=[jax.ShapeDtypeStruct((packed, LANE...  4.82 us
    ppermute x1, starting transfers between devices, per_device(): lax.ppermute(second, 'elem', [(i, i + 1 if i % 2 else i - 1) for i in ran...  4.59 us
    pallas_call x1, Pallas kernels, per_device(): pl.pallas_call(edges_kernel, out_shape=[pltpu.VMEM((SENT_ROWS, LANES), F3...  2.42 us
    pallas_call x1, Pallas kernels, per_device(): pl.pallas_call(inner_kernel, out_shape=[pltpu.VMEM((parts, half, LANES),...  2.12 us
    pallas_call x1, Pallas kernels, per_device(): pl.pallas_call(final_kernel, out_shape=[jax.ShapeDtypeStruct((1, quarter)...  1.58 us
  transfers between devices with their start and end apart: 5, of which 0 were waited for; matrix products, arithmetic and copies ran while one was open for 0% of the time, Pallas kernels for 5%

profile of v9, /device:TPU:1, one launch (start us, length us, event | category | flops | bytes accessed | tf_op | source)
XLA Modules:
  0.0 40.9 jit_solution(11887184571425235739)
XLA Ops:
  0.6 2.4 %edges.1 = (f32[80,128]{1,0:T(8,128)S(1)}, f32[80,128]{1,0:T(8,128)S(1)}, f32[104,128]{1,0:T(8,128)S(1)}, bf16[208,256]{1,0:T(8,128)(2,1)S(1)}, f32[48,128]{1,0:T(8,128)S(1)}, /*index=5*/f32[3072,128]{1,0:T(8,128)S(1)}) custom-call(f32[3072,128]{1,0:T(8,128)} %bitcast.14, f32[1,128]{1,0:T(1,128)} %bitcast.11, f32[1,128]{1,0:T(1,128)} %bitcast.15, ...), custom_call_target="tpu_custom_call" | custom-call | tf_op jit(solution)/shard_map/edges/pallas_call | solution.py:565
  3.1 4.6 %collective-permute-start = (f32[80,128]{1,0:T(8,128)S(1)}, f32[80,128]{1,0:T(8,128)S(1)}, u32[]{:S(2)}, u32[]{:S(2)}) collective-permute-start(f32[80,128]{1,0:T(8,128)S(1)} %get-tuple-element.27), channel_id=1, source_target_pairs={{4,8},{8,4},{12,16},{16,12},{20,24},{24,20},{28,32},{32,28},{36,40... | collective-permute-start | bytes 122888 | tf_op jit(solution)/shard_map/ppermute | solution.py:591
  7.7 0.1 collective-permute-start.1
  7.8 2.1 %inner.1 = (f32[64,48,128]{2,1,0:T(8,128)S(1)}, f32[64,48,128]{2,1,0:T(8,128)S(1)}, f32[32,48,128]{2,1,0:T(8,128)S(1)}, f32[512,128]{1,0:T(8,128)S(1)}) custom-call(f32[3072,128]{1,0:T(8,128)S(1)} %get-tuple-element.19.load_ref, f32[104,128]{1,0:T(8,128)S(1)} %get-tuple-element.20.own_ref, bf16[208,256]{1,0:T(8,128)(2,1)S(1)} %get-tuple-element.21.lhs_ref, ...), custom_call_target="tpu_custom_call" | custom-call | tf_op jit(solution)/shard_map/inner/pallas_call | solution.py:594
  9.9 0.0 collective-permute-done.second_ref
  9.9 0.0 collective-permute-done.1.first_ref
  9.9 0.0 copy-start
  9.9 0.0 copy-start.1
  9.9 0.0 copy-start.2
  9.9 0.0 copy-start.3
  9.9 0.0 copy-start.4
  10.0 4.8 %krylov.1 = (f32[288,128]{1,0:T(8,128)S(1)}, f32[288,128]{1,0:T(8,128)S(1)}, f32[288,128]{1,0:T(8,128)S(1)}, f32[288,128]{1,0:T(8,128)S(1)}, f32[256,128]{1,0:T(8,128)S(1)}) custom-call(f32[64,48,128]{2,1,0:T(8,128)S(1)} %get-tuple-element.23.image_ref, f32[64,48,128]{2,1,0:T(8,128)S(1)} %get-tuple-element.24.load_ref, ...), custom_call_target="tpu_custom_call" | custom-call | tf_op jit(solution)/shard_map/krylov/pallas_call | solution.py:608
  14.8 1.7 %collective-permute-start.2 = (f32[288,128]{1,0:T(8,128)S(1)}, f32[288,128]{1,0:T(8,128)S(1)}, u32[]{:S(2)}, u32[]{:S(2)}) collective-permute-start(f32[288,128]{1,0:T(8,128)S(1)} %get-tuple-element.31), channel_id=1, source_target_pairs={{0,1},{1,0},{2,3},{3,2},{4,5},{5,4},{6,7},{7,6},{8,9},{9,8},{10,11... | collective-permute-start | bytes 442376 | tf_op jit(solution)/shard_map/ppermute | solution.py:625
  16.5 2.2 %collective-permute-start.3 = (f32[288,128]{1,0:T(8,128)S(1)}, f32[288,128]{1,0:T(8,128)S(1)}, u32[]{:S(2)}, u32[]{:S(2)}) collective-permute-start(f32[288,128]{1,0:T(8,128)S(1)} %get-tuple-element.32), channel_id=1, source_target_pairs={{0,3},{1,2},{2,1},{3,0},{4,7},{5,6},{6,5},{7,4},{8,11},{9,10},{10,... | collective-permute-start | bytes 442376 | tf_op jit(solution)/shard_map/ppermute | solution.py:625
  18.7 1.1 %collective-permute-start.4 = (f32[288,128]{1,0:T(8,128)S(1)}, f32[288,128]{1,0:T(8,128)S(1)}, u32[]{:S(2)}, u32[]{:S(2)}) collective-permute-start(f32[288,128]{1,0:T(8,128)S(1)} %get-tuple-element.33), channel_id=1, source_target_pairs={{0,2},{1,3},{2,0},{3,1},{4,6},{5,7},{6,4},{7,5},{8,10},{9,11},{10,... | collective-permute-start | bytes 442376 | tf_op jit(solution)/shard_map/ppermute | solution.py:625
  19.8 19.5 %all_to_all.5 = f32[128,2,128]{2,1,0:T(2,128)S(1)} all-to-all(f32[128,2,128]{2,1,0:T(2,128)S(1)} %bitcast.10), channel_id=1, replica_groups=mesh['elem'=32,'freq'=4] {'elem','freq'}, dimensions={0} | all-to-all | bytes 262144 | tf_op jit(solution)/shard_map/all_to_all | solution.py:628
  39.3 0.0 collective-permute-done.2.part1_ref
  39.3 0.0 collective-permute-done.3.part2_ref
  39.3 0.0 collective-permute-done.4.part3_ref
  39.3 0.0 copy-done
  39.3 0.0 copy-done.1
  39.3 0.0 copy-done.2
  39.3 0.0 copy-done.3
  39.4 1.6 %response.1 = (f32[1,32]{1,0:T(1,128)}, f32[1,32]{1,0:T(1,128)}) custom-call(f32[4,16]{1,0:T(4,128)S(1)} %copy-done.2, f32[256,128]{1,0:T(8,128)S(1)} %bitcast.9, f32[288,128]{1,0:T(8,128)S(1)} %get-tuple-element.30.part0_ref, f32[288,128]{1,0:T(8,128)S(1)} %collective-permute-done.2.part1_ref, f32[288,128]{1,0:T(8,128)S(1)} %collective-permute-done.3.part2_ref, ...), custom_call_target="tpu_custom_call" | custom-call | tf_op jit(solution)/shard_map/response/pallas_call | solution.py:633
  (1 shorter events, 0.0 us)
Async XLA Ops:
  3.1 6.8 %collective-permute-start = (f32[80,128]{1,0:T(8,128)S(1)}, f32[80,128]{1,0:T(8,128)S(1)}, u32[]{:S(2)}, u32[]{:S(2)}) collective-permute-start(f32[80,128]{1,0:T(8,128)S(1)} %get-tuple-element.27), channel_id=1, source_target_pairs={{4,8},{8,4},{12,16},{16,12},{20,24},{24,20},{28,32},{32,28},{36,40... | collective-permute-start | bytes 122888 | tf_op jit(solution)/shard_map/ppermute | solution.py:591
  7.7 2.2 %collective-permute-start.1 = (f32[80,128]{1,0:T(8,128)S(1)}, f32[80,128]{1,0:T(8,128)S(1)}, u32[]{:S(2)}, u32[]{:S(2)}) collective-permute-start(f32[80,128]{1,0:T(8,128)S(1)} %get-tuple-element.28), channel_id=1, source_target_pairs={{0,4},{4,0},{8,12},{12,8},{16,20},{20,16},{24,28},{28,24},{32,36},... | collective-permute-start | bytes 122888 | tf_op jit(solution)/shard_map/ppermute | solution.py:590
  9.9 29.4 %copy-start = (bf16[512,256]{1,0:T(8,128)(2,1)S(1)}, bf16[512,256]{1,0:T(8,128)(2,1)}, u32[]{:S(2)}) copy-start(bf16[512,256]{1,0:T(8,128)(2,1)} %constant.5.clone.table_low_ref) | copy-start | bytes 786436
  9.9 29.4 %copy-start.1 = (bf16[512,256]{1,0:T(8,128)(2,1)S(1)}, bf16[512,256]{1,0:T(8,128)(2,1)}, u32[]{:S(2)}) copy-start(bf16[512,256]{1,0:T(8,128)(2,1)} %constant.4.clone.table_high_ref) | copy-start | bytes 786436
  9.9 29.4 %copy-start.2 = (f32[4,16]{1,0:T(4,128)S(1)}, f32[4,16]{1,0:T(4,128)}, u32[]{:S(2)}) copy-start(f32[4,16]{1,0:T(4,128)} %curves_in_ref.1) | copy-start | bytes 772
  9.9 29.4 %copy-start.3 = (f32[128]{0:T(128)S(1)}, f32[128]{0:T(128)}, u32[]{:S(2)}) copy-start(f32[128]{0:T(128)} %param.13) | copy-start | bytes 1540
  9.9 29.4 %copy-start.4 = (s32[32]{0:T(128)S(1)}, s32[32]{0:T(128)}, u32[]{:S(2)}) copy-start(s32[32]{0:T(128)} %param.17) | copy-start | bytes 388
  14.8 24.5 %collective-permute-start.2 = (f32[288,128]{1,0:T(8,128)S(1)}, f32[288,128]{1,0:T(8,128)S(1)}, u32[]{:S(2)}, u32[]{:S(2)}) collective-permute-start(f32[288,128]{1,0:T(8,128)S(1)} %get-tuple-element.31), channel_id=1, source_target_pairs={{0,1},{1,0},{2,3},{3,2},{4,5},{5,4},{6,7},{7,6},{8,9},{9,8},{10,11... | collective-permute-start | bytes 442376 | tf_op jit(solution)/shard_map/ppermute | solution.py:625
  16.5 22.8 %collective-permute-start.3 = (f32[288,128]{1,0:T(8,128)S(1)}, f32[288,128]{1,0:T(8,128)S(1)}, u32[]{:S(2)}, u32[]{:S(2)}) collective-permute-start(f32[288,128]{1,0:T(8,128)S(1)} %get-tuple-element.32), channel_id=1, source_target_pairs={{0,3},{1,2},{2,1},{3,0},{4,7},{5,6},{6,5},{7,4},{8,11},{9,10},{10,... | collective-permute-start | bytes 442376 | tf_op jit(solution)/shard_map/ppermute | solution.py:625
  18.7 20.6 %collective-permute-start.4 = (f32[288,128]{1,0:T(8,128)S(1)}, f32[288,128]{1,0:T(8,128)S(1)}, u32[]{:S(2)}, u32[]{:S(2)}) collective-permute-start(f32[288,128]{1,0:T(8,128)S(1)} %get-tuple-element.33), channel_id=1, source_target_pairs={{0,2},{1,3},{2,0},{3,1},{4,6},{5,7},{6,4},{7,5},{8,10},{9,11},{10,... | collective-permute-start | bytes 442376 | tf_op jit(solution)/shard_map/ppermute | solution.py:625

commit v10 on v9

--- a/solution.py
+++ b/solution.py
@@ -19,6 +19,7 @@
 SLOT = 8
 DEPTH = 176
 UNROLL = 32
+AHEAD = 1
 STEPS = (0, 1, 3, 2)
 DOTS = 6
 F32 = jnp.float32
@@ -337,9 +338,9 @@
         shift = (lane + 2 * LANES - 1 - 2 * (2 * f + k)) % LANES
         return jnp.where(lanes == lane, pltpu.roll(border_ref[which, :half, :], shift, 1), place)
 
-    def images(f, stage, fields):
+    def images(f, stage, ready):
         result = []
-        for k, z in enumerate(products(lhs, *fields)):
+        for k, z in enumerate(ready):
             added, added_strain = borders(stage, f, k)
             put_strain(stage, f, k, strain_of(z) + added_strain)
             result.append(-(image_of(mod_main, z) + added))
@@ -365,21 +366,18 @@
         put_dot(2, f, zip(nexts, image))
         return carry
 
-    def second(f, carry):
+    def second(f, fields, ready):
         inv = inv_ref[f]
-        fields = [field_ref[2 * f + k] for k in range(2)]
-        image = images(f, 1, fields)
+        image = images(f, 1, ready)
         nexts = [inv * t for t in image]
         for k in range(2):
             field_ref[2 * f + k] = nexts[k]
         put_dot(3, f, zip(fields, image))
         put_dot(4, f, zip(nexts, image))
-        return carry
-
-    def third(f, carry):
-        fields = [field_ref[2 * f + k] for k in range(2)]
+
+    def third(f, fields, ready):
         totals, extras = [], []
-        for k, z in enumerate(products(lhs[: 3 * half + 16], *fields)):
+        for k, z in enumerate(ready):
             z11, z22, z12 = z[:3]
             added, added_strain = borders(2, f, k)
             twice = 2.0 * (later(mod_sent_down * z12) + added)
@@ -389,7 +387,15 @@
             extras.append(strain[6:7])
         energy = jnp.sum(totals[0] + totals[1], axis=0, keepdims=True) + extras[0] + extras[1]
         dots_ref[pl.ds(5 * freqs + f, 1), :] = -energy
-        return carry
+
+    def run_ahead(step, matrix):
+        waiting = []
+        for f in range(freqs + AHEAD):
+            if f < freqs:
+                fields = [field_ref[2 * f + k] for k in range(2)]
+                waiting.append((f, fields, products(matrix, *fields)))
+            if f >= AHEAD:
+                step(*waiting.pop(0))
 
     quarter = LANES // 4
     cell = lane_ids(8) // quarter
@@ -418,7 +424,10 @@
 
     for stage, step in enumerate((first, second, third)):
         rims = rim_stage(stage, rims)
-        lax.fori_loop(0, freqs, step, 0, unroll=UNROLL)
+        if stage == 0:
+            lax.fori_loop(0, freqs, step, 0, unroll=UNROLL)
+        else:
+            run_ahead(step, lhs if stage == 1 else lhs[: 3 * half + 16])
         for block in range(freqs // 8):
             pack(stage, block)
 

time: 41.1 us -> 41.1 us (level)
  no operation moved by 1% of the time
where the time goes in v10:
time: 41.1 us; the launch traced here: 40.9 us
  blocking collectives  19.5 us (47%)
  Pallas kernels  10.9 us (27%)
  starting transfers between devices  9.72 us (24%)
  between operations  0.77 us (2%)
    all_to_all x1, blocking collectives, per_device(): lax.all_to_all(outs[4].reshape(slabs * groups, 2, LANES), ('elem', 'freq'...  19.5 us
    ppermute x3, starting transfers between devices, per_device(): lax.ppermute(outs[step], 'freq', [(i, i ^ STEPS[step]) for i in range(gro...  5.04 us
    pallas_call x1, Pallas kernels, per_device(): pl.pallas_call(main_kernel, out_shape=[jax.ShapeDtypeStruct((packed, LANE...  4.82 us
    ppermute x1, starting transfers between devices, per_device(): lax.ppermute(second, 'elem', [(i, i + 1 if i % 2 else i - 1) for i in ran...  4.59 us
    pallas_call x1, Pallas kernels, per_device(): pl.pallas_call(edges_kernel, out_shape=[pltpu.VMEM((SENT_ROWS, LANES), F3...  2.42 us
    pallas_call x1, Pallas kernels, per_device(): pl.pallas_call(inner_kernel, out_shape=[pltpu.VMEM((parts, half, LANES),...  2.12 us
    pallas_call x1, Pallas kernels, per_device(): pl.pallas_call(final_kernel, out_shape=[jax.ShapeDtypeStruct((1, quarter)...  1.58 us
  transfers between devices with their start and end apart: 5, of which 0 were waited for; matrix products, arithmetic and copies ran while one was open for 0% of the time, Pallas kernels for 5%

profile of v10, /device:TPU:1, one launch (start us, length us, event | category | flops | bytes accessed | tf_op | source)
XLA Modules:
  0.0 40.9 jit_solution(9945171349626130193)
XLA Ops:
  0.6 2.4 %edges.1 = (f32[80,128]{1,0:T(8,128)S(1)}, f32[80,128]{1,0:T(8,128)S(1)}, f32[104,128]{1,0:T(8,128)S(1)}, bf16[208,256]{1,0:T(8,128)(2,1)S(1)}, f32[48,128]{1,0:T(8,128)S(1)}, /*index=5*/f32[3072,128]{1,0:T(8,128)S(1)}) custom-call(f32[3072,128]{1,0:T(8,128)} %bitcast.14, f32[1,128]{1,0:T(1,128)} %bitcast.11, f32[1,128]{1,0:T(1,128)} %bitcast.15, ...), custom_call_target="tpu_custom_call" | custom-call | tf_op jit(solution)/shard_map/edges/pallas_call | solution.py:574
  3.1 4.6 %collective-permute-start = (f32[80,128]{1,0:T(8,128)S(1)}, f32[80,128]{1,0:T(8,128)S(1)}, u32[]{:S(2)}, u32[]{:S(2)}) collective-permute-start(f32[80,128]{1,0:T(8,128)S(1)} %get-tuple-element.27), channel_id=1, source_target_pairs={{4,8},{8,4},{12,16},{16,12},{20,24},{24,20},{28,32},{32,28},{36,40... | collective-permute-start | bytes 122888 | tf_op jit(solution)/shard_map/ppermute | solution.py:600
  7.7 0.1 collective-permute-start.1
  7.8 2.1 %inner.1 = (f32[64,48,128]{2,1,0:T(8,128)S(1)}, f32[64,48,128]{2,1,0:T(8,128)S(1)}, f32[32,48,128]{2,1,0:T(8,128)S(1)}, f32[512,128]{1,0:T(8,128)S(1)}) custom-call(f32[3072,128]{1,0:T(8,128)S(1)} %get-tuple-element.19.load_ref, f32[104,128]{1,0:T(8,128)S(1)} %get-tuple-element.20.own_ref, bf16[208,256]{1,0:T(8,128)(2,1)S(1)} %get-tuple-element.21.lhs_ref, ...), custom_call_target="tpu_custom_call" | custom-call | tf_op jit(solution)/shard_map/inner/pallas_call | solution.py:603
  9.9 0.0 collective-permute-done.second_ref
  9.9 0.0 collective-permute-done.1.first_ref
  9.9 0.0 copy-start
  9.9 0.0 copy-start.1
  9.9 0.0 copy-start.2
  9.9 0.0 copy-start.3
  9.9 0.0 copy-start.4
  10.0 4.8 %krylov.1 = (f32[288,128]{1,0:T(8,128)S(1)}, f32[288,128]{1,0:T(8,128)S(1)}, f32[288,128]{1,0:T(8,128)S(1)}, f32[288,128]{1,0:T(8,128)S(1)}, f32[256,128]{1,0:T(8,128)S(1)}) custom-call(f32[64,48,128]{2,1,0:T(8,128)S(1)} %get-tuple-element.23.image_ref, f32[64,48,128]{2,1,0:T(8,128)S(1)} %get-tuple-element.24.load_ref, ...), custom_call_target="tpu_custom_call" | custom-call | tf_op jit(solution)/shard_map/krylov/pallas_call | solution.py:617
  14.8 1.7 %collective-permute-start.2 = (f32[288,128]{1,0:T(8,128)S(1)}, f32[288,128]{1,0:T(8,128)S(1)}, u32[]{:S(2)}, u32[]{:S(2)}) collective-permute-start(f32[288,128]{1,0:T(8,128)S(1)} %get-tuple-element.31), channel_id=1, source_target_pairs={{0,1},{1,0},{2,3},{3,2},{4,5},{5,4},{6,7},{7,6},{8,9},{9,8},{10,11... | collective-permute-start | bytes 442376 | tf_op jit(solution)/shard_map/ppermute | solution.py:634
  16.5 2.2 %collective-permute-start.3 = (f32[288,128]{1,0:T(8,128)S(1)}, f32[288,128]{1,0:T(8,128)S(1)}, u32[]{:S(2)}, u32[]{:S(2)}) collective-permute-start(f32[288,128]{1,0:T(8,128)S(1)} %get-tuple-element.32), channel_id=1, source_target_pairs={{0,3},{1,2},{2,1},{3,0},{4,7},{5,6},{6,5},{7,4},{8,11},{9,10},{10,... | collective-permute-start | bytes 442376 | tf_op jit(solution)/shard_map/ppermute | solution.py:634
  18.7 1.1 %collective-permute-start.4 = (f32[288,128]{1,0:T(8,128)S(1)}, f32[288,128]{1,0:T(8,128)S(1)}, u32[]{:S(2)}, u32[]{:S(2)}) collective-permute-start(f32[288,128]{1,0:T(8,128)S(1)} %get-tuple-element.33), channel_id=1, source_target_pairs={{0,2},{1,3},{2,0},{3,1},{4,6},{5,7},{6,4},{7,5},{8,10},{9,11},{10,... | collective-permute-start | bytes 442376 | tf_op jit(solution)/shard_map/ppermute | solution.py:634
  19.8 19.5 %all_to_all.5 = f32[128,2,128]{2,1,0:T(2,128)S(1)} all-to-all(f32[128,2,128]{2,1,0:T(2,128)S(1)} %bitcast.10), channel_id=1, replica_groups=mesh['elem'=32,'freq'=4] {'elem','freq'}, dimensions={0} | all-to-all | bytes 262144 | tf_op jit(solution)/shard_map/all_to_all | solution.py:637
  39.3 0.0 collective-permute-done.2.part1_ref
  39.3 0.0 collective-permute-done.3.part2_ref
  39.3 0.0 collective-permute-done.4.part3_ref
  39.3 0.0 copy-done
  39.3 0.0 copy-done.1
  39.3 0.0 copy-done.2
  39.3 0.0 copy-done.3
  39.4 1.6 %response.1 = (f32[1,32]{1,0:T(1,128)}, f32[1,32]{1,0:T(1,128)}) custom-call(f32[4,16]{1,0:T(4,128)S(1)} %copy-done.2, f32[256,128]{1,0:T(8,128)S(1)} %bitcast.9, f32[288,128]{1,0:T(8,128)S(1)} %get-tuple-element.30.part0_ref, f32[288,128]{1,0:T(8,128)S(1)} %collective-permute-done.2.part1_ref, f32[288,128]{1,0:T(8,128)S(1)} %collective-permute-done.3.part2_ref, ...), custom_call_target="tpu_custom_call" | custom-call | tf_op jit(solution)/shard_map/response/pallas_call | solution.py:642
  (1 shorter events, 0.0 us)
Async XLA Ops:
  3.1 6.8 %collective-permute-start = (f32[80,128]{1,0:T(8,128)S(1)}, f32[80,128]{1,0:T(8,128)S(1)}, u32[]{:S(2)}, u32[]{:S(2)}) collective-permute-start(f32[80,128]{1,0:T(8,128)S(1)} %get-tuple-element.27), channel_id=1, source_target_pairs={{4,8},{8,4},{12,16},{16,12},{20,24},{24,20},{28,32},{32,28},{36,40... | collective-permute-start | bytes 122888 | tf_op jit(solution)/shard_map/ppermute | solution.py:600
  7.7 2.2 %collective-permute-start.1 = (f32[80,128]{1,0:T(8,128)S(1)}, f32[80,128]{1,0:T(8,128)S(1)}, u32[]{:S(2)}, u32[]{:S(2)}) collective-permute-start(f32[80,128]{1,0:T(8,128)S(1)} %get-tuple-element.28), channel_id=1, source_target_pairs={{0,4},{4,0},{8,12},{12,8},{16,20},{20,16},{24,28},{28,24},{32,36},... | collective-permute-start | bytes 122888 | tf_op jit(solution)/shard_map/ppermute | solution.py:599
  9.9 29.4 %copy-start = (bf16[512,256]{1,0:T(8,128)(2,1)S(1)}, bf16[512,256]{1,0:T(8,128)(2,1)}, u32[]{:S(2)}) copy-start(bf16[512,256]{1,0:T(8,128)(2,1)} %constant.5.clone.table_low_ref) | copy-start | bytes 786436
  9.9 29.4 %copy-start.1 = (bf16[512,256]{1,0:T(8,128)(2,1)S(1)}, bf16[512,256]{1,0:T(8,128)(2,1)}, u32[]{:S(2)}) copy-start(bf16[512,256]{1,0:T(8,128)(2,1)} %constant.4.clone.table_high_ref) | copy-start | bytes 786436
  9.9 29.4 %copy-start.2 = (f32[4,16]{1,0:T(4,128)S(1)}, f32[4,16]{1,0:T(4,128)}, u32[]{:S(2)}) copy-start(f32[4,16]{1,0:T(4,128)} %curves_in_ref.1) | copy-start | bytes 772
  9.9 29.4 %copy-start.3 = (f32[128]{0:T(128)S(1)}, f32[128]{0:T(128)}, u32[]{:S(2)}) copy-start(f32[128]{0:T(128)} %param.13) | copy-start | bytes 1540
  9.9 29.4 %copy-start.4 = (s32[32]{0:T(128)S(1)}, s32[32]{0:T(128)}, u32[]{:S(2)}) copy-start(s32[32]{0:T(128)} %param.17) | copy-start | bytes 388
  14.8 24.5 %collective-permute-start.2 = (f32[288,128]{1,0:T(8,128)S(1)}, f32[288,128]{1,0:T(8,128)S(1)}, u32[]{:S(2)}, u32[]{:S(2)}) collective-permute-start(f32[288,128]{1,0:T(8,128)S(1)} %get-tuple-element.31), channel_id=1, source_target_pairs={{0,1},{1,0},{2,3},{3,2},{4,5},{5,4},{6,7},{7,6},{8,9},{9,8},{10,11... | collective-permute-start | bytes 442376 | tf_op jit(solution)/shard_map/ppermute | solution.py:634
  16.5 22.8 %collective-permute-start.3 = (f32[288,128]{1,0:T(8,128)S(1)}, f32[288,128]{1,0:T(8,128)S(1)}, u32[]{:S(2)}, u32[]{:S(2)}) collective-permute-start(f32[288,128]{1,0:T(8,128)S(1)} %get-tuple-element.32), channel_id=1, source_target_pairs={{0,3},{1,2},{2,1},{3,0},{4,7},{5,6},{6,5},{7,4},{8,11},{9,10},{10,... | collective-permute-start | bytes 442376 | tf_op jit(solution)/shard_map/ppermute | solution.py:634
  18.7 20.6 %collective-permute-start.4 = (f32[288,128]{1,0:T(8,128)S(1)}, f32[288,128]{1,0:T(8,128)S(1)}, u32[]{:S(2)}, u32[]{:S(2)}) collective-permute-start(f32[288,128]{1,0:T(8,128)S(1)} %get-tuple-element.33), channel_id=1, source_target_pairs={{0,2},{1,3},{2,0},{3,1},{4,6},{5,7},{6,4},{7,5},{8,10},{9,11},{10,... | collective-permute-start | bytes 442376 | tf_op jit(solution)/shard_map/ppermute | solution.py:634
